TPU v7x, 256 devices: a whole 4x4x8 slice. The times are simulated.
256 devices in a mesh: seq: 8 (over x_hi, y), row: 32 (over x_lo, z, core).
Axes of the slice: x: 4 (x_hi: 2, x_lo: 2; x = x_hi * 2 + x_lo), y: 4, z: 8, core: 2. Of those that a mesh axis runs over, the one named last changes fastest.
Arguments:
- tokens: bfloat16 [2, 2048, 3072], P(None, ('seq', 'row')), may hold values from -6 to 6
- w_qkv: bfloat16 [6144, 3072], P('row'), may hold values from -0.109375 to 0.109375
- w_rate: bfloat16 [32, 3072], P('row'), may hold values from -0.109375 to 0.109375
- rate_bias: float32 [32], P('row'), may hold values from -3 to 1
- w_out: bfloat16 [2048, 3072], P('row'), may hold values from -0.125 to 0.125
- w_first_init: float32 [32, 64, 256], P('row'), may hold values from -0.75 to 0.75
- b_first_init: float32 [32, 256], P('row'), may hold values from -3 to 3
- w_second_init: float32 [32, 256, 64], P('row'), may hold values from -0.375 to 0.375
- b_second_init: float32 [32, 64], P('row'), may hold values from -3 to 3
- ln_gain: float32 [32, 64], P('row'), may hold values from 0.5 to 1.5
- ln_bias: float32 [32, 64], P('row'), may hold values from -3 to 3
Outputs:
- mixed: bfloat16 [2, 2048, 3072], P(None, ('seq', 'row'))
All inputs are finite; a program needn't handle non-finite values.
Results may differ from a plain program's by a relative error of at most 0.0056.
Values may be sent and summed in bfloat16 or wider, within the bound.
A program may use at most 64 MiB of HBM per device.

v0:
```python
from functools import partial

import jax
import jax.numpy as jnp
from jax import lax
from jax.sharding import PartitionSpec as P

MINI = 64


gelu_coef = 0.7978845608028654
base_rate = 0.01
ln_eps = 1e-06


def passed_along(array, axis, by):
    size = lax.axis_size(axis)
    pairs = [(i, i + by) for i in range(size) if 0 <= i + by < size]
    return lax.ppermute(array, axis, pairs)


def gelu_tanh(entries):
    tanh_arg = gelu_coef * (entries + 0.044715 * entries * entries * entries)
    return 0.5 * entries * (1.0 + jnp.tanh(tanh_arg))


def gelu_slope(entries):
    tanh_arg = gelu_coef * (entries + 0.044715 * entries * entries * entries)
    tangent = jnp.tanh(tanh_arg)
    return 0.5 * (1.0 + tangent) + 0.5 * entries * (1.0 - tangent * tangent) * gelu_coef * (
        1.0 + 3.0 * 0.044715 * entries * entries
    )


def matmul(left, right):
    return jnp.dot(left, right, precision=lax.Precision.HIGHEST, preferred_element_type=jnp.float32)


def normalize(entries):
    centred = entries - jnp.mean(entries, axis=-1, keepdims=True)
    spread = jnp.sqrt(jnp.mean(centred * centred, axis=-1, keepdims=True) + ln_eps)
    return (centred / spread, spread)


def mini_step(inner_state, batch_block, norm_gain, offset):
    w_first, b_first, w_second, b_second = inner_state
    queries, key_rows, value_rows, lr_rows = batch_block
    mini_len = queries.shape[0]
    hidden_pre = matmul(key_rows, w_first) + b_first
    hidden = gelu_tanh(hidden_pre)
    second = matmul(hidden, w_second) + b_second
    target = value_rows - key_rows
    normed, spread = normalize(second)
    grad_out = norm_gain * (norm_gain * normed + offset - target)
    feat_width = second.shape[-1]
    grad_second = (
        feat_width * grad_out
        - jnp.sum(grad_out, axis=-1, keepdims=True)
        - normed * jnp.sum(grad_out * normed, axis=-1, keepdims=True)
    ) / (feat_width * spread)
    grad_first = matmul(grad_second, w_second.T) * gelu_slope(hidden_pre)
    tri_mask = jnp.tril(jnp.ones((mini_len, mini_len), jnp.float32))
    eta_last = lr_rows / mini_len
    eta_table = tri_mask * eta_last[None, :]
    query_keys = matmul(queries, key_rows.T) * eta_table
    bias_first = b_first - matmul(eta_table, grad_first)
    first_bar = matmul(queries, w_first) - matmul(query_keys, grad_first) + bias_first
    hidden_bar = gelu_tanh(first_bar)
    hidden_pairs = matmul(hidden_bar, hidden.T) * eta_table
    bias_second = b_second - matmul(eta_table, grad_second)
    second_bar = matmul(hidden_bar, w_second) - matmul(hidden_pairs, grad_second) + bias_second
    w_first = w_first - matmul((key_rows * eta_last[:, None]).T, grad_first)
    b_first = b_first - matmul(eta_last[None, :], grad_first)[0]
    w_second = w_second - matmul((hidden * eta_last[:, None]).T, grad_second)
    b_second = b_second - matmul(eta_last[None, :], grad_second)[0]
    normed_bar, spread_bar = normalize(second_bar)
    result = queries + norm_gain * normed_bar + offset
    return ((w_first, b_first, w_second, b_second), result)


def run_blocks(inner_state, queries, key_rows, value_rows, lr_rows, norm_gain, offset, mini_len):
    block_count = queries.shape[0] // mini_len
    blocks = (
        queries.reshape(block_count, mini_len, -1),
        key_rows.reshape(block_count, mini_len, -1),
        value_rows.reshape(block_count, mini_len, -1),
        lr_rows.reshape(block_count, mini_len),
    )

    def advance(loop_carry, batch_block):
        return mini_step(loop_carry, batch_block, norm_gain, offset)

    inner_state, results = lax.scan(advance, inner_state, blocks)
    return (inner_state, results.reshape(queries.shape[0], -1))


def on_device(
    tokens,
    w_qkv,
    w_rate,
    rate_bias,
    w_out,
    w_first_init,
    b_first_init,
    w_second_init,
    b_second_init,
    ln_gain,
    ln_bias,
):
    videos, tok_part, feat_width = tokens.shape
    row_count = lax.axis_size("row")
    seg_len = tok_part * row_count
    tok_rows = videos * seg_len
    proj_width = w_qkv.shape[0]
    head_size = proj_width // 3
    stacked = jnp.concatenate([w_qkv, w_rate], axis=0)
    combined = jnp.einsum(
        "vkd,cd->vkc",
        lax.all_gather(tokens, "row", axis=1, tiled=True),
        stacked,
        preferred_element_type=jnp.float32,
    )
    projected = lax.optimization_barrier(combined[:, :, :proj_width].astype(jnp.bfloat16)).astype(
        jnp.float32
    )
    queries = projected[:, :, :head_size]
    key_rows = projected[:, :, head_size : 2 * head_size]
    value_rows = projected[:, :, 2 * head_size :]
    lr_rows = base_rate * jax.nn.sigmoid(combined[:, :, proj_width] + rate_bias[0])
    initial = (w_first_init[0], b_first_init[0], w_second_init[0], b_second_init[0])
    norm_gain = ln_gain[0]
    offset = ln_bias[0]

    def segment(inner_state, video_q, video_k, video_v, video_lr):
        return run_blocks(inner_state, video_q, video_k, video_v, video_lr, norm_gain, offset, MINI)

    seq_count = lax.axis_size("seq")
    seq_place = lax.axis_index("seq")
    first_device = seq_place == 0

    def spread_videos(entries):
        return jnp.broadcast_to(entries, (videos,) + entries.shape)

    start_states = jax.tree.map(spread_videos, initial)
    incoming = start_states
    for turn_idx in range(seq_count):
        finals, results = jax.vmap(segment)(incoming, queries, key_rows, value_rows, lr_rows)
        if turn_idx + 1 < seq_count:
            received = passed_along(finals, "seq", 1)
            incoming = jax.tree.map(partial(jnp.where, first_device), start_states, received)
    heads_rows = results.astype(jnp.bfloat16)
    partial_terms = jnp.dot(
        heads_rows.reshape(tok_rows, head_size), w_out, preferred_element_type=jnp.float32
    )
    mixed_out = lax.psum_scatter(
        partial_terms.reshape(videos, seg_len, feat_width), "row", scatter_dimension=1, tiled=True
    ).astype(jnp.bfloat16)
    return mixed_out


def solution(mesh):
    in_specs = (
        P(None, ("seq", "row"), None),
        P("row", None),
        P("row", None),
        P("row"),
        P("row", None),
        P("row", None, None),
        P("row", None),
        P("row", None, None),
        P("row", None),
        P("row", None),
        P("row", None),
    )
    out_specs = P(None, ("seq", "row"), None)
    return jax.shard_map(
        on_device, mesh=mesh, in_specs=in_specs, out_specs=out_specs, check_vma=False
    )
```

profile of v0, /device:TPU:4, one launch (start us, length us, event | category | flops | bytes accessed | tf_op | source)
XLA Modules:
  0.0 433.6 jit_solution(14161290089676213497)
XLA Ops:
  8.0 70.0 %all-gather.2.cloned.1.call-done = bf16[2,256,3072]{2,1,0:T(8,128)(2,1)} async-done(((bf16[2,8,3072]{2,1,0:T(8,128)(2,1)}), bf16[2,256,3072]{2,1,0:T(8,128)(2,1)}) %all-gather.2.cloned.1.call-update) | async-done | bytes 3145744 | tf_op jit(solution)/shard_map/all_gather | solution.py:119
  78.0 3.4 fusion.203
  82.4 10.8 %while.130 = (s32[]{:T(128)}, f32[2,64,256]{2,1,0:T(8,128)S(1)}, f32[2,256]{1,0:T(2,128)S(1)}, f32[2,256,64]{1,2,0:T(8,128)S(1)}, f32[2,64]{1,0:T(2,128)S(1)}, /...) while((s32[]{:T(128)}, f32[2,64,256]{2,1,0:T(8,128)S(1)}, ...), condition=%wide.region_5.6_spmd, body=%wide.region_0.5_spmd.sunk | while | flops 127755136 | bytes 2386057 | solution.py:93
  93.2 3.4 collective-permute-start.3
  96.7 3.4 collective-permute-start.1
  100.1 3.1 collective-permute-start
  103.2 1.9 collective-permute-start.2
  105.7 4.9 %collective-permute-done = f32[2,64,256]{2,1,0:T(8,128)S(1)} collective-permute-done((f32[2,64,256]{2,1,0:T(8,128)S(1)}, f32[2,64,256]{2,1,0:T(8,128)S(1)}, u32[]{:S(2)}, u32[]{:S(2)}) %collective-permute-start) | collective-permute-done | bytes 131104 | tf_op jit(solution)/shard_map/ppermute | solution.py:19
  110.7 3.0 collective-permute-done.2
  113.6 10.8 %while.131 = (s32[]{:T(128)}, f32[2,64,256]{2,1,0:T(8,128)S(1)}, f32[2,256]{1,0:T(2,128)S(1)}, f32[2,256,64]{1,2,0:T(8,128)S(1)}, f32[2,64]{1,0:T(2,128)S(1)}, /...) while((s32[]{:T(128)}, f32[2,64,256]{2,1,0:T(8,128)S(1)}, ...), condition=%wide.region_11.12_spmd, body=%wide.region_6.11_spmd.sunk | while | flops 127755136 | bytes 2386057 | solution.py:93
  124.5 1.9 collective-permute-start.7
  126.4 1.9 collective-permute-start.5
  128.4 1.9 collective-permute-start.4
  130.3 1.9 collective-permute-start.6
  133.6 1.9 collective-permute-done.5
  135.5 3.9 collective-permute-done.4
  139.5 1.4 collective-permute-done.6
  140.9 10.8 %while.132 = (s32[]{:T(128)}, f32[2,64,256]{2,1,0:T(8,128)S(1)}, f32[2,256]{1,0:T(2,128)S(1)}, f32[2,256,64]{1,2,0:T(8,128)S(1)}, f32[2,64]{1,0:T(2,128)S(1)}, /...) while((s32[]{:T(128)}, f32[2,64,256]{2,1,0:T(8,128)S(1)}, ...), condition=%wide.region_17.18_spmd, body=%wide.region_12.17_spmd.sunk | while | flops 127755136 | bytes 2386057 | solution.py:93
  151.7 1.9 collective-permute-start.11
  153.6 1.9 collective-permute-start.9
  155.6 1.9 collective-permute-start.8
  157.5 1.9 collective-permute-start.10
  159.4 1.4 collective-permute-done.11
  160.8 2.0 collective-permute-done.9
  162.8 3.6 collective-permute-done.8
  166.4 1.6 collective-permute-done.10
  168.0 10.8 %while.133 = (s32[]{:T(128)}, f32[2,64,256]{2,1,0:T(8,128)S(1)}, f32[2,256]{1,0:T(2,128)S(1)}, f32[2,256,64]{1,2,0:T(8,128)S(1)}, f32[2,64]{1,0:T(2,128)S(1)}, /...) while((s32[]{:T(128)}, f32[2,64,256]{2,1,0:T(8,128)S(1)}, ...), condition=%wide.region_23.24_spmd, body=%wide.region_18.23_spmd.sunk | while | flops 127755136 | bytes 2386057 | solution.py:93
  178.8 1.9 collective-permute-start.15
  180.8 1.9 collective-permute-start.13
  182.7 1.9 collective-permute-start.12
  184.6 1.9 collective-permute-start.14
  186.5 1.4 collective-permute-done.15
  187.9 1.9 collective-permute-done.13
  189.9 3.3 collective-permute-done.12
  193.2 1.9 collective-permute-done.14
  195.1 10.8 %while.134 = (s32[]{:T(128)}, f32[2,64,256]{2,1,0:T(8,128)S(1)}, f32[2,256]{1,0:T(2,128)S(1)}, f32[2,256,64]{1,2,0:T(8,128)S(1)}, f32[2,64]{1,0:T(2,128)S(1)}, /...) while((s32[]{:T(128)}, f32[2,64,256]{2,1,0:T(8,128)S(1)}, ...), condition=%wide.region_29.30_spmd, body=%wide.region_24.29_spmd.sunk | while | flops 127755136 | bytes 2386057 | solution.py:93
  205.9 1.9 collective-permute-start.19
  207.9 1.9 collective-permute-start.17
  209.8 1.9 collective-permute-start.16
  211.7 2.1 collective-permute-start.18
  215.0 1.9 collective-permute-done.17
  217.0 3.3 collective-permute-done.16
  220.3 1.9 collective-permute-done.18
  222.2 10.9 %while.135 = (s32[]{:T(128)}, f32[2,64,256]{2,1,0:T(8,128)S(1)}, f32[2,256]{1,0:T(2,128)S(1)}, f32[2,256,64]{1,2,0:T(8,128)S(1)}, f32[2,64]{1,0:T(2,128)S(1)}, /...) while((s32[]{:T(128)}, f32[2,64,256]{2,1,0:T(8,128)S(1)}, ...), condition=%wide.region_35.36_spmd, body=%wide.region_30.35_spmd.sunk | while | flops 127755136 | bytes 2386057 | solution.py:93
  233.1 1.9 collective-permute-start.23
  235.0 1.9 collective-permute-start.21
  236.9 1.9 collective-permute-start.20
  238.9 1.9 collective-permute-start.22
  240.8 1.4 collective-permute-done.23
  242.2 1.9 collective-permute-done.21
  244.1 3.3 collective-permute-done.20
  247.4 1.9 collective-permute-done.22
  249.4 10.8 %while.136 = (s32[]{:T(128)}, f32[2,64,256]{2,1,0:T(8,128)S(1)}, f32[2,256]{1,0:T(2,128)S(1)}, f32[2,256,64]{1,2,0:T(8,128)S(1)}, f32[2,64]{1,0:T(2,128)S(1)}, /...) while((s32[]{:T(128)}, f32[2,64,256]{2,1,0:T(8,128)S(1)}, ...), condition=%wide.region_41.42_spmd, body=%wide.region_36.41_spmd.sunk | while | flops 127755136 | bytes 2386057 | solution.py:93
  260.2 1.9 collective-permute-start.27
  262.5 1.9 collective-permute-start.25
  264.4 1.9 collective-permute-start.24
  266.3 1.9 collective-permute-start.26
  269.3 2.3 collective-permute-done.25
  271.6 3.3 collective-permute-done.24
  274.9 1.9 collective-permute-done.26
  276.8 20.8 %while.137 = (s32[]{:T(128)}, f32[2,64,256]{2,1,0:T(8,128)S(1)}, f32[2,256]{1,0:T(2,128)S(1)}, f32[2,256,64]{1,2,0:T(8,128)S(1)}, f32[2,64]{1,0:T(2,128)S(1)}, /...) while((s32[]{:T(128)}, f32[2,64,256]{2,1,0:T(8,128)S(1)}, ...), condition=%wide.region_49.50_spmd, body=%wide.region_42.49_spmd.sunk | while | flops 273236992 | bytes 4856481 | solution.py:93
  297.9 3.7 fusion.204
  301.6 123.6 %reduce-scatter.2.cloned.1.call-done = f32[2,8,3072]{2,1,0:T(8,128)} async-done(((f32[2,256,3072]{2,1,0:T(8,128)}), f32[2,8,3072]{2,1,0:T(8,128)}) %reduce-scatter.2.cloned.1.call-update) | async-done | bytes 196624 | tf_op jit(solution)/shard_map/reduce_scatter | solution.py:155
  425.2 1.6 convert_element_type.22
  (633 shorter events, 100.3 us)
Async XLA Ops:
  6.5 291.4 %copy-start = (bf16[64,3072]{1,0:T(8,128)(2,1)S(1)}, bf16[64,3072]{1,0:T(8,128)(2,1)}, u32[]{:S(2)}) copy-start(bf16[64,3072]{1,0:T(8,128)(2,1)} %param.31) | copy-start | bytes 1179652
  6.5 71.4 %all-gather.2.cloned.1.call-start = ((), (), s32[]{:S(2)}) async-start(), calls=%async_computation.1 | async-start | bytes 3244032 | tf_op jit(solution)/shard_map/all_gather | solution.py:119
  7.3 418.0 %reduce-scatter.2.cloned.1.call-start = ((), (), s32[]{:S(2)}) async-start(), calls=%async_computation.2 | async-start | bytes 6488064 | tf_op jit(solution)/shard_map/reduce_scatter | solution.py:155
  81.4 0.9 copy-start.6
  81.4 0.9 copy-start.5
  81.4 0.9 copy-start.1
  81.4 0.9 copy-start.2
  81.5 0.9 copy-start.3
  81.5 0.9 copy-start.4
  93.2 11.8 %collective-permute-start.3 = (f32[2,64]{1,0:T(2,128)S(1)}, f32[2,64]{1,0:T(2,128)S(1)}, u32[]{:S(2)}, u32[]{:S(2)}) collective-permute-start(f32[2,64]{1,0:T(2,128)S(1)} %get-tuple-element.455), channel_id=1, source_target_pairs={{0,32},{32,64},{64,96},{96,128},{128,160},{160,192},{192,224},{1,3... | collective-permute-start | bytes 1544 | tf_op jit(solution)/shard_map/ppermute | solution.py:19
  96.7 9.1 %collective-permute-start.1 = (f32[2,256]{1,0:T(2,128)S(1)}, f32[2,256]{1,0:T(2,128)S(1)}, u32[]{:S(2)}, u32[]{:S(2)}) collective-permute-start(f32[2,256]{1,0:T(2,128)S(1)} %get-tuple-element.453), channel_id=1, source_target_pairs={{0,32},{32,64},{64,96},{96,128},{128,160},{160,192},{192,224},{1,3... | collective-permute-start | bytes 6152 | tf_op jit(solution)/shard_map/ppermute | solution.py:19
  100.1 10.6 %collective-permute-start = (f32[2,64,256]{2,1,0:T(8,128)S(1)}, f32[2,64,256]{2,1,0:T(8,128)S(1)}, u32[]{:S(2)}, u32[]{:S(2)}) collective-permute-start(f32[2,64,256]{2,1,0:T(8,128)S(1)} %get-tuple-element.452), channel_id=1, source_target_pairs={{0,32},{32,64},{64,96},{96,128},{128,160},{160,192},{192,224},{1,3... | collective-permute-start | bytes 393224 | tf_op jit(solution)/shard_map/ppermute | solution.py:19
  103.2 10.5 %collective-permute-start.2 = (f32[2,256,64]{1,2,0:T(8,128)S(1)}, f32[2,256,64]{1,2,0:T(8,128)S(1)}, u32[]{:S(2)}, u32[]{:S(2)}) collective-permute-start(f32[2,256,64]{1,2,0:T(8,128)S(1)} %get-tuple-element.454), channel_id=1, source_target_pairs={{0,32},{32,64},{64,96},{96,128},{128,160},{160,192},{192,224},{1,3... | collective-permute-start | bytes 393224 | tf_op jit(solution)/shard_map/ppermute | solution.py:19
  124.5 9.1 %collective-permute-start.7 = (f32[2,64]{1,0:T(2,128)S(1)}, f32[2,64]{1,0:T(2,128)S(1)}, u32[]{:S(2)}, u32[]{:S(2)}) collective-permute-start(f32[2,64]{1,0:T(2,128)S(1)} %get-tuple-element.459), channel_id=1, source_target_pairs={{0,32},{32,64},{64,96},{96,128},{128,160},{160,192},{192,224},{1,3... | collective-permute-start | bytes 1544 | tf_op jit(solution)/shard_map/ppermute | solution.py:19
  126.4 9.1 %collective-permute-start.5 = (f32[2,256]{1,0:T(2,128)S(1)}, f32[2,256]{1,0:T(2,128)S(1)}, u32[]{:S(2)}, u32[]{:S(2)}) collective-permute-start(f32[2,256]{1,0:T(2,128)S(1)} %get-tuple-element.457), channel_id=1, source_target_pairs={{0,32},{32,64},{64,96},{96,128},{128,160},{160,192},{192,224},{1,3... | collective-permute-start | bytes 6152 | tf_op jit(solution)/shard_map/ppermute | solution.py:19
  128.4 11.1 %collective-permute-start.4 = (f32[2,64,256]{2,1,0:T(8,128)S(1)}, f32[2,64,256]{2,1,0:T(8,128)S(1)}, u32[]{:S(2)}, u32[]{:S(2)}) collective-permute-start(f32[2,64,256]{2,1,0:T(8,128)S(1)} %get-tuple-element.456), channel_id=1, source_target_pairs={{0,32},{32,64},{64,96},{96,128},{128,160},{160,192},{192,224},{1,3... | collective-permute-start | bytes 393224 | tf_op jit(solution)/shard_map/ppermute | solution.py:19
  130.3 10.6 %collective-permute-start.6 = (f32[2,256,64]{1,2,0:T(8,128)S(1)}, f32[2,256,64]{1,2,0:T(8,128)S(1)}, u32[]{:S(2)}, u32[]{:S(2)}) collective-permute-start(f32[2,256,64]{1,2,0:T(8,128)S(1)} %get-tuple-element.458), channel_id=1, source_target_pairs={{0,32},{32,64},{64,96},{96,128},{128,160},{160,192},{192,224},{1,3... | collective-permute-start | bytes 393224 | tf_op jit(solution)/shard_map/ppermute | solution.py:19
  151.7 9.1 %collective-permute-start.11 = (f32[2,64]{1,0:T(2,128)S(1)}, f32[2,64]{1,0:T(2,128)S(1)}, u32[]{:S(2)}, u32[]{:S(2)}) collective-permute-start(f32[2,64]{1,0:T(2,128)S(1)} %get-tuple-element.463), channel_id=1, source_target_pairs={{0,32},{32,64},{64,96},{96,128},{128,160},{160,192},{192,224},{1,3... | collective-permute-start | bytes 1544 | tf_op jit(solution)/shard_map/ppermute | solution.py:19
  153.6 9.1 %collective-permute-start.9 = (f32[2,256]{1,0:T(2,128)S(1)}, f32[2,256]{1,0:T(2,128)S(1)}, u32[]{:S(2)}, u32[]{:S(2)}) collective-permute-start(f32[2,256]{1,0:T(2,128)S(1)} %get-tuple-element.461), channel_id=1, source_target_pairs={{0,32},{32,64},{64,96},{96,128},{128,160},{160,192},{192,224},{1,3... | collective-permute-start | bytes 6152 | tf_op jit(solution)/shard_map/ppermute | solution.py:19
  155.6 10.8 %collective-permute-start.8 = (f32[2,64,256]{2,1,0:T(8,128)S(1)}, f32[2,64,256]{2,1,0:T(8,128)S(1)}, u32[]{:S(2)}, u32[]{:S(2)}) collective-permute-start(f32[2,64,256]{2,1,0:T(8,128)S(1)} %get-tuple-element.460), channel_id=1, source_target_pairs={{0,32},{32,64},{64,96},{96,128},{128,160},{160,192},{192,224},{1,3... | collective-permute-start | bytes 393224 | tf_op jit(solution)/shard_map/ppermute | solution.py:19
  157.5 10.5 %collective-permute-start.10 = (f32[2,256,64]{1,2,0:T(8,128)S(1)}, f32[2,256,64]{1,2,0:T(8,128)S(1)}, u32[]{:S(2)}, u32[]{:S(2)}) collective-permute-start(f32[2,256,64]{1,2,0:T(8,128)S(1)} %get-tuple-element.462), channel_id=1, source_target_pairs={{0,32},{32,64},{64,96},{96,128},{128,160},{160,192},{192,224},{1,3... | collective-permute-start | bytes 393224 | tf_op jit(solution)/shard_map/ppermute | solution.py:19
  178.8 9.1 %collective-permute-start.15 = (f32[2,64]{1,0:T(2,128)S(1)}, f32[2,64]{1,0:T(2,128)S(1)}, u32[]{:S(2)}, u32[]{:S(2)}) collective-permute-start(f32[2,64]{1,0:T(2,128)S(1)} %get-tuple-element.467), channel_id=1, source_target_pairs={{0,32},{32,64},{64,96},{96,128},{128,160},{160,192},{192,224},{1,3... | collective-permute-start | bytes 1544 | tf_op jit(solution)/shard_map/ppermute | solution.py:19
  180.8 9.1 %collective-permute-start.13 = (f32[2,256]{1,0:T(2,128)S(1)}, f32[2,256]{1,0:T(2,128)S(1)}, u32[]{:S(2)}, u32[]{:S(2)}) collective-permute-start(f32[2,256]{1,0:T(2,128)S(1)} %get-tuple-element.465), channel_id=1, source_target_pairs={{0,32},{32,64},{64,96},{96,128},{128,160},{160,192},{192,224},{1,3... | collective-permute-start | bytes 6152 | tf_op jit(solution)/shard_map/ppermute | solution.py:19
  182.7 10.5 %collective-permute-start.12 = (f32[2,64,256]{2,1,0:T(8,128)S(1)}, f32[2,64,256]{2,1,0:T(8,128)S(1)}, u32[]{:S(2)}, u32[]{:S(2)}) collective-permute-start(f32[2,64,256]{2,1,0:T(8,128)S(1)} %get-tuple-element.464), channel_id=1, source_target_pairs={{0,32},{32,64},{64,96},{96,128},{128,160},{160,192},{192,224},{1,3... | collective-permute-start | bytes 393224 | tf_op jit(solution)/shard_map/ppermute | solution.py:19
  184.6 10.5 %collective-permute-start.14 = (f32[2,256,64]{1,2,0:T(8,128)S(1)}, f32[2,256,64]{1,2,0:T(8,128)S(1)}, u32[]{:S(2)}, u32[]{:S(2)}) collective-permute-start(f32[2,256,64]{1,2,0:T(8,128)S(1)} %get-tuple-element.466), channel_id=1, source_target_pairs={{0,32},{32,64},{64,96},{96,128},{128,160},{160,192},{192,224},{1,3... | collective-permute-start | bytes 393224 | tf_op jit(solution)/shard_map/ppermute | solution.py:19
  205.9 9.1 %collective-permute-start.19 = (f32[2,64]{1,0:T(2,128)S(1)}, f32[2,64]{1,0:T(2,128)S(1)}, u32[]{:S(2)}, u32[]{:S(2)}) collective-permute-start(f32[2,64]{1,0:T(2,128)S(1)} %get-tuple-element.471), channel_id=1, source_target_pairs={{0,32},{32,64},{64,96},{96,128},{128,160},{160,192},{192,224},{1,3... | collective-permute-start | bytes 1544 | tf_op jit(solution)/shard_map/ppermute | solution.py:19
  207.9 9.1 %collective-permute-start.17 = (f32[2,256]{1,0:T(2,128)S(1)}, f32[2,256]{1,0:T(2,128)S(1)}, u32[]{:S(2)}, u32[]{:S(2)}) collective-permute-start(f32[2,256]{1,0:T(2,128)S(1)} %get-tuple-element.469), channel_id=1, source_target_pairs={{0,32},{32,64},{64,96},{96,128},{128,160},{160,192},{192,224},{1,3... | collective-permute-start | bytes 6152 | tf_op jit(solution)/shard_map/ppermute | solution.py:19
  209.8 10.5 %collective-permute-start.16 = (f32[2,64,256]{2,1,0:T(8,128)S(1)}, f32[2,64,256]{2,1,0:T(8,128)S(1)}, u32[]{:S(2)}, u32[]{:S(2)}) collective-permute-start(f32[2,64,256]{2,1,0:T(8,128)S(1)} %get-tuple-element.468), channel_id=1, source_target_pairs={{0,32},{32,64},{64,96},{96,128},{128,160},{160,192},{192,224},{1,3... | collective-permute-start | bytes 393224 | tf_op jit(solution)/shard_map/ppermute | solution.py:19
  211.7 10.5 %collective-permute-start.18 = (f32[2,256,64]{1,2,0:T(8,128)S(1)}, f32[2,256,64]{1,2,0:T(8,128)S(1)}, u32[]{:S(2)}, u32[]{:S(2)}) collective-permute-start(f32[2,256,64]{1,2,0:T(8,128)S(1)} %get-tuple-element.470), channel_id=1, source_target_pairs={{0,32},{32,64},{64,96},{96,128},{128,160},{160,192},{192,224},{1,3... | collective-permute-start | bytes 393224 | tf_op jit(solution)/shard_map/ppermute | solution.py:19
  233.1 9.1 %collective-permute-start.23 = (f32[2,64]{1,0:T(2,128)S(1)}, f32[2,64]{1,0:T(2,128)S(1)}, u32[]{:S(2)}, u32[]{:S(2)}) collective-permute-start(f32[2,64]{1,0:T(2,128)S(1)} %get-tuple-element.475), channel_id=1, source_target_pairs={{0,32},{32,64},{64,96},{96,128},{128,160},{160,192},{192,224},{1,3... | collective-permute-start | bytes 1544 | tf_op jit(solution)/shard_map/ppermute | solution.py:19
  235.0 9.1 %collective-permute-start.21 = (f32[2,256]{1,0:T(2,128)S(1)}, f32[2,256]{1,0:T(2,128)S(1)}, u32[]{:S(2)}, u32[]{:S(2)}) collective-permute-start(f32[2,256]{1,0:T(2,128)S(1)} %get-tuple-element.473), channel_id=1, source_target_pairs={{0,32},{32,64},{64,96},{96,128},{128,160},{160,192},{192,224},{1,3... | collective-permute-start | bytes 6152 | tf_op jit(solution)/shard_map/ppermute | solution.py:19
  236.9 10.5 %collective-permute-start.20 = (f32[2,64,256]{2,1,0:T(8,128)S(1)}, f32[2,64,256]{2,1,0:T(8,128)S(1)}, u32[]{:S(2)}, u32[]{:S(2)}) collective-permute-start(f32[2,64,256]{2,1,0:T(8,128)S(1)} %get-tuple-element.472), channel_id=1, source_target_pairs={{0,32},{32,64},{64,96},{96,128},{128,160},{160,192},{192,224},{1,3... | collective-permute-start | bytes 393224 | tf_op jit(solution)/shard_map/ppermute | solution.py:19
  238.9 10.5 %collective-permute-start.22 = (f32[2,256,64]{1,2,0:T(8,128)S(1)}, f32[2,256,64]{1,2,0:T(8,128)S(1)}, u32[]{:S(2)}, u32[]{:S(2)}) collective-permute-start(f32[2,256,64]{1,2,0:T(8,128)S(1)} %get-tuple-element.474), channel_id=1, source_target_pairs={{0,32},{32,64},{64,96},{96,128},{128,160},{160,192},{192,224},{1,3... | collective-permute-start | bytes 393224 | tf_op jit(solution)/shard_map/ppermute | solution.py:19
  260.2 9.1 %collective-permute-start.27 = (f32[2,64]{1,0:T(2,128)S(1)}, f32[2,64]{1,0:T(2,128)S(1)}, u32[]{:S(2)}, u32[]{:S(2)}) collective-permute-start(f32[2,64]{1,0:T(2,128)S(1)} %get-tuple-element.479), channel_id=1, source_target_pairs={{0,32},{32,64},{64,96},{96,128},{128,160},{160,192},{192,224},{1,3... | collective-permute-start | bytes 1544 | tf_op jit(solution)/shard_map/ppermute | solution.py:19
  262.5 9.1 %collective-permute-start.25 = (f32[2,256]{1,0:T(2,128)S(1)}, f32[2,256]{1,0:T(2,128)S(1)}, u32[]{:S(2)}, u32[]{:S(2)}) collective-permute-start(f32[2,256]{1,0:T(2,128)S(1)} %get-tuple-element.477), channel_id=1, source_target_pairs={{0,32},{32,64},{64,96},{96,128},{128,160},{160,192},{192,224},{1,3... | collective-permute-start | bytes 6152 | tf_op jit(solution)/shard_map/ppermute | solution.py:19
  264.4 10.5 %collective-permute-start.24 = (f32[2,64,256]{2,1,0:T(8,128)S(1)}, f32[2,64,256]{2,1,0:T(8,128)S(1)}, u32[]{:S(2)}, u32[]{:S(2)}) collective-permute-start(f32[2,64,256]{2,1,0:T(8,128)S(1)} %get-tuple-element.476), channel_id=1, source_target_pairs={{0,32},{32,64},{64,96},{96,128},{128,160},{160,192},{192,224},{1,3... | collective-permute-start | bytes 393224 | tf_op jit(solution)/shard_map/ppermute | solution.py:19
  266.3 10.5 %collective-permute-start.26 = (f32[2,256,64]{1,2,0:T(8,128)S(1)}, f32[2,256,64]{1,2,0:T(8,128)S(1)}, u32[]{:S(2)}, u32[]{:S(2)}) collective-permute-start(f32[2,256,64]{1,2,0:T(8,128)S(1)} %get-tuple-element.478), channel_id=1, source_target_pairs={{0,32},{32,64},{64,96},{96,128},{128,160},{160,192},{192,224},{1,3... | collective-permute-start | bytes 393224 | tf_op jit(solution)/shard_map/ppermute | solution.py:19
Sparse Core Ops, SparseCore 0:
  9.2 68.7 all-gather.1
  301.7 123.4 reduce-scatter.1
where the time goes:
time: 435 us; the launch traced here: 434 us
  waiting for transfers between devices  254 us (58%)
  matrix products  80.4 us (18%)
  starting transfers between devices  58.1 us (13%)
  other arithmetic  22.2 us (5%)
  between operations  14.6 us (3%)
    reduce_scatter x1, waiting for transfers between devices, on_device(): lax.psum_scatter(partial_terms.reshape(videos, seg_len, feat_width), 'row...  124 us
    dot_general x256, matrix products, matmul(): jnp.dot(left, right, precision=lax.Precision.HIGHEST, preferred_element_t...  73.3 us
    all_gather x1, waiting for transfers between devices, on_device(): lax.all_gather(tokens, 'row', axis=1, tiled=True)  70 us
    ppermute x28, waiting for transfers between devices, passed_along(): return lax.ppermute(array, axis, pairs)  59.5 us
    ppermute x28, starting transfers between devices, passed_along(): return lax.ppermute(array, axis, pairs)  58.1 us
  transfers between devices with their start and end apart: 30, of which 29 were waited for; matrix products, arithmetic and copies ran while one was open for 0% of the time, Pallas kernels for 0%

commit v1 on v0

--- a/solution.py
+++ b/solution.py
@@ -94,6 +94,21 @@
     return (inner_state, results.reshape(queries.shape[0], -1))
 
 
+def pack_state(state):
+    videos = state[0].shape[0]
+    return jnp.concatenate([part.reshape(videos, -1) for part in state], axis=1)
+
+
+def unpack_state(flat, like):
+    parts = []
+    at = 0
+    for part in like:
+        width = part[0].size
+        parts.append(flat[:, at : at + width].reshape(part.shape))
+        at += width
+    return tuple(parts)
+
+
 def on_device(
     tokens,
     w_qkv,
@@ -108,15 +123,21 @@
     ln_bias,
 ):
     videos, tok_part, feat_width = tokens.shape
-    row_count = lax.axis_size("row")
+    row_axes = ("xlo", "z", "core")
+    pair_axes = ("xlo", "core")
+    row_count = lax.axis_size(row_axes)
+    z_count = lax.axis_size("z")
+    pair_count = lax.axis_size(pair_axes)
     seg_len = tok_part * row_count
-    tok_rows = videos * seg_len
     proj_width = w_qkv.shape[0]
     head_size = proj_width // 3
     stacked = jnp.concatenate([w_qkv, w_rate], axis=0)
+    gathered = lax.all_gather(tokens, row_axes, axis=1, tiled=True)
+    gathered, w_out = lax.optimization_barrier((gathered, w_out))
+    w_out_pair = lax.all_gather(w_out, pair_axes, axis=0, tiled=True)
     combined = jnp.einsum(
         "vkd,cd->vkc",
-        lax.all_gather(tokens, "row", axis=1, tiled=True),
+        gathered,
         stacked,
         preferred_element_type=jnp.float32,
     )
@@ -146,33 +167,49 @@
     for turn_idx in range(seq_count):
         finals, results = jax.vmap(segment)(incoming, queries, key_rows, value_rows, lr_rows)
         if turn_idx + 1 < seq_count:
-            received = passed_along(finals, "seq", 1)
+            with jax.named_scope("state_hop"):
+                received = unpack_state(passed_along(pack_state(finals), "seq", 1), finals)
             incoming = jax.tree.map(partial(jnp.where, first_device), start_states, received)
     heads_rows = results.astype(jnp.bfloat16)
-    partial_terms = jnp.dot(
-        heads_rows.reshape(tok_rows, head_size), w_out, preferred_element_type=jnp.float32
-    )
-    mixed_out = lax.psum_scatter(
-        partial_terms.reshape(videos, seg_len, feat_width), "row", scatter_dimension=1, tiled=True
-    ).astype(jnp.bfloat16)
-    return mixed_out
+    with jax.named_scope("output_mix"):
+        by_owner = heads_rows.reshape(videos, 2, z_count, 2, tok_part, head_size)
+        by_owner = by_owner.transpose(1, 3, 0, 2, 4, 5).reshape(
+            pair_count, videos, z_count, tok_part, head_size
+        )
+        by_head = lax.all_to_all(by_owner, pair_axes, 0, 0, tiled=True)
+        partial_terms = jnp.einsum(
+            "gvzic,gcd->zvid",
+            by_head,
+            w_out_pair.reshape(pair_count, head_size, feat_width),
+            preferred_element_type=jnp.float32,
+        )
+        mixed_out = lax.psum_scatter(
+            partial_terms.reshape(z_count, -1), "z", scatter_dimension=0, tiled=True
+        )
+        mixed_out = lax.optimization_barrier(mixed_out)
+    return mixed_out.reshape(videos, tok_part, feat_width).astype(jnp.bfloat16)
 
 
 def solution(mesh):
+    seq_count, row_count = mesh.devices.shape
+    fine = jax.sharding.Mesh(
+        mesh.devices.reshape(seq_count, 2, row_count // 4, 2), ("seq", "xlo", "z", "core")
+    )
+    row = ("xlo", "z", "core")
     in_specs = (
-        P(None, ("seq", "row"), None),
-        P("row", None),
-        P("row", None),
-        P("row"),
-        P("row", None),
-        P("row", None, None),
-        P("row", None),
-        P("row", None, None),
-        P("row", None),
-        P("row", None),
-        P("row", None),
-    )
-    out_specs = P(None, ("seq", "row"), None)
+        P(None, ("seq",) + row, None),
+        P(row, None),
+        P(row, None),
+        P(row),
+        P(row, None),
+        P(row, None, None),
+        P(row, None),
+        P(row, None, None),
+        P(row, None),
+        P(row, None),
+        P(row, None),
+    )
+    out_specs = P(None, ("seq",) + row, None)
     return jax.shard_map(
-        on_device, mesh=mesh, in_specs=in_specs, out_specs=out_specs, check_vma=False
-    )
+        on_device, mesh=fine, in_specs=in_specs, out_specs=out_specs, check_vma=False
+    )

time: 435 us -> 356 us (0.82)
  waiting for transfers between devices: 254 us -> 146 us
  blocking collectives: 0 us -> 62.7 us
  starting transfers between devices: 58.1 us -> 18.6 us
  local copies, waits for them, and re-layouts: 1.38 us -> 10.9 us
    reduce_scatter x1 -> x0, waiting for transfers between devices: 124 us -> none  [on_device(): lax.psum_scatter(partial_terms.reshape(videos, seg_len, feat_width), 'row...]
    unnamed x0 -> x1, blocking collectives: none -> 62.7 us
    ppermute x28 -> x7, starting transfers between devices: 58.1 us -> 15.1 us  [passed_along(): return lax.ppermute(array, axis, pairs)]
    ppermute x28 -> x7, waiting for transfers between devices: 59.5 us -> 71.6 us  [passed_along(): return lax.ppermute(array, axis, pairs)]
    all_gather x1 -> x2, waiting for transfers between devices: 70 us -> 70 us  [the longest x1 70 us: on_device(): gathered = lax.all_gather(tokens, row_axes, axis=1, tiled=True)]
  transfers between devices with their start and end apart: 30 -> 10, of which waited for: 29 -> 9; matrix products, arithmetic and copies ran while one was open for 0% -> 6% of each run, Pallas kernels for 0% -> 0%
where the time goes in v1:
time: 356 us
  waiting for transfers between devices  146 us (41%)
  matrix products  78.5 us (22%)
  blocking collectives  62.7 us (18%)
  other arithmetic  21.7 us (6%)
  starting transfers between devices  18.6 us (5%)
  between operations  14.9 us (4%)
  local copies, waits for them, and re-layouts  10.9 us (3%)
    dot_general x256, matrix products, matmul(): jnp.dot(left, right, precision=lax.Precision.HIGHEST, preferred_element_t...  73.3 us
    ppermute x7, waiting for transfers between devices, passed_along(): return lax.ppermute(array, axis, pairs)  71.6 us
    all_gather x1, waiting for transfers between devices, on_device(): gathered = lax.all_gather(tokens, row_axes, axis=1, tiled=True)  70 us
    unnamed x1, blocking collectives  62.7 us
    ppermute x7, starting transfers between devices, passed_along(): return lax.ppermute(array, axis, pairs)  15.1 us
  transfers between devices with their start and end apart: 10, of which 9 were waited for; matrix products, arithmetic and copies ran while one was open for 6% of the time, Pallas kernels for 0%

profile of v1, /device:TPU:4, one launch (start us, length us, event | category | flops | bytes accessed | tf_op | source)
XLA Modules:
  0.0 355.5 jit_solution(17340669928445101169)
XLA Ops:
  6.5 0.7 all-gather.3.cloned.1.call-update
  7.9 70.0 %all-gather.3.cloned.1.call-done = bf16[2,256,3072]{2,1,0:T(8,128)(2,1)} async-done(((bf16[2,8,3072]{2,1,0:T(8,128)(2,1)}), bf16[2,256,3072]{2,1,0:T(8,128)(2,1)}) %all-gather.3.cloned.1.call-update) | async-done | bytes 3145744 | tf_op jit(solution)/shard_map/all_gather | solution.py:135
  78.0 3.4 fusion.200
  82.3 10.8 %while.130 = (s32[]{:T(128)}, f32[2,64,256]{2,1,0:T(8,128)S(1)}, f32[2,256]{1,0:T(2,128)S(1)}, f32[2,256,64]{1,2,0:T(8,128)S(1)}, f32[2,64]{1,0:T(2,128)S(1)}, /...) while((s32[]{:T(128)}, f32[2,64,256]{2,1,0:T(8,128)S(1)}, ...), condition=%wide.region_5.6_spmd, body=%wide.region_0.5_spmd.sunk | while | flops 127755136 | bytes 2386049 | solution.py:93
  84.3 0.4 convolution_subtract_fusion.38
  88.0 0.4 fusion.529
  89.6 0.4 convolution_subtract_fusion.38
  90.7 0.4 fusion.529
  92.3 0.4 convolution_subtract_fusion.38
  93.7 3.4 collective-permute-start
  97.2 10.5 %collective-permute-done = f32[2,33088]{1,0:T(2,128)S(1)} collective-permute-done((f32[2,33088]{1,0:T(2,128)S(1)}, f32[2,33088]{1,0:T(2,128)S(1)}, u32[]{:S(2)}, u32[]{:S(2)}) %collective-permute-start) | collective-permute-done | bytes 264736 | tf_op jit(solution)/shard_map/state_hop/ppermute | solution.py:19
  108.1 10.8 %while.131 = (s32[]{:T(128)}, f32[2,64,256]{2,1,0:T(8,128)S(1)}, f32[2,256]{1,0:T(2,128)S(1)}, f32[2,256,64]{1,2,0:T(8,128)S(1)}, f32[2,64]{1,0:T(2,128)S(1)}, /...) while((s32[]{:T(128)}, f32[2,64,256]{2,1,0:T(8,128)S(1)}, ...), condition=%wide.region_11.12_spmd, body=%wide.region_6.11_spmd.sunk | while | flops 127755136 | bytes 2386049 | solution.py:93
  108.4 0.4 fusion.546
  111.1 0.4 fusion.546
  112.7 0.4 convolution_subtract_fusion.40
  116.5 0.4 fusion.546
  118.1 0.4 convolution_subtract_fusion.40
  119.5 1.9 collective-permute-start.1
  121.4 11.3 %collective-permute-done.1 = f32[2,33088]{1,0:T(2,128)S(1)} collective-permute-done((f32[2,33088]{1,0:T(2,128)S(1)}, f32[2,33088]{1,0:T(2,128)S(1)}, u32[]{:S(2)}, u32[]{:S(2)}) %collective-permute-start.1) | collective-permute-done | bytes 264736 | tf_op jit(solution)/shard_map/state_hop/ppermute | solution.py:19
  133.1 10.8 %while.132 = (s32[]{:T(128)}, f32[2,64,256]{2,1,0:T(8,128)S(1)}, f32[2,256]{1,0:T(2,128)S(1)}, f32[2,256,64]{1,2,0:T(8,128)S(1)}, f32[2,64]{1,0:T(2,128)S(1)}, /...) while((s32[]{:T(128)}, f32[2,64,256]{2,1,0:T(8,128)S(1)}, ...), condition=%wide.region_17.18_spmd, body=%wide.region_12.17_spmd.sunk | while | flops 127755136 | bytes 2386049 | solution.py:93
  133.4 0.4 fusion.563
  136.1 0.4 fusion.563
  137.7 0.4 convolution_subtract_fusion.42
  141.5 0.4 fusion.563
  143.1 0.4 convolution_subtract_fusion.42
  144.4 1.9 collective-permute-start.2
  146.4 10.4 %collective-permute-done.2 = f32[2,33088]{1,0:T(2,128)S(1)} collective-permute-done((f32[2,33088]{1,0:T(2,128)S(1)}, f32[2,33088]{1,0:T(2,128)S(1)}, u32[]{:S(2)}, u32[]{:S(2)}) %collective-permute-start.2) | collective-permute-done | bytes 264736 | tf_op jit(solution)/shard_map/state_hop/ppermute | solution.py:19
  157.1 10.8 %while.133 = (s32[]{:T(128)}, f32[2,64,256]{2,1,0:T(8,128)S(1)}, f32[2,256]{1,0:T(2,128)S(1)}, f32[2,256,64]{1,2,0:T(8,128)S(1)}, f32[2,64]{1,0:T(2,128)S(1)}, /...) while((s32[]{:T(128)}, f32[2,64,256]{2,1,0:T(8,128)S(1)}, ...), condition=%wide.region_23.24_spmd, body=%wide.region_18.23_spmd.sunk | while | flops 127755136 | bytes 2386049 | solution.py:93
  157.4 0.4 fusion.580
  161.7 0.4 convolution_subtract_fusion.44
  167.2 0.4 convolution_subtract_fusion.44
  168.5 2.1 collective-permute-start.3
  170.6 9.8 %collective-permute-done.3 = f32[2,33088]{1,0:T(2,128)S(1)} collective-permute-done((f32[2,33088]{1,0:T(2,128)S(1)}, f32[2,33088]{1,0:T(2,128)S(1)}, u32[]{:S(2)}, u32[]{:S(2)}) %collective-permute-start.3) | collective-permute-done | bytes 264736 | tf_op jit(solution)/shard_map/state_hop/ppermute | solution.py:19
  180.8 10.8 %while.134 = (s32[]{:T(128)}, f32[2,64,256]{2,1,0:T(8,128)S(1)}, f32[2,256]{1,0:T(2,128)S(1)}, f32[2,256,64]{1,2,0:T(8,128)S(1)}, f32[2,64]{1,0:T(2,128)S(1)}, /...) while((s32[]{:T(128)}, f32[2,64,256]{2,1,0:T(8,128)S(1)}, ...), condition=%wide.region_29.30_spmd, body=%wide.region_24.29_spmd.sunk | while | flops 127755136 | bytes 2386049 | solution.py:93
  185.4 0.4 convolution_subtract_fusion.46
  190.8 0.4 convolution_subtract_fusion.46
  192.2 1.9 collective-permute-start.4
  194.1 10.0 %collective-permute-done.4 = f32[2,33088]{1,0:T(2,128)S(1)} collective-permute-done((f32[2,33088]{1,0:T(2,128)S(1)}, f32[2,33088]{1,0:T(2,128)S(1)}, u32[]{:S(2)}, u32[]{:S(2)}) %collective-permute-start.4) | collective-permute-done | bytes 264736 | tf_op jit(solution)/shard_map/state_hop/ppermute | solution.py:19
  204.5 10.8 %while.135 = (s32[]{:T(128)}, f32[2,64,256]{2,1,0:T(8,128)S(1)}, f32[2,256]{1,0:T(2,128)S(1)}, f32[2,256,64]{1,2,0:T(8,128)S(1)}, f32[2,64]{1,0:T(2,128)S(1)}, /...) while((s32[]{:T(128)}, f32[2,64,256]{2,1,0:T(8,128)S(1)}, ...), condition=%wide.region_35.36_spmd, body=%wide.region_30.35_spmd.sunk | while | flops 127755136 | bytes 2386049 | solution.py:93
  209.1 0.4 convolution_subtract_fusion.48
  214.5 0.4 convolution_subtract_fusion.48
  215.8 1.9 collective-permute-start.5
  217.8 10.0 %collective-permute-done.5 = f32[2,33088]{1,0:T(2,128)S(1)} collective-permute-done((f32[2,33088]{1,0:T(2,128)S(1)}, f32[2,33088]{1,0:T(2,128)S(1)}, u32[]{:S(2)}, u32[]{:S(2)}) %collective-permute-start.5) | collective-permute-done | bytes 264736 | tf_op jit(solution)/shard_map/state_hop/ppermute | solution.py:19
  228.2 10.8 %while.136 = (s32[]{:T(128)}, f32[2,64,256]{2,1,0:T(8,128)S(1)}, f32[2,256]{1,0:T(2,128)S(1)}, f32[2,256,64]{1,2,0:T(8,128)S(1)}, f32[2,64]{1,0:T(2,128)S(1)}, /...) while((s32[]{:T(128)}, f32[2,64,256]{2,1,0:T(8,128)S(1)}, ...), condition=%wide.region_41.42_spmd, body=%wide.region_36.41_spmd.sunk | while | flops 127755136 | bytes 2386049 | solution.py:93
  232.8 0.4 convolution_subtract_fusion.50
  238.2 0.4 convolution_subtract_fusion.50
  239.5 1.9 collective-permute-start.6
  241.8 9.6 %collective-permute-done.6 = f32[2,33088]{1,0:T(2,128)S(1)} collective-permute-done((f32[2,33088]{1,0:T(2,128)S(1)}, f32[2,33088]{1,0:T(2,128)S(1)}, u32[]{:S(2)}, u32[]{:S(2)}) %collective-permute-start.6) | collective-permute-done | bytes 264736 | tf_op jit(solution)/shard_map/state_hop/ppermute | solution.py:19
  251.9 20.8 %while.137 = (s32[]{:T(128)}, f32[2,64,256]{2,1,0:T(8,128)S(1)}, f32[2,256]{1,0:T(2,128)S(1)}, f32[2,256,64]{1,2,0:T(8,128)S(1)}, f32[2,64]{1,0:T(2,128)S(1)}, /...) while((s32[]{:T(128)}, f32[2,64,256]{2,1,0:T(8,128)S(1)}, ...), condition=%wide.region_49.50_spmd, body=%wide.region_42.49_spmd.sunk | while | flops 273236992 | bytes 4856473 | solution.py:93
  252.2 0.4 fusion.662
  257.3 0.4 fusion.662
  261.5 0.4 convolution_subtract_fusion.52
  266.7 0.4 convolution_subtract_fusion.52
  267.7 0.4 fusion.662
  272.7 0.8 reshape.533
  273.5 3.5 all-to-all-start
  277.0 0.6 dynamic-slice
  277.6 3.2 all-to-all-done
  281.0 1.8 convolution_bitcast_fusion
  283.0 0.9 copy.288
  283.9 62.7 %all-reduce.2 = bf16[8,49152]{1,0:T(8,128)(2,1)S(1)} all-reduce(f32[8,49152]{1,0:T(8,128)S(1)} %bitcast.719), channel_id=2, replica_groups=mesh['seq'=8,'xlo'=2,'z'=8,'core'=2] {'z'}, use_global_device_ids=true, to_apply=%region_50.51.clone | all-reduce | flops 393216 | bytes 2359296
  346.6 0.8 constant_dynamic-slice_fusion.1
  347.5 0.6 convert_reduce_fusion
  348.0 0.7 convert_element_type.25
  (650 shorter events, 90.0 us)
Async XLA Ops:
  6.5 71.4 %all-gather.3.cloned.1.call-start = ((), (), s32[]{:S(2)}) async-start(), calls=%async_computation.1 | async-start | bytes 3244032 | tf_op jit(solution)/shard_map/all_gather | solution.py:135
  7.3 273.8 %all-gather.5.cloned.1.call-start = ((), (), s32[]{:S(2)}) async-start(), calls=%async_computation.2 | async-start | bytes 1966080 | tf_op jit(solution)/shard_map/all_gather | solution.py:137
  81.4 0.9 copy-start
  81.4 0.9 copy-start.4
  81.4 0.9 copy-start.5
  81.4 0.9 copy-start.3
  81.4 0.9 copy-start.1
  81.4 0.9 copy-start.2
  93.7 14.0 %collective-permute-start = (f32[2,33088]{1,0:T(2,128)S(1)}, f32[2,33088]{1,0:T(2,128)S(1)}, u32[]{:S(2)}, u32[]{:S(2)}) collective-permute-start(f32[2,33088]{1,0:T(2,128)S(1)} %pad_maximum_fusion), channel_id=1, source_target_pairs={{0,32},{32,64},{64,96},{96,128},{128,160},{160,192},{192,224},{1,3... | collective-permute-start | bytes 794120 | tf_op jit(solution)/shard_map/state_hop/ppermute | solution.py:19
  119.5 13.2 %collective-permute-start.1 = (f32[2,33088]{1,0:T(2,128)S(1)}, f32[2,33088]{1,0:T(2,128)S(1)}, u32[]{:S(2)}, u32[]{:S(2)}) collective-permute-start(f32[2,33088]{1,0:T(2,128)S(1)} %pad_maximum_fusion.1), channel_id=1, source_target_pairs={{0,32},{32,64},{64,96},{96,128},{128,160},{160,192},{192,224},{1,3... | collective-permute-start | bytes 794120 | tf_op jit(solution)/shard_map/state_hop/ppermute | solution.py:19
  144.4 12.3 %collective-permute-start.2 = (f32[2,33088]{1,0:T(2,128)S(1)}, f32[2,33088]{1,0:T(2,128)S(1)}, u32[]{:S(2)}, u32[]{:S(2)}) collective-permute-start(f32[2,33088]{1,0:T(2,128)S(1)} %pad_maximum_fusion.2), channel_id=1, source_target_pairs={{0,32},{32,64},{64,96},{96,128},{128,160},{160,192},{192,224},{1,3... | collective-permute-start | bytes 794120 | tf_op jit(solution)/shard_map/state_hop/ppermute | solution.py:19
  168.5 11.9 %collective-permute-start.3 = (f32[2,33088]{1,0:T(2,128)S(1)}, f32[2,33088]{1,0:T(2,128)S(1)}, u32[]{:S(2)}, u32[]{:S(2)}) collective-permute-start(f32[2,33088]{1,0:T(2,128)S(1)} %pad_maximum_fusion.3), channel_id=1, source_target_pairs={{0,32},{32,64},{64,96},{96,128},{128,160},{160,192},{192,224},{1,3... | collective-permute-start | bytes 794120 | tf_op jit(solution)/shard_map/state_hop/ppermute | solution.py:19
  192.2 11.9 %collective-permute-start.4 = (f32[2,33088]{1,0:T(2,128)S(1)}, f32[2,33088]{1,0:T(2,128)S(1)}, u32[]{:S(2)}, u32[]{:S(2)}) collective-permute-start(f32[2,33088]{1,0:T(2,128)S(1)} %pad_maximum_fusion.4), channel_id=1, source_target_pairs={{0,32},{32,64},{64,96},{96,128},{128,160},{160,192},{192,224},{1,3... | collective-permute-start | bytes 794120 | tf_op jit(solution)/shard_map/state_hop/ppermute | solution.py:19
  215.8 11.9 %collective-permute-start.5 = (f32[2,33088]{1,0:T(2,128)S(1)}, f32[2,33088]{1,0:T(2,128)S(1)}, u32[]{:S(2)}, u32[]{:S(2)}) collective-permute-start(f32[2,33088]{1,0:T(2,128)S(1)} %pad_maximum_fusion.5), channel_id=1, source_target_pairs={{0,32},{32,64},{64,96},{96,128},{128,160},{160,192},{192,224},{1,3... | collective-permute-start | bytes 794120 | tf_op jit(solution)/shard_map/state_hop/ppermute | solution.py:19
  239.5 11.9 %collective-permute-start.6 = (f32[2,33088]{1,0:T(2,128)S(1)}, f32[2,33088]{1,0:T(2,128)S(1)}, u32[]{:S(2)}, u32[]{:S(2)}) collective-permute-start(f32[2,33088]{1,0:T(2,128)S(1)} %pad_maximum_fusion.6), channel_id=1, source_target_pairs={{0,32},{32,64},{64,96},{96,128},{128,160},{160,192},{192,224},{1,3... | collective-permute-start | bytes 794120 | tf_op jit(solution)/shard_map/state_hop/ppermute | solution.py:19
  251.9 25.1 %copy-start.6 = (u32[256]{0:T(256)S(1)}, u32[256]{0:T(256)}, u32[]{:S(2)}) copy-start(u32[256]{0:T(256)} %constant.275) | copy-start | bytes 3076
  273.5 7.4 %all-to-all-start = ((bf16[4,2,4096]{2,1,0:T(2,128)(2,1)}), bf16[4,2,4096]{2,1,0:T(2,128)(2,1)S(1)}, u32[]{:S(2)}, u32[]{:S(2)}) async-start(bf16[4,2,4096]{2,1,0:T(2,128)(2,1)} %reshape.533), calls=%async_computation | async-start | bytes 131072 | tf_op jit(solution)/shard_map/output_mix/all_to_all | solution.py:179
Sparse Core Ops, SparseCore 0:
  9.2 68.7 all-gather.2
  241.9 27.2 all-gather.4

commit v2 on v1

--- a/solution.py
+++ b/solution.py
@@ -166,6 +166,8 @@
     incoming = start_states
     for turn_idx in range(seq_count):
         finals, results = jax.vmap(segment)(incoming, queries, key_rows, value_rows, lr_rows)
+        if turn_idx == 1:
+            w_out_pair, finals = lax.optimization_barrier((w_out_pair, finals))
         if turn_idx + 1 < seq_count:
             with jax.named_scope("state_hop"):
                 received = unpack_state(passed_along(pack_state(finals), "seq", 1), finals)
@@ -183,10 +185,8 @@
             w_out_pair.reshape(pair_count, head_size, feat_width),
             preferred_element_type=jnp.float32,
         )
-        mixed_out = lax.psum_scatter(
-            partial_terms.reshape(z_count, -1), "z", scatter_dimension=0, tiled=True
-        )
-        mixed_out = lax.optimization_barrier(mixed_out)
+        pieces = lax.all_to_all(partial_terms, "z", 0, 0, tiled=True)
+        mixed_out = jnp.sum(pieces, axis=0)
     return mixed_out.reshape(videos, tok_part, feat_width).astype(jnp.bfloat16)
 
 

time: 356 us -> 342 us (0.961)
  blocking collectives: 62.7 us -> 53.2 us
  local copies, waits for them, and re-layouts: 10.9 us -> 6.66 us
    unnamed x1 -> x0, blocking collectives: 62.7 us -> none
    all_to_all x0 -> x2, blocking collectives: none -> 53.2 us  [the longest x1 46.7 us: on_device(): pieces = lax.all_to_all(partial_terms, 'z', 0, 0, tiled=True)]
    all_gather x1, waiting for transfers between devices: 0.02 us -> 5.24 us  [on_device(): w_out_pair = lax.all_gather(w_out, pair_axes, axis=0, tiled=True)]
  transfers between devices with their start and end apart: 10 -> 9, of which waited for: 9 -> 9; matrix products, arithmetic and copies ran while one was open for 6% -> 3% of each run, Pallas kernels for 0% -> 0%
where the time goes in v2:
time: 342 us
  waiting for transfers between devices  148 us (43%)
  matrix products  77.1 us (23%)
  blocking collectives  53.2 us (16%)
  other arithmetic  22.5 us (7%)
  starting transfers between devices  16.6 us (5%)
  between operations  14.9 us (4%)
  local copies, waits for them, and re-layouts  6.66 us (2%)
    dot_general x256, matrix products, matmul(): jnp.dot(left, right, precision=lax.Precision.HIGHEST, preferred_element_t...  73.3 us
    ppermute x7, waiting for transfers between devices, passed_along(): return lax.ppermute(array, axis, pairs)  72.5 us
    all_gather x1, waiting for transfers between devices, on_device(): gathered = lax.all_gather(tokens, row_axes, axis=1, tiled=True)  70 us
    all_to_all x1, blocking collectives, on_device(): pieces = lax.all_to_all(partial_terms, 'z', 0, 0, tiled=True)  46.7 us
    ppermute x7, starting transfers between devices, passed_along(): return lax.ppermute(array, axis, pairs)  16.5 us
    reduce_sum x32, other arithmetic, mini_step(): jnp.sum(grad_out, axis=-1, keepdims=True)  6.92 us
  transfers between devices with their start and end apart: 9, of which 9 were waited for; matrix products, arithmetic and copies ran while one was open for 3% of the time, Pallas kernels for 0%

profile of v2, /device:TPU:4, one launch (start us, length us, event | category | flops | bytes accessed | tf_op | source)
XLA Modules:
  0.0 341.9 jit_solution(8566038847159366962)
XLA Ops:
  6.5 0.7 all-gather.3.cloned.1.call-update
  7.9 70.0 %all-gather.3.cloned.1.call-done = bf16[2,256,3072]{2,1,0:T(8,128)(2,1)} async-done(((bf16[2,8,3072]{2,1,0:T(8,128)(2,1)}), bf16[2,256,3072]{2,1,0:T(8,128)(2,1)}) %all-gather.3.cloned.1.call-update) | async-done | bytes 3145744 | tf_op jit(solution)/shard_map/all_gather | solution.py:135
  78.0 3.4 fusion.200
  82.3 10.8 %while.130 = (s32[]{:T(128)}, f32[2,64,256]{2,1,0:T(8,128)S(1)}, f32[2,256]{1,0:T(2,128)S(1)}, f32[2,256,64]{1,2,0:T(8,128)S(1)}, f32[2,64]{1,0:T(2,128)S(1)}, /...) while((s32[]{:T(128)}, f32[2,64,256]{2,1,0:T(8,128)S(1)}, ...), condition=%wide.region_5.6_spmd, body=%wide.region_0.5_spmd.sunk | while | flops 127755136 | bytes 2386049 | solution.py:93
  84.3 0.4 convolution_subtract_fusion.38
  88.0 0.4 fusion.529
  89.6 0.4 convolution_subtract_fusion.38
  90.7 0.4 fusion.529
  92.3 0.4 convolution_subtract_fusion.38
  93.7 3.4 collective-permute-start
  97.2 10.5 %collective-permute-done = f32[2,33088]{1,0:T(2,128)S(1)} collective-permute-done((f32[2,33088]{1,0:T(2,128)S(1)}, f32[2,33088]{1,0:T(2,128)S(1)}, u32[]{:S(2)}, u32[]{:S(2)}) %collective-permute-start) | collective-permute-done | bytes 264736 | tf_op jit(solution)/shard_map/state_hop/ppermute | solution.py:19
  108.1 10.8 %while.131 = (s32[]{:T(128)}, f32[2,64,256]{2,1,0:T(8,128)S(1)}, f32[2,256]{1,0:T(2,128)S(1)}, f32[2,256,64]{1,2,0:T(8,128)S(1)}, f32[2,64]{1,0:T(2,128)S(1)}, /...) while((s32[]{:T(128)}, f32[2,64,256]{2,1,0:T(8,128)S(1)}, ...), condition=%wide.region_11.12_spmd, body=%wide.region_6.11_spmd.sunk | while | flops 127755136 | bytes 2386049 | solution.py:93
  108.4 0.4 fusion.546
  112.7 0.4 convolution_subtract_fusion.40
  113.8 0.4 fusion.546
  118.1 0.4 convolution_subtract_fusion.40
  118.9 5.2 %all-gather.5.cloned.1.call-done = bf16[256,3072]{1,0:T(8,128)(2,1)} async-done(((bf16[64,3072]{1,0:T(8,128)(2,1)}), bf16[256,3072]{1,0:T(8,128)(2,1)}) %all-gather.5.cloned.1.call-update) | async-done | bytes 1572880 | tf_op jit(solution)/shard_map/all_gather | solution.py:137
  124.7 3.3 collective-permute-start.1
  128.0 10.7 %collective-permute-done.1 = f32[2,33088]{1,0:T(2,128)S(1)} collective-permute-done((f32[2,33088]{1,0:T(2,128)S(1)}, f32[2,33088]{1,0:T(2,128)S(1)}, u32[]{:S(2)}, u32[]{:S(2)}) %collective-permute-start.1) | collective-permute-done | bytes 264736 | tf_op jit(solution)/shard_map/state_hop/ppermute | solution.py:19
  139.2 10.8 %while.132 = (s32[]{:T(128)}, f32[2,64,256]{2,1,0:T(8,128)S(1)}, f32[2,256]{1,0:T(2,128)S(1)}, f32[2,256,64]{1,2,0:T(8,128)S(1)}, f32[2,64]{1,0:T(2,128)S(1)}, /...) while((s32[]{:T(128)}, f32[2,64,256]{2,1,0:T(8,128)S(1)}, ...), condition=%wide.region_17.18_spmd, body=%wide.region_12.17_spmd.sunk | while | flops 127755136 | bytes 2386049 | solution.py:93
  139.5 0.4 fusion.563
  142.2 0.4 fusion.563
  143.8 0.4 convolution_subtract_fusion.42
  147.6 0.4 fusion.563
  149.2 0.4 convolution_subtract_fusion.42
  150.5 1.9 collective-permute-start.2
  152.5 11.4 %collective-permute-done.2 = f32[2,33088]{1,0:T(2,128)S(1)} collective-permute-done((f32[2,33088]{1,0:T(2,128)S(1)}, f32[2,33088]{1,0:T(2,128)S(1)}, u32[]{:S(2)}, u32[]{:S(2)}) %collective-permute-start.2) | collective-permute-done | bytes 264736 | tf_op jit(solution)/shard_map/state_hop/ppermute | solution.py:19
  164.2 10.8 %while.133 = (s32[]{:T(128)}, f32[2,64,256]{2,1,0:T(8,128)S(1)}, f32[2,256]{1,0:T(2,128)S(1)}, f32[2,256,64]{1,2,0:T(8,128)S(1)}, f32[2,64]{1,0:T(2,128)S(1)}, /...) while((s32[]{:T(128)}, f32[2,64,256]{2,1,0:T(8,128)S(1)}, ...), condition=%wide.region_23.24_spmd, body=%wide.region_18.23_spmd.sunk | while | flops 127755136 | bytes 2386049 | solution.py:93
  164.5 0.4 fusion.580
  167.2 0.4 fusion.580
  168.8 0.4 convolution_subtract_fusion.44
  172.6 0.4 fusion.580
  174.2 0.4 convolution_subtract_fusion.44
  175.6 2.1 collective-permute-start.3
  177.7 10.3 %collective-permute-done.3 = f32[2,33088]{1,0:T(2,128)S(1)} collective-permute-done((f32[2,33088]{1,0:T(2,128)S(1)}, f32[2,33088]{1,0:T(2,128)S(1)}, u32[]{:S(2)}, u32[]{:S(2)}) %collective-permute-start.3) | collective-permute-done | bytes 264736 | tf_op jit(solution)/shard_map/state_hop/ppermute | solution.py:19
  188.4 10.8 %while.134 = (s32[]{:T(128)}, f32[2,64,256]{2,1,0:T(8,128)S(1)}, f32[2,256]{1,0:T(2,128)S(1)}, f32[2,256,64]{1,2,0:T(8,128)S(1)}, f32[2,64]{1,0:T(2,128)S(1)}, /...) while((s32[]{:T(128)}, f32[2,64,256]{2,1,0:T(8,128)S(1)}, ...), condition=%wide.region_29.30_spmd, body=%wide.region_24.29_spmd.sunk | while | flops 127755136 | bytes 2386049 | solution.py:93
  191.3 0.4 fusion.597
  193.0 0.4 convolution_subtract_fusion.46
  196.7 0.4 fusion.597
  198.4 0.4 convolution_subtract_fusion.46
  199.7 1.9 collective-permute-start.4
  201.6 10.0 %collective-permute-done.4 = f32[2,33088]{1,0:T(2,128)S(1)} collective-permute-done((f32[2,33088]{1,0:T(2,128)S(1)}, f32[2,33088]{1,0:T(2,128)S(1)}, u32[]{:S(2)}, u32[]{:S(2)}) %collective-permute-start.4) | collective-permute-done | bytes 264736 | tf_op jit(solution)/shard_map/state_hop/ppermute | solution.py:19
  212.0 10.8 %while.135 = (s32[]{:T(128)}, f32[2,64,256]{2,1,0:T(8,128)S(1)}, f32[2,256]{1,0:T(2,128)S(1)}, f32[2,256,64]{1,2,0:T(8,128)S(1)}, f32[2,64]{1,0:T(2,128)S(1)}, /...) while((s32[]{:T(128)}, f32[2,64,256]{2,1,0:T(8,128)S(1)}, ...), condition=%wide.region_35.36_spmd, body=%wide.region_30.35_spmd.sunk | while | flops 127755136 | bytes 2386049 | solution.py:93
  215.0 0.4 fusion.614
  216.6 0.4 convolution_subtract_fusion.48
  220.4 0.4 fusion.614
  222.1 0.4 convolution_subtract_fusion.48
  223.4 1.9 collective-permute-start.5
  225.3 10.0 %collective-permute-done.5 = f32[2,33088]{1,0:T(2,128)S(1)} collective-permute-done((f32[2,33088]{1,0:T(2,128)S(1)}, f32[2,33088]{1,0:T(2,128)S(1)}, u32[]{:S(2)}, u32[]{:S(2)}) %collective-permute-start.5) | collective-permute-done | bytes 264736 | tf_op jit(solution)/shard_map/state_hop/ppermute | solution.py:19
  235.7 10.8 %while.136 = (s32[]{:T(128)}, f32[2,64,256]{2,1,0:T(8,128)S(1)}, f32[2,256]{1,0:T(2,128)S(1)}, f32[2,256,64]{1,2,0:T(8,128)S(1)}, f32[2,64]{1,0:T(2,128)S(1)}, /...) while((s32[]{:T(128)}, f32[2,64,256]{2,1,0:T(8,128)S(1)}, ...), condition=%wide.region_41.42_spmd, body=%wide.region_36.41_spmd.sunk | while | flops 127755136 | bytes 2386049 | solution.py:93
  240.3 0.4 convolution_subtract_fusion.50
  245.7 0.4 convolution_subtract_fusion.50
  247.1 1.9 collective-permute-start.6
  249.3 9.7 %collective-permute-done.6 = f32[2,33088]{1,0:T(2,128)S(1)} collective-permute-done((f32[2,33088]{1,0:T(2,128)S(1)}, f32[2,33088]{1,0:T(2,128)S(1)}, u32[]{:S(2)}, u32[]{:S(2)}) %collective-permute-start.6) | collective-permute-done | bytes 264736 | tf_op jit(solution)/shard_map/state_hop/ppermute | solution.py:19
  259.4 20.8 %while.137 = (s32[]{:T(128)}, f32[2,64,256]{2,1,0:T(8,128)S(1)}, f32[2,256]{1,0:T(2,128)S(1)}, f32[2,256,64]{1,2,0:T(8,128)S(1)}, f32[2,64]{1,0:T(2,128)S(1)}, /...) while((s32[]{:T(128)}, f32[2,64,256]{2,1,0:T(8,128)S(1)}, ...), condition=%wide.region_49.50_spmd, body=%wide.region_42.49_spmd.sunk | while | flops 273236992 | bytes 4856473 | solution.py:93
  263.8 0.4 convolution_subtract_fusion.52
  269.0 0.4 convolution_subtract_fusion.52
  270.1 0.4 fusion.662
  275.3 0.4 fusion.662
  279.4 0.4 convolution_subtract_fusion.52
  280.4 6.5 %all_to_all.10 = bf16[4,2,4096]{2,1,0:T(2,128)(2,1)S(1)} all-to-all(bf16[4,2,4096]{2,1,0:T(2,128)(2,1)S(1)} %reshape.525), channel_id=1, replica_groups=mesh['seq'=8,'xlo'=2,'z'=8,'core'=2] {'xlo','core'}, dimensions={0} | all-to-all | bytes 131072 | tf_op jit(solution)/shard_map/output_mix/all_to_all | solution.py:181
  287.1 0.4 convolution_bitcast_fusion
  287.6 46.7 %all_to_all.11 = f32[8,2,8,3072]{3,2,1,0:T(8,128)S(1)} all-to-all(f32[8,2,8,3072]{3,2,1,0:T(8,128)S(1)} %copy.214), channel_id=1, replica_groups=mesh['seq'=8,'xlo'=2,'z'=8,'core'=2] {'z'}, dimensions={0} | all-to-all | bytes 3145728 | tf_op jit(solution)/shard_map/output_mix/all_to_all | solution.py:188
  334.3 0.7 reduce_sum.315
  (645 shorter events, 88.1 us)
Async XLA Ops:
  6.5 71.4 %all-gather.3.cloned.1.call-start = ((), (), s32[]{:S(2)}) async-start(), calls=%async_computation.2 | async-start | bytes 3244032 | tf_op jit(solution)/shard_map/all_gather | solution.py:135
  7.3 116.9 %all-gather.5.cloned.1.call-start = ((), (), s32[]{:S(2)}) async-start(), calls=%async_computation.3 | async-start | bytes 1966080 | tf_op jit(solution)/shard_map/all_gather | solution.py:137
  81.4 0.9 copy-start
  81.4 0.9 copy-start.4
  81.4 0.9 copy-start.5
  81.4 0.9 copy-start.3
  81.4 0.9 copy-start.1
  81.4 0.9 copy-start.2
  93.7 14.0 %collective-permute-start = (f32[2,33088]{1,0:T(2,128)S(1)}, f32[2,33088]{1,0:T(2,128)S(1)}, u32[]{:S(2)}, u32[]{:S(2)}) collective-permute-start(f32[2,33088]{1,0:T(2,128)S(1)} %pad_maximum_fusion), channel_id=1, source_target_pairs={{0,32},{32,64},{64,96},{96,128},{128,160},{160,192},{192,224},{1,3... | collective-permute-start | bytes 794120 | tf_op jit(solution)/shard_map/state_hop/ppermute | solution.py:19
  124.7 14.1 %collective-permute-start.1 = (f32[2,33088]{1,0:T(2,128)S(1)}, f32[2,33088]{1,0:T(2,128)S(1)}, u32[]{:S(2)}, u32[]{:S(2)}) collective-permute-start(f32[2,33088]{1,0:T(2,128)S(1)} %pad_maximum_fusion.1), channel_id=1, source_target_pairs={{0,32},{32,64},{64,96},{96,128},{128,160},{160,192},{192,224},{1,3... | collective-permute-start | bytes 794120 | tf_op jit(solution)/shard_map/state_hop/ppermute | solution.py:19
  150.5 13.3 %collective-permute-start.2 = (f32[2,33088]{1,0:T(2,128)S(1)}, f32[2,33088]{1,0:T(2,128)S(1)}, u32[]{:S(2)}, u32[]{:S(2)}) collective-permute-start(f32[2,33088]{1,0:T(2,128)S(1)} %pad_maximum_fusion.2), channel_id=1, source_target_pairs={{0,32},{32,64},{64,96},{96,128},{128,160},{160,192},{192,224},{1,3... | collective-permute-start | bytes 794120 | tf_op jit(solution)/shard_map/state_hop/ppermute | solution.py:19
  175.6 12.4 %collective-permute-start.3 = (f32[2,33088]{1,0:T(2,128)S(1)}, f32[2,33088]{1,0:T(2,128)S(1)}, u32[]{:S(2)}, u32[]{:S(2)}) collective-permute-start(f32[2,33088]{1,0:T(2,128)S(1)} %pad_maximum_fusion.3), channel_id=1, source_target_pairs={{0,32},{32,64},{64,96},{96,128},{128,160},{160,192},{192,224},{1,3... | collective-permute-start | bytes 794120 | tf_op jit(solution)/shard_map/state_hop/ppermute | solution.py:19
  199.7 11.9 %collective-permute-start.4 = (f32[2,33088]{1,0:T(2,128)S(1)}, f32[2,33088]{1,0:T(2,128)S(1)}, u32[]{:S(2)}, u32[]{:S(2)}) collective-permute-start(f32[2,33088]{1,0:T(2,128)S(1)} %pad_maximum_fusion.4), channel_id=1, source_target_pairs={{0,32},{32,64},{64,96},{96,128},{128,160},{160,192},{192,224},{1,3... | collective-permute-start | bytes 794120 | tf_op jit(solution)/shard_map/state_hop/ppermute | solution.py:19
  223.4 11.9 %collective-permute-start.5 = (f32[2,33088]{1,0:T(2,128)S(1)}, f32[2,33088]{1,0:T(2,128)S(1)}, u32[]{:S(2)}, u32[]{:S(2)}) collective-permute-start(f32[2,33088]{1,0:T(2,128)S(1)} %pad_maximum_fusion.5), channel_id=1, source_target_pairs={{0,32},{32,64},{64,96},{96,128},{128,160},{160,192},{192,224},{1,3... | collective-permute-start | bytes 794120 | tf_op jit(solution)/shard_map/state_hop/ppermute | solution.py:19
  247.1 11.9 %collective-permute-start.6 = (f32[2,33088]{1,0:T(2,128)S(1)}, f32[2,33088]{1,0:T(2,128)S(1)}, u32[]{:S(2)}, u32[]{:S(2)}) collective-permute-start(f32[2,33088]{1,0:T(2,128)S(1)} %pad_maximum_fusion.6), channel_id=1, source_target_pairs={{0,32},{32,64},{64,96},{96,128},{128,160},{160,192},{192,224},{1,3... | collective-permute-start | bytes 794120 | tf_op jit(solution)/shard_map/state_hop/ppermute | solution.py:19
  259.4 27.6 %copy-start.6 = (bf16[256,3072]{1,0:T(8,128)(2,1)S(1)}, bf16[256,3072]{1,0:T(8,128)(2,1)}, u32[]{:S(2)}) copy-start(bf16[256,3072]{1,0:T(8,128)(2,1)} %all-gather.5.cloned.1.call-done) | copy-start | bytes 4718596
Sparse Core Ops, SparseCore 0:
  9.2 68.7 all-gather.2
  97.3 26.7 all-gather.4

commit v3 on v2

--- a/solution.py
+++ b/solution.py
@@ -3,7 +3,11 @@
 import jax
 import jax.numpy as jnp
 from jax import lax
+from jax.experimental import pallas as pl
+from jax.experimental.pallas import tpu as pltpu
 from jax.sharding import PartitionSpec as P
+
+MESH_ID = pl.DeviceIdType.MESH
 
 MINI = 64
 
@@ -109,6 +113,51 @@
     return tuple(parts)
 
 
+def exchange_kernel(peer_count, part_ref, recv_ref, send_sems, recv_sems, own_sem):
+    me = lax.axis_index("z")
+    barrier = pltpu.get_barrier_semaphore()
+    for step in range(1, peer_count):
+        peer = lax.rem(me + step, peer_count)
+        pl.semaphore_signal(barrier, inc=1, device_id={"z": peer}, device_id_type=MESH_ID)
+    pl.semaphore_wait(barrier, peer_count - 1)
+    own = pltpu.make_async_copy(part_ref.at[me], recv_ref.at[me], own_sem)
+    own.start()
+    copies = []
+    for step in range(1, peer_count):
+        peer = lax.rem(me + step, peer_count)
+        copy = pltpu.make_async_remote_copy(
+            src_ref=part_ref.at[peer],
+            dst_ref=recv_ref.at[me],
+            send_sem=send_sems.at[step],
+            recv_sem=recv_sems.at[step],
+            device_id={"z": peer},
+            device_id_type=MESH_ID,
+        )
+        copy.start()
+        copies.append(copy)
+    for copy in copies:
+        copy.wait()
+    own.wait()
+
+
+def exchange_over_z(pieces):
+    peer_count = pieces.shape[0]
+    moved = pieces.size * pieces.dtype.itemsize
+    return pl.pallas_call(
+        partial(exchange_kernel, peer_count),
+        out_shape=jax.ShapeDtypeStruct(pieces.shape, pieces.dtype),
+        in_specs=[pl.BlockSpec(memory_space=pl.ANY)],
+        out_specs=pl.BlockSpec(memory_space=pl.ANY),
+        scratch_shapes=[
+            pltpu.SemaphoreType.DMA((peer_count,)),
+            pltpu.SemaphoreType.DMA((peer_count,)),
+            pltpu.SemaphoreType.DMA(()),
+        ],
+        compiler_params=pltpu.CompilerParams(collective_id=0, has_side_effects=True),
+        cost_estimate=pl.CostEstimate(flops=0, bytes_accessed=2 * moved, transcendentals=0),
+    )(pieces)
+
+
 def on_device(
     tokens,
     w_qkv,
@@ -185,7 +234,7 @@
             w_out_pair.reshape(pair_count, head_size, feat_width),
             preferred_element_type=jnp.float32,
         )
-        pieces = lax.all_to_all(partial_terms, "z", 0, 0, tiled=True)
+        pieces = exchange_over_z(partial_terms.reshape(z_count, -1))
         mixed_out = jnp.sum(pieces, axis=0)
     return mixed_out.reshape(videos, tok_part, feat_width).astype(jnp.bfloat16)
 

time: 342 us -> 340 us (level)
  blocking collectives: 53.2 us -> 6.49 us
  Pallas kernels: 0 us -> 40.9 us
    all_to_all x1 -> x0, blocking collectives: 46.7 us -> none  [on_device(): pieces = lax.all_to_all(partial_terms, 'z', 0, 0, tiled=True)]
    pallas_call x0 -> x1, Pallas kernels: none -> 40.9 us  [exchange_over_z(): pl.pallas_call(partial(exchange_kernel, peer_count), out_shape=jax.ShapeD...]
where the time goes in v3:
time: 340 us
  waiting for transfers between devices  148 us (44%)
  matrix products  77.1 us (23%)
  Pallas kernels  40.9 us (12%)
  other arithmetic  23.5 us (7%)
  starting transfers between devices  16.6 us (5%)
  between operations  14.9 us (4%)
  local copies, waits for them, and re-layouts  9.27 us (3%)
  blocking collectives  6.49 us (2%)
    dot_general x256, matrix products, matmul(): jnp.dot(left, right, precision=lax.Precision.HIGHEST, preferred_element_t...  73.3 us
    ppermute x7, waiting for transfers between devices, passed_along(): return lax.ppermute(array, axis, pairs)  72.5 us
    all_gather x1, waiting for transfers between devices, on_device(): gathered = lax.all_gather(tokens, row_axes, axis=1, tiled=True)  70 us
    pallas_call x1, Pallas kernels, exchange_over_z(): pl.pallas_call(partial(exchange_kernel, peer_count), out_shape=jax.ShapeD...  40.9 us
    ppermute x7, starting transfers between devices, passed_along(): return lax.ppermute(array, axis, pairs)  16.5 us
    reduce_sum x32, other arithmetic, mini_step(): jnp.sum(grad_out, axis=-1, keepdims=True)  6.92 us
  transfers between devices with their start and end apart: 9, of which 9 were waited for; matrix products, arithmetic and copies ran while one was open for 3% of the time, Pallas kernels for 0%

profile of v3, /device:TPU:4, one launch (start us, length us, event | category | flops | bytes accessed | tf_op | source)
XLA Modules:
  0.0 339.7 jit_solution(3895531808743941191)
XLA Ops:
  6.5 0.7 all-gather.3.cloned.1.call-update
  7.9 70.0 %all-gather.3.cloned.1.call-done = bf16[2,256,3072]{2,1,0:T(8,128)(2,1)} async-done(((bf16[2,8,3072]{2,1,0:T(8,128)(2,1)}), bf16[2,256,3072]{2,1,0:T(8,128)(2,1)}) %all-gather.3.cloned.1.call-update) | async-done | bytes 3145744 | tf_op jit(solution)/shard_map/all_gather | solution.py:184
  78.0 3.4 fusion.200
  82.3 10.8 %while.130 = (s32[]{:T(128)}, f32[2,64,256]{2,1,0:T(8,128)S(1)}, f32[2,256]{1,0:T(2,128)S(1)}, f32[2,256,64]{1,2,0:T(8,128)S(1)}, f32[2,64]{1,0:T(2,128)S(1)}, /...) while((s32[]{:T(128)}, f32[2,64,256]{2,1,0:T(8,128)S(1)}, ...), condition=%wide.region_5.6_spmd, body=%wide.region_0.5_spmd.sunk | while | flops 127755136 | bytes 2386049 | solution.py:97
  84.3 0.4 convolution_subtract_fusion.38
  88.0 0.4 fusion.529
  89.6 0.4 convolution_subtract_fusion.38
  90.7 0.4 fusion.529
  92.3 0.4 convolution_subtract_fusion.38
  93.7 3.4 collective-permute-start
  97.2 10.5 %collective-permute-done = f32[2,33088]{1,0:T(2,128)S(1)} collective-permute-done((f32[2,33088]{1,0:T(2,128)S(1)}, f32[2,33088]{1,0:T(2,128)S(1)}, u32[]{:S(2)}, u32[]{:S(2)}) %collective-permute-start) | collective-permute-done | bytes 264736 | tf_op jit(solution)/shard_map/state_hop/ppermute | solution.py:23
  108.1 10.8 %while.131 = (s32[]{:T(128)}, f32[2,64,256]{2,1,0:T(8,128)S(1)}, f32[2,256]{1,0:T(2,128)S(1)}, f32[2,256,64]{1,2,0:T(8,128)S(1)}, f32[2,64]{1,0:T(2,128)S(1)}, /...) while((s32[]{:T(128)}, f32[2,64,256]{2,1,0:T(8,128)S(1)}, ...), condition=%wide.region_11.12_spmd, body=%wide.region_6.11_spmd.sunk | while | flops 127755136 | bytes 2386049 | solution.py:97
  108.4 0.4 fusion.546
  112.7 0.4 convolution_subtract_fusion.40
  113.8 0.4 fusion.546
  118.1 0.4 convolution_subtract_fusion.40
  118.9 5.2 %all-gather.5.cloned.1.call-done = bf16[256,3072]{1,0:T(8,128)(2,1)} async-done(((bf16[64,3072]{1,0:T(8,128)(2,1)}), bf16[256,3072]{1,0:T(8,128)(2,1)}) %all-gather.5.cloned.1.call-update) | async-done | bytes 1572880 | tf_op jit(solution)/shard_map/all_gather | solution.py:186
  124.7 3.3 collective-permute-start.1
  128.0 10.7 %collective-permute-done.1 = f32[2,33088]{1,0:T(2,128)S(1)} collective-permute-done((f32[2,33088]{1,0:T(2,128)S(1)}, f32[2,33088]{1,0:T(2,128)S(1)}, u32[]{:S(2)}, u32[]{:S(2)}) %collective-permute-start.1) | collective-permute-done | bytes 264736 | tf_op jit(solution)/shard_map/state_hop/ppermute | solution.py:23
  139.2 10.8 %while.132 = (s32[]{:T(128)}, f32[2,64,256]{2,1,0:T(8,128)S(1)}, f32[2,256]{1,0:T(2,128)S(1)}, f32[2,256,64]{1,2,0:T(8,128)S(1)}, f32[2,64]{1,0:T(2,128)S(1)}, /...) while((s32[]{:T(128)}, f32[2,64,256]{2,1,0:T(8,128)S(1)}, ...), condition=%wide.region_17.18_spmd, body=%wide.region_12.17_spmd.sunk | while | flops 127755136 | bytes 2386049 | solution.py:97
  139.5 0.4 fusion.563
  142.2 0.4 fusion.563
  143.8 0.4 convolution_subtract_fusion.42
  147.6 0.4 fusion.563
  149.2 0.4 convolution_subtract_fusion.42
  150.5 1.9 collective-permute-start.2
  152.5 11.4 %collective-permute-done.2 = f32[2,33088]{1,0:T(2,128)S(1)} collective-permute-done((f32[2,33088]{1,0:T(2,128)S(1)}, f32[2,33088]{1,0:T(2,128)S(1)}, u32[]{:S(2)}, u32[]{:S(2)}) %collective-permute-start.2) | collective-permute-done | bytes 264736 | tf_op jit(solution)/shard_map/state_hop/ppermute | solution.py:23
  164.2 10.8 %while.133 = (s32[]{:T(128)}, f32[2,64,256]{2,1,0:T(8,128)S(1)}, f32[2,256]{1,0:T(2,128)S(1)}, f32[2,256,64]{1,2,0:T(8,128)S(1)}, f32[2,64]{1,0:T(2,128)S(1)}, /...) while((s32[]{:T(128)}, f32[2,64,256]{2,1,0:T(8,128)S(1)}, ...), condition=%wide.region_23.24_spmd, body=%wide.region_18.23_spmd.sunk | while | flops 127755136 | bytes 2386049 | solution.py:97
  164.5 0.4 fusion.580
  167.2 0.4 fusion.580
  168.8 0.4 convolution_subtract_fusion.44
  172.6 0.4 fusion.580
  174.2 0.4 convolution_subtract_fusion.44
  175.6 2.1 collective-permute-start.3
  177.7 10.3 %collective-permute-done.3 = f32[2,33088]{1,0:T(2,128)S(1)} collective-permute-done((f32[2,33088]{1,0:T(2,128)S(1)}, f32[2,33088]{1,0:T(2,128)S(1)}, u32[]{:S(2)}, u32[]{:S(2)}) %collective-permute-start.3) | collective-permute-done | bytes 264736 | tf_op jit(solution)/shard_map/state_hop/ppermute | solution.py:23
  188.4 10.8 %while.134 = (s32[]{:T(128)}, f32[2,64,256]{2,1,0:T(8,128)S(1)}, f32[2,256]{1,0:T(2,128)S(1)}, f32[2,256,64]{1,2,0:T(8,128)S(1)}, f32[2,64]{1,0:T(2,128)S(1)}, /...) while((s32[]{:T(128)}, f32[2,64,256]{2,1,0:T(8,128)S(1)}, ...), condition=%wide.region_29.30_spmd, body=%wide.region_24.29_spmd.sunk | while | flops 127755136 | bytes 2386049 | solution.py:97
  191.3 0.4 fusion.597
  193.0 0.4 convolution_subtract_fusion.46
  196.7 0.4 fusion.597
  198.4 0.4 convolution_subtract_fusion.46
  199.7 1.9 collective-permute-start.4
  201.6 10.0 %collective-permute-done.4 = f32[2,33088]{1,0:T(2,128)S(1)} collective-permute-done((f32[2,33088]{1,0:T(2,128)S(1)}, f32[2,33088]{1,0:T(2,128)S(1)}, u32[]{:S(2)}, u32[]{:S(2)}) %collective-permute-start.4) | collective-permute-done | bytes 264736 | tf_op jit(solution)/shard_map/state_hop/ppermute | solution.py:23
  212.0 10.8 %while.135 = (s32[]{:T(128)}, f32[2,64,256]{2,1,0:T(8,128)S(1)}, f32[2,256]{1,0:T(2,128)S(1)}, f32[2,256,64]{1,2,0:T(8,128)S(1)}, f32[2,64]{1,0:T(2,128)S(1)}, /...) while((s32[]{:T(128)}, f32[2,64,256]{2,1,0:T(8,128)S(1)}, ...), condition=%wide.region_35.36_spmd, body=%wide.region_30.35_spmd.sunk | while | flops 127755136 | bytes 2386049 | solution.py:97
  216.6 0.4 convolution_subtract_fusion.48
  222.1 0.4 convolution_subtract_fusion.48
  223.4 1.9 collective-permute-start.5
  225.3 10.0 %collective-permute-done.5 = f32[2,33088]{1,0:T(2,128)S(1)} collective-permute-done((f32[2,33088]{1,0:T(2,128)S(1)}, f32[2,33088]{1,0:T(2,128)S(1)}, u32[]{:S(2)}, u32[]{:S(2)}) %collective-permute-start.5) | collective-permute-done | bytes 264736 | tf_op jit(solution)/shard_map/state_hop/ppermute | solution.py:23
  235.7 10.8 %while.136 = (s32[]{:T(128)}, f32[2,64,256]{2,1,0:T(8,128)S(1)}, f32[2,256]{1,0:T(2,128)S(1)}, f32[2,256,64]{1,2,0:T(8,128)S(1)}, f32[2,64]{1,0:T(2,128)S(1)}, /...) while((s32[]{:T(128)}, f32[2,64,256]{2,1,0:T(8,128)S(1)}, ...), condition=%wide.region_41.42_spmd, body=%wide.region_36.41_spmd.sunk | while | flops 127755136 | bytes 2386049 | solution.py:97
  240.3 0.4 convolution_subtract_fusion.50
  245.7 0.4 convolution_subtract_fusion.50
  247.1 1.9 collective-permute-start.6
  249.3 9.7 %collective-permute-done.6 = f32[2,33088]{1,0:T(2,128)S(1)} collective-permute-done((f32[2,33088]{1,0:T(2,128)S(1)}, f32[2,33088]{1,0:T(2,128)S(1)}, u32[]{:S(2)}, u32[]{:S(2)}) %collective-permute-start.6) | collective-permute-done | bytes 264736 | tf_op jit(solution)/shard_map/state_hop/ppermute | solution.py:23
  259.4 20.8 %while.137 = (s32[]{:T(128)}, f32[2,64,256]{2,1,0:T(8,128)S(1)}, f32[2,256]{1,0:T(2,128)S(1)}, f32[2,256,64]{1,2,0:T(8,128)S(1)}, f32[2,64]{1,0:T(2,128)S(1)}, /...) while((s32[]{:T(128)}, f32[2,64,256]{2,1,0:T(8,128)S(1)}, ...), condition=%wide.region_49.50_spmd, body=%wide.region_42.49_spmd.sunk | while | flops 273236992 | bytes 4856473 | solution.py:97
  263.8 0.4 convolution_subtract_fusion.52
  269.0 0.4 convolution_subtract_fusion.52
  270.1 0.4 fusion.662
  275.3 0.4 fusion.662
  279.4 0.4 convolution_subtract_fusion.52
  280.4 6.5 %all_to_all.5 = bf16[4,2,4096]{2,1,0:T(2,128)(2,1)S(1)} all-to-all(bf16[4,2,4096]{2,1,0:T(2,128)(2,1)S(1)} %reshape.531), channel_id=1, replica_groups=mesh['seq'=8,'xlo'=2,'z'=8,'core'=2] {'xlo','core'}, dimensions={0} | all-to-all | bytes 131072 | tf_op jit(solution)/shard_map/output_mix/all_to_all | solution.py:230
  287.1 0.4 convolution_bitcast_fusion
  287.5 2.1 copy.216
  289.5 40.9 %output_mix.1 = f32[8,49152]{1,0:T(8,128)} custom-call(f32[8,49152]{1,0:T(8,128)} %bitcast.713), custom_call_target="tpu_custom_call" | custom-call | bytes 3145728 | tf_op jit(solution)/shard_map/output_mix/pallas_call | solution.py:146
  330.4 1.8 reduce_sum.315
  332.2 0.7 convert_element_type.25
  (646 shorter events, 88.8 us)
Async XLA Ops:
  6.5 71.4 %all-gather.3.cloned.1.call-start = ((), (), s32[]{:S(2)}) async-start(), calls=%async_computation.1 | async-start | bytes 3244032 | tf_op jit(solution)/shard_map/all_gather | solution.py:184
  7.3 116.9 %all-gather.5.cloned.1.call-start = ((), (), s32[]{:S(2)}) async-start(), calls=%async_computation.2 | async-start | bytes 1966080 | tf_op jit(solution)/shard_map/all_gather | solution.py:186
  81.4 0.9 copy-start
  81.4 0.9 copy-start.4
  81.4 0.9 copy-start.5
  81.4 0.9 copy-start.3
  81.4 0.9 copy-start.1
  81.4 0.9 copy-start.2
  93.7 14.0 %collective-permute-start = (f32[2,33088]{1,0:T(2,128)S(1)}, f32[2,33088]{1,0:T(2,128)S(1)}, u32[]{:S(2)}, u32[]{:S(2)}) collective-permute-start(f32[2,33088]{1,0:T(2,128)S(1)} %pad_maximum_fusion), channel_id=1, source_target_pairs={{0,32},{32,64},{64,96},{96,128},{128,160},{160,192},{192,224},{1,3... | collective-permute-start | bytes 794120 | tf_op jit(solution)/shard_map/state_hop/ppermute | solution.py:23
  124.7 14.1 %collective-permute-start.1 = (f32[2,33088]{1,0:T(2,128)S(1)}, f32[2,33088]{1,0:T(2,128)S(1)}, u32[]{:S(2)}, u32[]{:S(2)}) collective-permute-start(f32[2,33088]{1,0:T(2,128)S(1)} %pad_maximum_fusion.1), channel_id=1, source_target_pairs={{0,32},{32,64},{64,96},{96,128},{128,160},{160,192},{192,224},{1,3... | collective-permute-start | bytes 794120 | tf_op jit(solution)/shard_map/state_hop/ppermute | solution.py:23
  150.5 13.3 %collective-permute-start.2 = (f32[2,33088]{1,0:T(2,128)S(1)}, f32[2,33088]{1,0:T(2,128)S(1)}, u32[]{:S(2)}, u32[]{:S(2)}) collective-permute-start(f32[2,33088]{1,0:T(2,128)S(1)} %pad_maximum_fusion.2), channel_id=1, source_target_pairs={{0,32},{32,64},{64,96},{96,128},{128,160},{160,192},{192,224},{1,3... | collective-permute-start | bytes 794120 | tf_op jit(solution)/shard_map/state_hop/ppermute | solution.py:23
  175.6 12.4 %collective-permute-start.3 = (f32[2,33088]{1,0:T(2,128)S(1)}, f32[2,33088]{1,0:T(2,128)S(1)}, u32[]{:S(2)}, u32[]{:S(2)}) collective-permute-start(f32[2,33088]{1,0:T(2,128)S(1)} %pad_maximum_fusion.3), channel_id=1, source_target_pairs={{0,32},{32,64},{64,96},{96,128},{128,160},{160,192},{192,224},{1,3... | collective-permute-start | bytes 794120 | tf_op jit(solution)/shard_map/state_hop/ppermute | solution.py:23
  199.7 11.9 %collective-permute-start.4 = (f32[2,33088]{1,0:T(2,128)S(1)}, f32[2,33088]{1,0:T(2,128)S(1)}, u32[]{:S(2)}, u32[]{:S(2)}) collective-permute-start(f32[2,33088]{1,0:T(2,128)S(1)} %pad_maximum_fusion.4), channel_id=1, source_target_pairs={{0,32},{32,64},{64,96},{96,128},{128,160},{160,192},{192,224},{1,3... | collective-permute-start | bytes 794120 | tf_op jit(solution)/shard_map/state_hop/ppermute | solution.py:23
  223.4 11.9 %collective-permute-start.5 = (f32[2,33088]{1,0:T(2,128)S(1)}, f32[2,33088]{1,0:T(2,128)S(1)}, u32[]{:S(2)}, u32[]{:S(2)}) collective-permute-start(f32[2,33088]{1,0:T(2,128)S(1)} %pad_maximum_fusion.5), channel_id=1, source_target_pairs={{0,32},{32,64},{64,96},{96,128},{128,160},{160,192},{192,224},{1,3... | collective-permute-start | bytes 794120 | tf_op jit(solution)/shard_map/state_hop/ppermute | solution.py:23
  247.1 11.9 %collective-permute-start.6 = (f32[2,33088]{1,0:T(2,128)S(1)}, f32[2,33088]{1,0:T(2,128)S(1)}, u32[]{:S(2)}, u32[]{:S(2)}) collective-permute-start(f32[2,33088]{1,0:T(2,128)S(1)} %pad_maximum_fusion.6), channel_id=1, source_target_pairs={{0,32},{32,64},{64,96},{96,128},{128,160},{160,192},{192,224},{1,3... | collective-permute-start | bytes 794120 | tf_op jit(solution)/shard_map/state_hop/ppermute | solution.py:23
  259.4 27.6 %copy-start.6 = (bf16[256,3072]{1,0:T(8,128)(2,1)S(1)}, bf16[256,3072]{1,0:T(8,128)(2,1)}, u32[]{:S(2)}) copy-start(bf16[256,3072]{1,0:T(8,128)(2,1)} %all-gather.5.cloned.1.call-done) | copy-start | bytes 4718596
Sparse Core Ops, SparseCore 0:
  9.2 68.7 all-gather.2
  97.3 26.7 all-gather.4

commit v4 on v3

--- a/solution.py
+++ b/solution.py
@@ -234,8 +234,10 @@
             w_out_pair.reshape(pair_count, head_size, feat_width),
             preferred_element_type=jnp.float32,
         )
-        pieces = exchange_over_z(partial_terms.reshape(z_count, -1))
-        mixed_out = jnp.sum(pieces, axis=0)
+        pieces = exchange_over_z(
+            partial_terms.reshape(z_count, -1, 1024).astype(jnp.bfloat16)
+        )
+        mixed_out = jnp.sum(pieces.astype(jnp.float32), axis=0)
     return mixed_out.reshape(videos, tok_part, feat_width).astype(jnp.bfloat16)
 
 

time: 340 us -> 322 us (0.947)
  Pallas kernels: 40.9 us -> 24 us
    pallas_call x1, Pallas kernels: 40.9 us -> 24 us  [exchange_over_z(): pl.pallas_call(partial(exchange_kernel, peer_count), out_shape=jax.ShapeD...]
  transfers between devices with their start and end apart: 9 -> 9, of which waited for: 9 -> 9; matrix products, arithmetic and copies ran while one was open for 3% -> 4% of each run, Pallas kernels for 0% -> 0%
where the time goes in v4:
time: 322 us
  waiting for transfers between devices  148 us (46%)
  matrix products  77.1 us (24%)
  Pallas kernels  24 us (7%)
  other arithmetic  23 us (7%)
  starting transfers between devices  16.6 us (5%)
  between operations  14.9 us (5%)
  local copies, waits for them, and re-layouts  8.5 us (3%)
  blocking collectives  6.49 us (2%)
    dot_general x256, matrix products, matmul(): jnp.dot(left, right, precision=lax.Precision.HIGHEST, preferred_element_t...  73.3 us
    ppermute x7, waiting for transfers between devices, passed_along(): return lax.ppermute(array, axis, pairs)  72.5 us
    all_gather x1, waiting for transfers between devices, on_device(): gathered = lax.all_gather(tokens, row_axes, axis=1, tiled=True)  70 us
    pallas_call x1, Pallas kernels, exchange_over_z(): pl.pallas_call(partial(exchange_kernel, peer_count), out_shape=jax.ShapeD...  24 us
    ppermute x7, starting transfers between devices, passed_along(): return lax.ppermute(array, axis, pairs)  16.5 us
    reduce_sum x32, other arithmetic, mini_step(): jnp.sum(grad_out, axis=-1, keepdims=True)  6.92 us
    all_to_all x1, blocking collectives, on_device(): by_head = lax.all_to_all(by_owner, pair_axes, 0, 0, tiled=True)  6.49 us
  transfers between devices with their start and end apart: 9, of which 9 were waited for; matrix products, arithmetic and copies ran while one was open for 4% of the time, Pallas kernels for 0%

profile of v4, /device:TPU:4, one launch (start us, length us, event | category | flops | bytes accessed | tf_op | source)
XLA Modules:
  0.0 321.6 jit_solution(7346157195290737458)
XLA Ops:
  6.5 0.7 all-gather.3.cloned.1.call-update
  7.9 70.0 %all-gather.3.cloned.1.call-done = bf16[2,256,3072]{2,1,0:T(8,128)(2,1)} async-done(((bf16[2,8,3072]{2,1,0:T(8,128)(2,1)}), bf16[2,256,3072]{2,1,0:T(8,128)(2,1)}) %all-gather.3.cloned.1.call-update) | async-done | bytes 3145744 | tf_op jit(solution)/shard_map/all_gather | solution.py:184
  78.0 3.4 %fusion.202 = f32[2,256,193]{1,2,0:T(8,128)S(1)} fusion(bf16[2,256,3072]{2,1,0:T(8,128)(2,1)} %all-gather.3.cloned.1.call-done, bf16[1,3072]{1,0:T(2,128)(2,1)} %param.29, bf16[192,3072]{1,0:T(8,128)(2,1)} %param.28), kind=kOutput, calls=%fused_computation.369 | convolution fusion | flops 609497088 | bytes 4726784 | tf_op jit(solution)/shard_map/vkd,cd->vkc/dot_general | solution.py:187
  82.3 10.8 %while.130 = (s32[]{:T(128)}, f32[2,64,256]{2,1,0:T(8,128)S(1)}, f32[2,256]{1,0:T(2,128)S(1)}, f32[2,256,64]{1,2,0:T(8,128)S(1)}, f32[2,64]{1,0:T(2,128)S(1)}, /...) while((s32[]{:T(128)}, f32[2,64,256]{2,1,0:T(8,128)S(1)}, ...), condition=%wide.region_5.6_spmd, body=%wide.region_0.5_spmd.sunk | while | flops 127755136 | bytes 2386049 | solution.py:97
  84.3 0.4 convolution_subtract_fusion.38
  88.0 0.4 fusion.531
  89.6 0.4 convolution_subtract_fusion.38
  90.7 0.4 fusion.531
  92.3 0.4 convolution_subtract_fusion.38
  93.7 3.4 %collective-permute-start = (f32[2,33088]{1,0:T(2,128)S(1)}, f32[2,33088]{1,0:T(2,128)S(1)}, u32[]{:S(2)}, u32[]{:S(2)}) collective-permute-start(f32[2,33088]{1,0:T(2,128)S(1)} %pad_maximum_fusion), channel_id=1, source_target_pairs={{0,32},{32,64},{64,96},{96,128},{128,160},{160,192},{192,224},{1,3... | collective-permute-start | bytes 794120 | tf_op jit(solution)/shard_map/state_hop/ppermute | solution.py:23
  97.2 10.5 %collective-permute-done = f32[2,33088]{1,0:T(2,128)S(1)} collective-permute-done((f32[2,33088]{1,0:T(2,128)S(1)}, f32[2,33088]{1,0:T(2,128)S(1)}, u32[]{:S(2)}, u32[]{:S(2)}) %collective-permute-start) | collective-permute-done | bytes 264736 | tf_op jit(solution)/shard_map/state_hop/ppermute | solution.py:23
  108.1 10.8 %while.131 = (s32[]{:T(128)}, f32[2,64,256]{2,1,0:T(8,128)S(1)}, f32[2,256]{1,0:T(2,128)S(1)}, f32[2,256,64]{1,2,0:T(8,128)S(1)}, f32[2,64]{1,0:T(2,128)S(1)}, /...) while((s32[]{:T(128)}, f32[2,64,256]{2,1,0:T(8,128)S(1)}, ...), condition=%wide.region_11.12_spmd, body=%wide.region_6.11_spmd.sunk | while | flops 127755136 | bytes 2386049 | solution.py:97
  108.4 0.4 fusion.548
  112.7 0.4 convolution_subtract_fusion.40
  113.8 0.4 fusion.548
  118.1 0.4 convolution_subtract_fusion.40
  118.9 5.2 %all-gather.5.cloned.1.call-done = bf16[256,3072]{1,0:T(8,128)(2,1)} async-done(((bf16[64,3072]{1,0:T(8,128)(2,1)}), bf16[256,3072]{1,0:T(8,128)(2,1)}) %all-gather.5.cloned.1.call-update) | async-done | bytes 1572880 | tf_op jit(solution)/shard_map/all_gather | solution.py:186
  124.7 3.3 %collective-permute-start.1 = (f32[2,33088]{1,0:T(2,128)S(1)}, f32[2,33088]{1,0:T(2,128)S(1)}, u32[]{:S(2)}, u32[]{:S(2)}) collective-permute-start(f32[2,33088]{1,0:T(2,128)S(1)} %pad_maximum_fusion.1), channel_id=1, source_target_pairs={{0,32},{32,64},{64,96},{96,128},{128,160},{160,192},{192,224},{1,3... | collective-permute-start | bytes 794120 | tf_op jit(solution)/shard_map/state_hop/ppermute | solution.py:23
  128.0 10.7 %collective-permute-done.1 = f32[2,33088]{1,0:T(2,128)S(1)} collective-permute-done((f32[2,33088]{1,0:T(2,128)S(1)}, f32[2,33088]{1,0:T(2,128)S(1)}, u32[]{:S(2)}, u32[]{:S(2)}) %collective-permute-start.1) | collective-permute-done | bytes 264736 | tf_op jit(solution)/shard_map/state_hop/ppermute | solution.py:23
  139.2 10.8 %while.132 = (s32[]{:T(128)}, f32[2,64,256]{2,1,0:T(8,128)S(1)}, f32[2,256]{1,0:T(2,128)S(1)}, f32[2,256,64]{1,2,0:T(8,128)S(1)}, f32[2,64]{1,0:T(2,128)S(1)}, /...) while((s32[]{:T(128)}, f32[2,64,256]{2,1,0:T(8,128)S(1)}, ...), condition=%wide.region_17.18_spmd, body=%wide.region_12.17_spmd.sunk | while | flops 127755136 | bytes 2386049 | solution.py:97
  139.5 0.4 fusion.565
  142.2 0.4 fusion.565
  143.8 0.4 convolution_subtract_fusion.42
  147.6 0.4 fusion.565
  149.2 0.4 convolution_subtract_fusion.42
  150.5 1.9 collective-permute-start.2
  152.5 11.4 %collective-permute-done.2 = f32[2,33088]{1,0:T(2,128)S(1)} collective-permute-done((f32[2,33088]{1,0:T(2,128)S(1)}, f32[2,33088]{1,0:T(2,128)S(1)}, u32[]{:S(2)}, u32[]{:S(2)}) %collective-permute-start.2) | collective-permute-done | bytes 264736 | tf_op jit(solution)/shard_map/state_hop/ppermute | solution.py:23
  164.2 10.8 %while.133 = (s32[]{:T(128)}, f32[2,64,256]{2,1,0:T(8,128)S(1)}, f32[2,256]{1,0:T(2,128)S(1)}, f32[2,256,64]{1,2,0:T(8,128)S(1)}, f32[2,64]{1,0:T(2,128)S(1)}, /...) while((s32[]{:T(128)}, f32[2,64,256]{2,1,0:T(8,128)S(1)}, ...), condition=%wide.region_23.24_spmd, body=%wide.region_18.23_spmd.sunk | while | flops 127755136 | bytes 2386049 | solution.py:97
  164.5 0.4 fusion.582
  167.2 0.4 fusion.582
  168.8 0.4 convolution_subtract_fusion.44
  172.6 0.4 fusion.582
  174.2 0.4 convolution_subtract_fusion.44
  175.6 2.1 collective-permute-start.3
  177.7 10.3 %collective-permute-done.3 = f32[2,33088]{1,0:T(2,128)S(1)} collective-permute-done((f32[2,33088]{1,0:T(2,128)S(1)}, f32[2,33088]{1,0:T(2,128)S(1)}, u32[]{:S(2)}, u32[]{:S(2)}) %collective-permute-start.3) | collective-permute-done | bytes 264736 | tf_op jit(solution)/shard_map/state_hop/ppermute | solution.py:23
  188.4 10.8 %while.134 = (s32[]{:T(128)}, f32[2,64,256]{2,1,0:T(8,128)S(1)}, f32[2,256]{1,0:T(2,128)S(1)}, f32[2,256,64]{1,2,0:T(8,128)S(1)}, f32[2,64]{1,0:T(2,128)S(1)}, /...) while((s32[]{:T(128)}, f32[2,64,256]{2,1,0:T(8,128)S(1)}, ...), condition=%wide.region_29.30_spmd, body=%wide.region_24.29_spmd.sunk | while | flops 127755136 | bytes 2386049 | solution.py:97
  191.3 0.4 fusion.599
  193.0 0.4 convolution_subtract_fusion.46
  196.7 0.4 fusion.599
  198.4 0.4 convolution_subtract_fusion.46
  199.7 1.9 collective-permute-start.4
  201.6 10.0 %collective-permute-done.4 = f32[2,33088]{1,0:T(2,128)S(1)} collective-permute-done((f32[2,33088]{1,0:T(2,128)S(1)}, f32[2,33088]{1,0:T(2,128)S(1)}, u32[]{:S(2)}, u32[]{:S(2)}) %collective-permute-start.4) | collective-permute-done | bytes 264736 | tf_op jit(solution)/shard_map/state_hop/ppermute | solution.py:23
  212.0 10.8 %while.135 = (s32[]{:T(128)}, f32[2,64,256]{2,1,0:T(8,128)S(1)}, f32[2,256]{1,0:T(2,128)S(1)}, f32[2,256,64]{1,2,0:T(8,128)S(1)}, f32[2,64]{1,0:T(2,128)S(1)}, /...) while((s32[]{:T(128)}, f32[2,64,256]{2,1,0:T(8,128)S(1)}, ...), condition=%wide.region_35.36_spmd, body=%wide.region_30.35_spmd.sunk | while | flops 127755136 | bytes 2386049 | solution.py:97
  216.6 0.4 convolution_subtract_fusion.48
  222.1 0.4 convolution_subtract_fusion.48
  223.4 1.9 collective-permute-start.5
  225.3 10.0 %collective-permute-done.5 = f32[2,33088]{1,0:T(2,128)S(1)} collective-permute-done((f32[2,33088]{1,0:T(2,128)S(1)}, f32[2,33088]{1,0:T(2,128)S(1)}, u32[]{:S(2)}, u32[]{:S(2)}) %collective-permute-start.5) | collective-permute-done | bytes 264736 | tf_op jit(solution)/shard_map/state_hop/ppermute | solution.py:23
  235.7 10.8 %while.136 = (s32[]{:T(128)}, f32[2,64,256]{2,1,0:T(8,128)S(1)}, f32[2,256]{1,0:T(2,128)S(1)}, f32[2,256,64]{1,2,0:T(8,128)S(1)}, f32[2,64]{1,0:T(2,128)S(1)}, /...) while((s32[]{:T(128)}, f32[2,64,256]{2,1,0:T(8,128)S(1)}, ...), condition=%wide.region_41.42_spmd, body=%wide.region_36.41_spmd.sunk | while | flops 127755136 | bytes 2386049 | solution.py:97
  240.3 0.4 convolution_subtract_fusion.50
  245.7 0.4 convolution_subtract_fusion.50
  247.1 1.9 collective-permute-start.6
  249.3 9.7 %collective-permute-done.6 = f32[2,33088]{1,0:T(2,128)S(1)} collective-permute-done((f32[2,33088]{1,0:T(2,128)S(1)}, f32[2,33088]{1,0:T(2,128)S(1)}, u32[]{:S(2)}, u32[]{:S(2)}) %collective-permute-start.6) | collective-permute-done | bytes 264736 | tf_op jit(solution)/shard_map/state_hop/ppermute | solution.py:23
  259.4 20.8 %while.137 = (s32[]{:T(128)}, f32[2,64,256]{2,1,0:T(8,128)S(1)}, f32[2,256]{1,0:T(2,128)S(1)}, f32[2,256,64]{1,2,0:T(8,128)S(1)}, f32[2,64]{1,0:T(2,128)S(1)}, /...) while((s32[]{:T(128)}, f32[2,64,256]{2,1,0:T(8,128)S(1)}, ...), condition=%wide.region_49.50_spmd, body=%wide.region_42.49_spmd.sunk | while | flops 273236992 | bytes 4856473 | solution.py:97
  263.8 0.4 convolution_subtract_fusion.52
  269.0 0.4 convolution_subtract_fusion.52
  270.1 0.4 fusion.664
  275.3 0.4 fusion.664
  279.4 0.4 convolution_subtract_fusion.52
  280.4 6.5 %all_to_all.5 = bf16[4,2,4096]{2,1,0:T(2,128)(2,1)S(1)} all-to-all(bf16[4,2,4096]{2,1,0:T(2,128)(2,1)S(1)} %reshape.529), channel_id=1, replica_groups=mesh['seq'=8,'xlo'=2,'z'=8,'core'=2] {'xlo','core'}, dimensions={0} | all-to-all | bytes 131072 | tf_op jit(solution)/shard_map/output_mix/all_to_all | solution.py:230
  287.1 0.4 fusion.201
  287.5 1.2 convert_element_type.32.part_ref
  288.8 24.0 %output_mix.1 = bf16[8,48,1024]{2,1,0:T(8,128)(2,1)} custom-call(bf16[8,48,1024]{2,1,0:T(8,128)(2,1)} %convert_element_type.32.part_ref), custom_call_target="tpu_custom_call" | custom-call | bytes 1572864 | tf_op jit(solution)/shard_map/output_mix/pallas_call | solution.py:146
  312.8 1.3 reduce_sum.318
  314.0 0.7 convert_element_type.33
  (647 shorter events, 88.8 us)
Async XLA Ops:
  6.5 71.4 %all-gather.3.cloned.1.call-start = ((), (), s32[]{:S(2)}) async-start(), calls=%async_computation.1 | async-start | bytes 3244032 | tf_op jit(solution)/shard_map/all_gather | solution.py:184
  7.3 116.9 %all-gather.5.cloned.1.call-start = ((), (), s32[]{:S(2)}) async-start(), calls=%async_computation.2 | async-start | bytes 1966080 | tf_op jit(solution)/shard_map/all_gather | solution.py:186
  81.4 0.9 copy-start
  81.4 0.9 copy-start.4
  81.4 0.9 copy-start.5
  81.4 0.9 copy-start.3
  81.4 0.9 copy-start.1
  81.4 0.9 copy-start.2
  93.7 14.0 %collective-permute-start = (f32[2,33088]{1,0:T(2,128)S(1)}, f32[2,33088]{1,0:T(2,128)S(1)}, u32[]{:S(2)}, u32[]{:S(2)}) collective-permute-start(f32[2,33088]{1,0:T(2,128)S(1)} %pad_maximum_fusion), channel_id=1, source_target_pairs={{0,32},{32,64},{64,96},{96,128},{128,160},{160,192},{192,224},{1,3... | collective-permute-start | bytes 794120 | tf_op jit(solution)/shard_map/state_hop/ppermute | solution.py:23
  124.7 14.1 %collective-permute-start.1 = (f32[2,33088]{1,0:T(2,128)S(1)}, f32[2,33088]{1,0:T(2,128)S(1)}, u32[]{:S(2)}, u32[]{:S(2)}) collective-permute-start(f32[2,33088]{1,0:T(2,128)S(1)} %pad_maximum_fusion.1), channel_id=1, source_target_pairs={{0,32},{32,64},{64,96},{96,128},{128,160},{160,192},{192,224},{1,3... | collective-permute-start | bytes 794120 | tf_op jit(solution)/shard_map/state_hop/ppermute | solution.py:23
  150.5 13.3 %collective-permute-start.2 = (f32[2,33088]{1,0:T(2,128)S(1)}, f32[2,33088]{1,0:T(2,128)S(1)}, u32[]{:S(2)}, u32[]{:S(2)}) collective-permute-start(f32[2,33088]{1,0:T(2,128)S(1)} %pad_maximum_fusion.2), channel_id=1, source_target_pairs={{0,32},{32,64},{64,96},{96,128},{128,160},{160,192},{192,224},{1,3... | collective-permute-start | bytes 794120 | tf_op jit(solution)/shard_map/state_hop/ppermute | solution.py:23
  175.6 12.4 %collective-permute-start.3 = (f32[2,33088]{1,0:T(2,128)S(1)}, f32[2,33088]{1,0:T(2,128)S(1)}, u32[]{:S(2)}, u32[]{:S(2)}) collective-permute-start(f32[2,33088]{1,0:T(2,128)S(1)} %pad_maximum_fusion.3), channel_id=1, source_target_pairs={{0,32},{32,64},{64,96},{96,128},{128,160},{160,192},{192,224},{1,3... | collective-permute-start | bytes 794120 | tf_op jit(solution)/shard_map/state_hop/ppermute | solution.py:23
  199.7 11.9 %collective-permute-start.4 = (f32[2,33088]{1,0:T(2,128)S(1)}, f32[2,33088]{1,0:T(2,128)S(1)}, u32[]{:S(2)}, u32[]{:S(2)}) collective-permute-start(f32[2,33088]{1,0:T(2,128)S(1)} %pad_maximum_fusion.4), channel_id=1, source_target_pairs={{0,32},{32,64},{64,96},{96,128},{128,160},{160,192},{192,224},{1,3... | collective-permute-start | bytes 794120 | tf_op jit(solution)/shard_map/state_hop/ppermute | solution.py:23
  223.4 11.9 %collective-permute-start.5 = (f32[2,33088]{1,0:T(2,128)S(1)}, f32[2,33088]{1,0:T(2,128)S(1)}, u32[]{:S(2)}, u32[]{:S(2)}) collective-permute-start(f32[2,33088]{1,0:T(2,128)S(1)} %pad_maximum_fusion.5), channel_id=1, source_target_pairs={{0,32},{32,64},{64,96},{96,128},{128,160},{160,192},{192,224},{1,3... | collective-permute-start | bytes 794120 | tf_op jit(solution)/shard_map/state_hop/ppermute | solution.py:23
  247.1 11.9 %collective-permute-start.6 = (f32[2,33088]{1,0:T(2,128)S(1)}, f32[2,33088]{1,0:T(2,128)S(1)}, u32[]{:S(2)}, u32[]{:S(2)}) collective-permute-start(f32[2,33088]{1,0:T(2,128)S(1)} %pad_maximum_fusion.6), channel_id=1, source_target_pairs={{0,32},{32,64},{64,96},{96,128},{128,160},{160,192},{192,224},{1,3... | collective-permute-start | bytes 794120 | tf_op jit(solution)/shard_map/state_hop/ppermute | solution.py:23
  259.4 27.6 %copy-start.6 = (bf16[256,3072]{1,0:T(8,128)(2,1)S(1)}, bf16[256,3072]{1,0:T(8,128)(2,1)}, u32[]{:S(2)}) copy-start(bf16[256,3072]{1,0:T(8,128)(2,1)} %all-gather.5.cloned.1.call-done) | copy-start | bytes 4718596
Sparse Core Ops, SparseCore 0:
  9.2 68.7 all-gather.2
  97.3 26.7 all-gather.4

commit v5 on v4

--- a/solution.py
+++ b/solution.py
@@ -98,6 +98,118 @@
     return (inner_state, results.reshape(queries.shape[0], -1))
 
 
+def turn_kernel(
+    w1_ref, b1_ref, w2_ref, b2_ref, q_ref, k_ref, v_ref, lrr_ref, lrc_ref, gain_ref, bias_ref,
+    w1_out, b1_out, w2_out, b2_out, res_ref,
+):
+    videos = q_ref.shape[0]
+    blocks = q_ref.shape[1] // MINI
+    feat = q_ref.shape[2]
+    gain = gain_ref[...]
+    bias = bias_ref[...]
+    lower = lax.broadcasted_iota(jnp.int32, (MINI, MINI), 0) >= lax.broadcasted_iota(
+        jnp.int32, (MINI, MINI), 1
+    )
+
+    def dot_nt(left, right):
+        return lax.dot_general(
+            left, right, (((1,), (1,)), ((), ())),
+            precision=lax.Precision.HIGHEST, preferred_element_type=jnp.float32,
+        )
+
+    def norm_rows(entries):
+        centred = entries - jnp.mean(entries, axis=-1, keepdims=True)
+        spread = jnp.sqrt(jnp.mean(centred * centred, axis=-1, keepdims=True) + ln_eps)
+        return centred / spread, spread
+
+    def one_block(blk, carried):
+        start = pl.multiple_of(blk * MINI, MINI)
+        span = pl.ds(start, MINI)
+        updated = []
+        for vid in range(videos):
+            w_first, b_first, w_second, b_second = carried[vid]
+            queries = q_ref[vid, span, :]
+            key_rows = k_ref[vid, span, :]
+            value_rows = v_ref[vid, span, :]
+            eta_row = lrr_ref[vid, pl.ds(blk, 1), :] / MINI
+            eta_col = lrc_ref[vid, span, :] / MINI
+            hidden_pre = matmul(key_rows, w_first) + b_first
+            hidden = gelu_tanh(hidden_pre)
+            second = matmul(hidden, w_second) + b_second
+            target = value_rows - key_rows
+            normed, spread = norm_rows(second)
+            grad_out = gain * (gain * normed + bias - target)
+            grad_second = (
+                feat * grad_out
+                - jnp.sum(grad_out, axis=-1, keepdims=True)
+                - normed * jnp.sum(grad_out * normed, axis=-1, keepdims=True)
+            ) / (feat * spread)
+            grad_first = dot_nt(grad_second, w_second) * gelu_slope(hidden_pre)
+            eta_table = jnp.where(lower, eta_row, 0.0)
+            query_keys = dot_nt(queries, key_rows) * eta_table
+            bias_first = b_first - matmul(eta_table, grad_first)
+            first_bar = matmul(queries, w_first) - matmul(query_keys, grad_first) + bias_first
+            hidden_bar = gelu_tanh(first_bar)
+            hidden_pairs = dot_nt(hidden_bar, hidden) * eta_table
+            bias_second = b_second - matmul(eta_table, grad_second)
+            second_bar = (
+                matmul(hidden_bar, w_second) - matmul(hidden_pairs, grad_second) + bias_second
+            )
+            w_first = w_first - matmul(jnp.transpose(key_rows * eta_col), grad_first)
+            b_first = b_first - jnp.sum(eta_col * grad_first, axis=0, keepdims=True)
+            w_second = w_second - matmul(jnp.transpose(hidden * eta_col), grad_second)
+            b_second = b_second - jnp.sum(eta_col * grad_second, axis=0, keepdims=True)
+            normed_bar, _ = norm_rows(second_bar)
+            res_ref[vid, span, :] = queries + gain * normed_bar + bias
+            updated.append((w_first, b_first, w_second, b_second))
+        return tuple(updated)
+
+    states = tuple(
+        (w1_ref[vid], b1_ref[vid], w2_ref[vid], b2_ref[vid]) for vid in range(videos)
+    )
+    states = lax.fori_loop(0, blocks, one_block, states)
+    for vid in range(videos):
+        w_first, b_first, w_second, b_second = states[vid]
+        w1_out[vid] = w_first
+        b1_out[vid] = b_first
+        w2_out[vid] = w_second
+        b2_out[vid] = b_second
+
+
+def run_turn(inner_state, queries, key_rows, value_rows, lr_rows, norm_gain, offset):
+    w_first, b_first, w_second, b_second = inner_state
+    videos, seg_len, feat = queries.shape
+    blocks = seg_len // MINI
+    hidden_width = w_first.shape[-1]
+    state_shapes = (
+        jax.ShapeDtypeStruct(w_first.shape, jnp.float32),
+        jax.ShapeDtypeStruct((videos, 1, hidden_width), jnp.float32),
+        jax.ShapeDtypeStruct(w_second.shape, jnp.float32),
+        jax.ShapeDtypeStruct((videos, 1, feat), jnp.float32),
+    )
+    flops = 2 * videos * blocks * MINI * (10 * MINI * hidden_width + 4 * MINI * feat) * 6
+    w1n, b1n, w2n, b2n, results = pl.pallas_call(
+        turn_kernel,
+        out_shape=state_shapes + (jax.ShapeDtypeStruct(queries.shape, jnp.float32),),
+        cost_estimate=pl.CostEstimate(
+            flops=flops, bytes_accessed=4 * (4 * queries.size + 4 * w_first.size), transcendentals=0
+        ),
+    )(
+        w_first,
+        b_first.reshape(videos, 1, hidden_width),
+        w_second,
+        b_second.reshape(videos, 1, feat),
+        queries,
+        key_rows,
+        value_rows,
+        lr_rows.reshape(videos, blocks, MINI),
+        lr_rows.reshape(videos, seg_len, 1),
+        norm_gain.reshape(1, feat),
+        offset.reshape(1, feat),
+    )
+    return (w1n, b1n.reshape(videos, hidden_width), w2n, b2n.reshape(videos, feat)), results
+
+
 def pack_state(state):
     videos = state[0].shape[0]
     return jnp.concatenate([part.reshape(videos, -1) for part in state], axis=1)
@@ -214,7 +326,9 @@
     start_states = jax.tree.map(spread_videos, initial)
     incoming = start_states
     for turn_idx in range(seq_count):
-        finals, results = jax.vmap(segment)(incoming, queries, key_rows, value_rows, lr_rows)
+        finals, results = run_turn(
+            incoming, queries, key_rows, value_rows, lr_rows, norm_gain, offset
+        )
         if turn_idx == 1:
             w_out_pair, finals = lax.optimization_barrier((w_out_pair, finals))
         if turn_idx + 1 < seq_count:

time: 322 us -> 395 us (1.23)
  Pallas kernels: 24 us -> 157 us
  matrix products: 77.1 us -> 3.79 us
  local copies, waits for them, and re-layouts: 8.5 us -> 32.8 us
  waiting for transfers between devices: 148 us -> 142 us
    pallas_call x0 -> x8, Pallas kernels: none -> 135 us  [run_turn(): pl.pallas_call(turn_kernel, out_shape=state_shapes + (jax.ShapeDtypeStruc...]
    dot_general x256 -> x0, matrix products: 73.3 us -> none  [matmul(): jnp.dot(left, right, precision=lax.Precision.HIGHEST, preferred_element_t...]
    select_n x28 -> x22, other arithmetic: 0.35 us -> 13.7 us  [on_device(): jax.tree.map(partial(jnp.where, first_device), start_states, received)]
    reduce_sum x68 -> x0, other arithmetic: 12.9 us -> none  [the longest x32 6.92 us: mini_step(): jnp.sum(grad_out, axis=-1, keepdims=True)]
    unnamed x23 -> x26, local copies, waits for them, and re-layouts: 1.07 us -> 12.3 us
    reshape x7, local copies, waits for them, and re-layouts: 1.02 us -> 7.66 us  [pack_state(): return jnp.concatenate([part.reshape(videos, -1) for part in state], axis=1)]
    div x132 -> x0, other arithmetic: 5.86 us -> none  [the longest x32 5.02 us: mini_step(): (feat_width * grad_out - jnp.sum(grad_out, axis=-1, keepdims=True) - norm...]
    all_gather x1, waiting for transfers between devices: 5.24 us -> 0.01 us  [on_device(): w_out_pair = lax.all_gather(w_out, pair_axes, axis=0, tiled=True)]
  transfers between devices with their start and end apart: 9 -> 9, of which waited for: 9 -> 8; matrix products, arithmetic and copies ran while one was open for 4% -> 1% of each run, Pallas kernels for 0% -> 4%
where the time goes in v5:
time: 395 us; the launch traced here: 394 us
  Pallas kernels  157 us (40%)
  waiting for transfers between devices  142 us (36%)
  local copies, waits for them, and re-layouts  32.8 us (8%)
  other arithmetic  22.2 us (6%)
  starting transfers between devices  15.4 us (4%)
  between operations  14.4 us (4%)
  blocking collectives  6.49 us (2%)
    pallas_call x8, Pallas kernels, run_turn(): pl.pallas_call(turn_kernel, out_shape=state_shapes + (jax.ShapeDtypeStruc...  135 us
    ppermute x7, waiting for transfers between devices, passed_along(): return lax.ppermute(array, axis, pairs)  71.8 us
    all_gather x1, waiting for transfers between devices, on_device(): gathered = lax.all_gather(tokens, row_axes, axis=1, tiled=True)  69.1 us
    pallas_call x1, Pallas kernels, exchange_over_z(): pl.pallas_call(partial(exchange_kernel, peer_count), out_shape=jax.ShapeD...  22.6 us
    ppermute x7, starting transfers between devices, passed_along(): return lax.ppermute(array, axis, pairs)  15.3 us
    select_n x22, other arithmetic, on_device(): jax.tree.map(partial(jnp.where, first_device), start_states, received)  13.7 us
    unnamed x26, local copies, waits for them, and re-layouts  12.3 us
  transfers between devices with their start and end apart: 9, of which 8 were waited for; matrix products, arithmetic and copies ran while one was open for 1% of the time, Pallas kernels for 4%

profile of v5, /device:TPU:4, one launch (start us, length us, event | category | flops | bytes accessed | tf_op | source)
XLA Modules:
  0.0 394.0 jit_solution(14774435778175979284)
XLA Ops:
  6.5 0.7 all-gather.3.cloned.1.call-update
  7.9 0.9 copy.67
  8.9 69.1 %all-gather.3.cloned.1.call-done = bf16[2,256,3072]{2,1,0:T(8,128)(2,1)} async-done(((bf16[2,8,3072]{2,1,0:T(8,128)(2,1)}), bf16[2,256,3072]{2,1,0:T(8,128)(2,1)}) %all-gather.3.cloned.1.call-update) | async-done | bytes 3145744 | tf_op jit(solution)/shard_map/all_gather | solution.py:296
  78.0 3.4 fusion.2
  81.6 0.9 fusion.20
  82.7 0.8 fusion.12
  83.5 0.7 reshape.274.lrr_ref
  84.1 0.7 broadcast_in_dim.13.w2_ref
  86.7 16.8 %shard_map.109 = (f32[2,64,256]{2,1,0:T(8,128)}, f32[2,1,256]{2,1,0:T(1,128)}, f32[2,256,64]{2,1,0:T(8,128)}, f32[2,1,64]{2,1,0:T(1,128)}, f32[2,256,64]{2,1,0:T(8,128)}) custom-call(f32[2,64,256]{2,1,0:T(8,128)} %broadcast_in_dim.12.w1_ref, f32[2,1,256]{2,1,0:T(1,128)} %reshape.210.b1_ref, f32[2,256,64]{2,1,0:T(8,128)} %broadcast_in_dim.13.w2_ref, ...), custom_call_target="tpu_custom_call" | custom-call | flops 1107296256 | bytes 1048576 | tf_op jit(solution)/shard_map/pallas_call | solution.py:191
  103.5 1.0 copy.99
  104.5 1.1 reshape.214
  106.3 0.8 pad_maximum_fusion
  107.0 3.4 collective-permute-start
  110.5 10.6 %collective-permute-done = f32[2,33088]{1,0:T(2,128)S(1)} collective-permute-done((f32[2,33088]{1,0:T(2,128)S(1)}, f32[2,33088]{1,0:T(2,128)S(1)}, u32[]{:S(2)}, u32[]{:S(2)}) %collective-permute-start) | collective-permute-done | bytes 264736 | tf_op jit(solution)/shard_map/state_hop/ppermute | solution.py:23
  123.1 0.8 broadcast_select_fusion.6.w2_ref
  123.9 16.8 %shard_map.110 = (f32[2,64,256]{2,1,0:T(8,128)}, f32[2,1,256]{2,1,0:T(1,128)}, f32[2,256,64]{2,1,0:T(8,128)}, f32[2,1,64]{2,1,0:T(1,128)}, f32[2,256,64]{2,1,0:T(8,128)}) custom-call(f32[2,64,256]{2,1,0:T(8,128)} %bitcast_select_fusion.6.w1_ref, f32[2,1,256]{2,1,0:T(1,128)} %copy.71.b1_ref, f32[2,256,64]{2,1,0:T(8,128)} %broadcast_select_fusion.6.w2_ref, ...), custom_call_target="tpu_custom_call" | custom-call | flops 1107296256 | bytes 1048576 | tf_op jit(solution)/shard_map/pallas_call | solution.py:191
  141.4 1.0 copy.101
  142.4 1.1 reshape.224
  143.5 0.8 pad_maximum_fusion.1
  144.2 1.9 collective-permute-start.1
  146.2 11.3 %collective-permute-done.1 = f32[2,33088]{1,0:T(2,128)S(1)} collective-permute-done((f32[2,33088]{1,0:T(2,128)S(1)}, f32[2,33088]{1,0:T(2,128)S(1)}, u32[]{:S(2)}, u32[]{:S(2)}) %collective-permute-start.1) | collective-permute-done | bytes 264736 | tf_op jit(solution)/shard_map/state_hop/ppermute | solution.py:23
  157.7 0.8 broadcast_select_fusion.5.w2_ref
  160.3 16.8 %shard_map.111 = (f32[2,64,256]{2,1,0:T(8,128)}, f32[2,1,256]{2,1,0:T(1,128)}, f32[2,256,64]{2,1,0:T(8,128)}, f32[2,1,64]{2,1,0:T(1,128)}, f32[2,256,64]{2,1,0:T(8,128)}) custom-call(f32[2,64,256]{2,1,0:T(8,128)} %bitcast_select_fusion.5.w1_ref, f32[2,1,256]{2,1,0:T(1,128)} %copy.73.b1_ref, f32[2,256,64]{2,1,0:T(8,128)} %broadcast_select_fusion.5.w2_ref, ...), custom_call_target="tpu_custom_call" | custom-call | flops 1107296256 | bytes 1048576 | tf_op jit(solution)/shard_map/pallas_call | solution.py:191
  177.1 1.0 copy.103
  178.1 1.1 reshape.231
  179.9 0.8 pad_maximum_fusion.2
  180.6 2.1 collective-permute-start.2
  182.8 10.2 %collective-permute-done.2 = f32[2,33088]{1,0:T(2,128)S(1)} collective-permute-done((f32[2,33088]{1,0:T(2,128)S(1)}, f32[2,33088]{1,0:T(2,128)S(1)}, u32[]{:S(2)}, u32[]{:S(2)}) %collective-permute-start.2) | collective-permute-done | bytes 264736 | tf_op jit(solution)/shard_map/state_hop/ppermute | solution.py:23
  193.2 0.8 broadcast_select_fusion.4.w2_ref
  195.8 16.8 %shard_map.112 = (f32[2,64,256]{2,1,0:T(8,128)}, f32[2,1,256]{2,1,0:T(1,128)}, f32[2,256,64]{2,1,0:T(8,128)}, f32[2,1,64]{2,1,0:T(1,128)}, f32[2,256,64]{2,1,0:T(8,128)}) custom-call(f32[2,64,256]{2,1,0:T(8,128)} %bitcast_select_fusion.4.w1_ref, f32[2,1,256]{2,1,0:T(1,128)} %copy.75.b1_ref, f32[2,256,64]{2,1,0:T(8,128)} %broadcast_select_fusion.4.w2_ref, ...), custom_call_target="tpu_custom_call" | custom-call | flops 1107296256 | bytes 1048576 | tf_op jit(solution)/shard_map/pallas_call | solution.py:191
  212.6 1.0 copy.105
  213.6 1.1 reshape.239
  215.4 0.8 pad_maximum_fusion.3
  216.1 1.9 collective-permute-start.3
  218.1 10.0 %collective-permute-done.3 = f32[2,33088]{1,0:T(2,128)S(1)} collective-permute-done((f32[2,33088]{1,0:T(2,128)S(1)}, f32[2,33088]{1,0:T(2,128)S(1)}, u32[]{:S(2)}, u32[]{:S(2)}) %collective-permute-start.3) | collective-permute-done | bytes 264736 | tf_op jit(solution)/shard_map/state_hop/ppermute | solution.py:23
  228.3 0.8 broadcast_select_fusion.3.w2_ref
  230.8 16.8 %shard_map.113 = (f32[2,64,256]{2,1,0:T(8,128)}, f32[2,1,256]{2,1,0:T(1,128)}, f32[2,256,64]{2,1,0:T(8,128)}, f32[2,1,64]{2,1,0:T(1,128)}, f32[2,256,64]{2,1,0:T(8,128)}) custom-call(f32[2,64,256]{2,1,0:T(8,128)} %bitcast_select_fusion.3.w1_ref, f32[2,1,256]{2,1,0:T(1,128)} %copy.77.b1_ref, f32[2,256,64]{2,1,0:T(8,128)} %broadcast_select_fusion.3.w2_ref, ...), custom_call_target="tpu_custom_call" | custom-call | flops 1107296256 | bytes 1048576 | tf_op jit(solution)/shard_map/pallas_call | solution.py:191
  247.7 1.0 copy.107
  248.7 1.1 reshape.247
  250.4 0.8 pad_maximum_fusion.4
  251.2 1.9 collective-permute-start.4
  253.1 10.0 %collective-permute-done.4 = f32[2,33088]{1,0:T(2,128)S(1)} collective-permute-done((f32[2,33088]{1,0:T(2,128)S(1)}, f32[2,33088]{1,0:T(2,128)S(1)}, u32[]{:S(2)}, u32[]{:S(2)}) %collective-permute-start.4) | collective-permute-done | bytes 264736 | tf_op jit(solution)/shard_map/state_hop/ppermute | solution.py:23
  263.3 0.8 broadcast_select_fusion.2.w2_ref
  265.9 16.8 %shard_map.114 = (f32[2,64,256]{2,1,0:T(8,128)}, f32[2,1,256]{2,1,0:T(1,128)}, f32[2,256,64]{2,1,0:T(8,128)}, f32[2,1,64]{2,1,0:T(1,128)}, f32[2,256,64]{2,1,0:T(8,128)}) custom-call(f32[2,64,256]{2,1,0:T(8,128)} %bitcast_select_fusion.2.w1_ref, f32[2,1,256]{2,1,0:T(1,128)} %copy.79.b1_ref, f32[2,256,64]{2,1,0:T(8,128)} %broadcast_select_fusion.2.w2_ref, ...), custom_call_target="tpu_custom_call" | custom-call | flops 1107296256 | bytes 1048576 | tf_op jit(solution)/shard_map/pallas_call | solution.py:191
  282.7 1.0 copy.109
  283.7 1.1 reshape.255
  285.5 0.8 pad_maximum_fusion.5
  286.3 2.1 collective-permute-start.5
  288.4 9.8 %collective-permute-done.5 = f32[2,33088]{1,0:T(2,128)S(1)} collective-permute-done((f32[2,33088]{1,0:T(2,128)S(1)}, f32[2,33088]{1,0:T(2,128)S(1)}, u32[]{:S(2)}, u32[]{:S(2)}) %collective-permute-start.5) | collective-permute-done | bytes 264736 | tf_op jit(solution)/shard_map/state_hop/ppermute | solution.py:23
  298.4 0.8 broadcast_select_fusion.1.w2_ref
  301.0 16.8 %shard_map.115 = (f32[2,64,256]{2,1,0:T(8,128)}, f32[2,1,256]{2,1,0:T(1,128)}, f32[2,256,64]{2,1,0:T(8,128)}, f32[2,1,64]{2,1,0:T(1,128)}, f32[2,256,64]{2,1,0:T(8,128)}) custom-call(f32[2,64,256]{2,1,0:T(8,128)} %bitcast_select_fusion.1.w1_ref, f32[2,1,256]{2,1,0:T(1,128)} %copy.81.b1_ref, f32[2,256,64]{2,1,0:T(8,128)} %broadcast_select_fusion.1.w2_ref, ...), custom_call_target="tpu_custom_call" | custom-call | flops 1107296256 | bytes 1048576 | tf_op jit(solution)/shard_map/pallas_call | solution.py:191
  317.8 1.0 copy.111
  318.8 1.1 reshape.263
  320.6 0.8 pad_maximum_fusion.6
  321.4 1.9 collective-permute-start.6
  323.3 10.0 %collective-permute-done.6 = f32[2,33088]{1,0:T(2,128)S(1)} collective-permute-done((f32[2,33088]{1,0:T(2,128)S(1)}, f32[2,33088]{1,0:T(2,128)S(1)}, u32[]{:S(2)}, u32[]{:S(2)}) %collective-permute-start.6) | collective-permute-done | bytes 264736 | tf_op jit(solution)/shard_map/state_hop/ppermute | solution.py:23
  333.5 0.8 broadcast_select_fusion.w2_ref
  336.1 16.9 %shard_map.116 = (f32[2,64,256]{2,1,0:T(8,128)}, f32[2,1,256]{2,1,0:T(1,128)}, f32[2,256,64]{2,1,0:T(8,128)}, f32[2,1,64]{2,1,0:T(1,128)}, f32[2,256,64]{2,1,0:T(8,128)}) custom-call(f32[2,64,256]{2,1,0:T(8,128)} %bitcast_select_fusion.w1_ref, f32[2,1,256]{2,1,0:T(1,128)} %reshape.266.b1_ref, f32[2,256,64]{2,1,0:T(8,128)} %broadcast_select_fusion.w2_ref, ...), custom_call_target="tpu_custom_call" | custom-call | flops 1107296256 | bytes 1048576 | tf_op jit(solution)/shard_map/pallas_call | solution.py:191
  353.0 1.0 convert_element_type.20
  354.2 6.5 %all_to_all.5 = bf16[4,2,4096]{2,1,0:T(2,128)(2,1)S(1)} all-to-all(bf16[4,2,4096]{2,1,0:T(2,128)(2,1)S(1)} %reshape.279), channel_id=1, replica_groups=mesh['seq'=8,'xlo'=2,'z'=8,'core'=2] {'xlo','core'}, dimensions={0} | all-to-all | bytes 131072 | tf_op jit(solution)/shard_map/output_mix/all_to_all | solution.py:344
  361.3 1.3 convert_element_type.23.part_ref
  362.5 22.6 %output_mix.1 = bf16[8,48,1024]{2,1,0:T(8,128)(2,1)} custom-call(bf16[8,48,1024]{2,1,0:T(8,128)(2,1)} %convert_element_type.23.part_ref), custom_call_target="tpu_custom_call" | custom-call | bytes 1572864 | tf_op jit(solution)/shard_map/output_mix/pallas_call | solution.py:258
  385.2 1.3 reduce_sum.12
  386.4 0.7 convert_element_type.24
  (73 shorter events, 21.7 us)
Async XLA Ops:
  6.5 71.4 %all-gather.3.cloned.1.call-start = ((), (), s32[]{:S(2)}) async-start(), calls=%async_computation.1 | async-start | bytes 3244032 | tf_op jit(solution)/shard_map/all_gather | solution.py:296
  7.3 134.1 %all-gather.5.cloned.1.call-start = ((), (), s32[]{:S(2)}) async-start(), calls=%async_computation.2 | async-start | bytes 1966080 | tf_op jit(solution)/shard_map/all_gather | solution.py:298
  81.4 3.5 copy-start
  81.5 4.0 %copy-start.1 = (f32[1,256]{1,0:T(1,128)S(1)}, f32[1,256]{1,0:T(1,128)}, u32[]{:S(2)}) copy-start(f32[1,256]{1,0:T(1,128)} %param.17) | copy-start | bytes 3076
  81.6 4.5 %copy-start.2 = (f32[1,64]{1,0:T(1,128)S(1)}, f32[1,64]{1,0:T(1,128)}, u32[]{:S(2)}) copy-start(f32[1,64]{1,0:T(1,128)} %param.19) | copy-start | bytes 772
  107.0 14.0 %collective-permute-start = (f32[2,33088]{1,0:T(2,128)S(1)}, f32[2,33088]{1,0:T(2,128)S(1)}, u32[]{:S(2)}, u32[]{:S(2)}) collective-permute-start(f32[2,33088]{1,0:T(2,128)S(1)} %pad_maximum_fusion), channel_id=1, source_target_pairs={{0,32},{32,64},{64,96},{96,128},{128,160},{160,192},{192,224},{1,3... | collective-permute-start | bytes 794120 | tf_op jit(solution)/shard_map/state_hop/ppermute | solution.py:23
  144.2 13.2 %collective-permute-start.1 = (f32[2,33088]{1,0:T(2,128)S(1)}, f32[2,33088]{1,0:T(2,128)S(1)}, u32[]{:S(2)}, u32[]{:S(2)}) collective-permute-start(f32[2,33088]{1,0:T(2,128)S(1)} %pad_maximum_fusion.1), channel_id=1, source_target_pairs={{0,32},{32,64},{64,96},{96,128},{128,160},{160,192},{192,224},{1,3... | collective-permute-start | bytes 794120 | tf_op jit(solution)/shard_map/state_hop/ppermute | solution.py:23
  180.6 12.3 %collective-permute-start.2 = (f32[2,33088]{1,0:T(2,128)S(1)}, f32[2,33088]{1,0:T(2,128)S(1)}, u32[]{:S(2)}, u32[]{:S(2)}) collective-permute-start(f32[2,33088]{1,0:T(2,128)S(1)} %pad_maximum_fusion.2), channel_id=1, source_target_pairs={{0,32},{32,64},{64,96},{96,128},{128,160},{160,192},{192,224},{1,3... | collective-permute-start | bytes 794120 | tf_op jit(solution)/shard_map/state_hop/ppermute | solution.py:23
  216.1 11.9 %collective-permute-start.3 = (f32[2,33088]{1,0:T(2,128)S(1)}, f32[2,33088]{1,0:T(2,128)S(1)}, u32[]{:S(2)}, u32[]{:S(2)}) collective-permute-start(f32[2,33088]{1,0:T(2,128)S(1)} %pad_maximum_fusion.3), channel_id=1, source_target_pairs={{0,32},{32,64},{64,96},{96,128},{128,160},{160,192},{192,224},{1,3... | collective-permute-start | bytes 794120 | tf_op jit(solution)/shard_map/state_hop/ppermute | solution.py:23
  251.2 11.9 %collective-permute-start.4 = (f32[2,33088]{1,0:T(2,128)S(1)}, f32[2,33088]{1,0:T(2,128)S(1)}, u32[]{:S(2)}, u32[]{:S(2)}) collective-permute-start(f32[2,33088]{1,0:T(2,128)S(1)} %pad_maximum_fusion.4), channel_id=1, source_target_pairs={{0,32},{32,64},{64,96},{96,128},{128,160},{160,192},{192,224},{1,3... | collective-permute-start | bytes 794120 | tf_op jit(solution)/shard_map/state_hop/ppermute | solution.py:23
  286.3 11.9 %collective-permute-start.5 = (f32[2,33088]{1,0:T(2,128)S(1)}, f32[2,33088]{1,0:T(2,128)S(1)}, u32[]{:S(2)}, u32[]{:S(2)}) collective-permute-start(f32[2,33088]{1,0:T(2,128)S(1)} %pad_maximum_fusion.5), channel_id=1, source_target_pairs={{0,32},{32,64},{64,96},{96,128},{128,160},{160,192},{192,224},{1,3... | collective-permute-start | bytes 794120 | tf_op jit(solution)/shard_map/state_hop/ppermute | solution.py:23
  321.4 11.9 %collective-permute-start.6 = (f32[2,33088]{1,0:T(2,128)S(1)}, f32[2,33088]{1,0:T(2,128)S(1)}, u32[]{:S(2)}, u32[]{:S(2)}) collective-permute-start(f32[2,33088]{1,0:T(2,128)S(1)} %pad_maximum_fusion.6), channel_id=1, source_target_pairs={{0,32},{32,64},{64,96},{96,128},{128,160},{160,192},{192,224},{1,3... | collective-permute-start | bytes 794120 | tf_op jit(solution)/shard_map/state_hop/ppermute | solution.py:23
  336.0 24.8 %copy-start.3 = (bf16[256,3072]{1,0:T(8,128)(2,1)S(1)}, bf16[256,3072]{1,0:T(8,128)(2,1)}, u32[]{:S(2)}) copy-start(bf16[256,3072]{1,0:T(8,128)(2,1)} %all-gather.5.cloned.1.call-done) | copy-start | bytes 4718596
Sparse Core Ops, SparseCore 0:
  9.2 68.7 all-gather.2
  110.6 26.7 all-gather.4

commit v6 on v4

--- a/solution.py
+++ b/solution.py
@@ -181,7 +181,9 @@
     proj_width = w_qkv.shape[0]
     head_size = proj_width // 3
     stacked = jnp.concatenate([w_qkv, w_rate], axis=0)
-    gathered = lax.all_gather(tokens, row_axes, axis=1, tiled=True)
+    gathered = lax.all_gather(tokens, "z", axis=1, tiled=True)
+    gathered = lax.all_gather(gathered, "xlo", axis=1, tiled=True)
+    gathered = lax.all_gather(gathered, "core", axis=1, tiled=True)
     gathered, w_out = lax.optimization_barrier((gathered, w_out))
     w_out_pair = lax.all_gather(w_out, pair_axes, axis=0, tiled=True)
     combined = jnp.einsum(
@@ -190,6 +192,8 @@
         stacked,
         preferred_element_type=jnp.float32,
     )
+    combined = combined.reshape(videos, 2, 2, z_count, tok_part, -1)
+    combined = combined.transpose(0, 2, 3, 1, 4, 5).reshape(videos, seg_len, -1)
     projected = lax.optimization_barrier(combined[:, :, :proj_width].astype(jnp.bfloat16)).astype(
         jnp.float32
     )

time: 322 us -> 336 us (1.043)
  blocking collectives: 6.49 us -> 38.6 us
  waiting for transfers between devices: 148 us -> 130 us
    all_gather x0 -> x1, blocking collectives: none -> 32.1 us  [on_device(): gathered = lax.all_gather(tokens, 'z', axis=1, tiled=True)]
    all_gather x1 -> x2, waiting for transfers between devices: 70 us -> 51.2 us  [the longest x1 31.3 us: on_device(): gathered = lax.all_gather(gathered, 'xlo', axis=1, tiled=True)]
  transfers between devices with their start and end apart: 9 -> 10, of which waited for: 9 -> 10; matrix products, arithmetic and copies ran while one was open for 4% -> 3% of each run, Pallas kernels for 0% -> 0%
where the time goes in v6:
time: 336 us
  waiting for transfers between devices  130 us (39%)
  matrix products  77 us (23%)
  blocking collectives  38.6 us (11%)
  Pallas kernels  24.1 us (7%)
  other arithmetic  23.1 us (7%)
  starting transfers between devices  16.7 us (5%)
  between operations  14.6 us (4%)
  local copies, waits for them, and re-layouts  9.24 us (3%)
    dot_general x256, matrix products, matmul(): jnp.dot(left, right, precision=lax.Precision.HIGHEST, preferred_element_t...  73.7 us
    ppermute x7, waiting for transfers between devices, passed_along(): return lax.ppermute(array, axis, pairs)  72.3 us
    all_gather x1, blocking collectives, on_device(): gathered = lax.all_gather(tokens, 'z', axis=1, tiled=True)  32.1 us
    all_gather x1, waiting for transfers between devices, on_device(): gathered = lax.all_gather(gathered, 'xlo', axis=1, tiled=True)  31.3 us
    pallas_call x1, Pallas kernels, exchange_over_z(): pl.pallas_call(partial(exchange_kernel, peer_count), out_shape=jax.ShapeD...  24.1 us
    all_gather x1, waiting for transfers between devices, on_device(): gathered = lax.all_gather(gathered, 'core', axis=1, tiled=True)  19.9 us
    ppermute x7, starting transfers between devices, passed_along(): return lax.ppermute(array, axis, pairs)  16.6 us
    reduce_sum x32, other arithmetic, mini_step(): jnp.sum(grad_out, axis=-1, keepdims=True)  6.92 us
  transfers between devices with their start and end apart: 10, of which 10 were waited for; matrix products, arithmetic and copies ran while one was open for 3% of the time, Pallas kernels for 0%

profile of v6, /device:TPU:4, one launch (start us, length us, event | category | flops | bytes accessed | tf_op | source)
XLA Modules:
  0.0 336.1 jit_solution(13843516819152224071)
XLA Ops:
  6.5 32.1 %all_gather.12 = bf16[2,64,3072]{2,1,0:T(8,128)(2,1)} all-gather(bf16[2,8,3072]{2,1,0:T(8,128)(2,1)} %param.27), channel_id=1, replica_groups=mesh['seq'=8,'xlo'=2,'z'=8,'core'=2] {'z'}, dimensions={1}, use_global_device_ids=true | all-gather | bytes 884736 | tf_op jit(solution)/shard_map/all_gather | solution.py:184
  38.7 31.3 %all-gather.4.cloned.1.call-done = bf16[2,128,3072]{2,1,0:T(8,128)(2,1)} async-done(((bf16[2,64,3072]{2,1,0:T(8,128)(2,1)}), bf16[2,128,3072]{2,1,0:T(8,128)(2,1)}) %all-gather.4.cloned.1.call-update) | async-done | bytes 1572880 | tf_op jit(solution)/shard_map/all_gather | solution.py:185
  70.8 19.9 %all-gather.6.cloned.1.call-done = bf16[2,256,3072]{2,1,0:T(8,128)(2,1)} async-done(((bf16[2,128,3072]{2,1,0:T(8,128)(2,1)}), bf16[2,256,3072]{2,1,0:T(8,128)(2,1)}) %all-gather.6.cloned.1.call-update) | async-done | bytes 3145744 | tf_op jit(solution)/shard_map/all_gather | solution.py:186
  90.6 2.9 fusion.196
  94.9 10.8 %while.130 = (s32[]{:T(128)}, f32[2,64,256]{2,1,0:T(8,128)S(1)}, f32[2,256]{1,0:T(2,128)S(1)}, f32[2,256,64]{1,2,0:T(8,128)S(1)}, f32[2,64]{1,0:T(2,128)S(1)}, /...) while((s32[]{:T(128)}, f32[2,64,256]{2,1,0:T(8,128)S(1)}, ...), condition=%wide.region_5.6_spmd, body=%wide.region_0.5_spmd.sunk | while | flops 127755136 | bytes 2386049 | solution.py:97
  97.9 0.4 fusion.522
  99.5 0.4 convolution_subtract_fusion.38
  100.6 0.4 fusion.522
  102.2 0.4 convolution_subtract_fusion.38
  106.2 3.4 %collective-permute-start = (f32[2,33088]{1,0:T(2,128)S(1)}, f32[2,33088]{1,0:T(2,128)S(1)}, u32[]{:S(2)}, u32[]{:S(2)}) collective-permute-start(f32[2,33088]{1,0:T(2,128)S(1)} %pad_maximum_fusion), channel_id=1, source_target_pairs={{0,32},{32,64},{64,96},{96,128},{128,160},{160,192},{192,224},{1,3... | collective-permute-start | bytes 794120 | tf_op jit(solution)/shard_map/state_hop/ppermute | solution.py:23
  109.7 10.6 %collective-permute-done = f32[2,33088]{1,0:T(2,128)S(1)} collective-permute-done((f32[2,33088]{1,0:T(2,128)S(1)}, f32[2,33088]{1,0:T(2,128)S(1)}, u32[]{:S(2)}, u32[]{:S(2)}) %collective-permute-start) | collective-permute-done | bytes 264736 | tf_op jit(solution)/shard_map/state_hop/ppermute | solution.py:23
  120.7 10.8 %while.131 = (s32[]{:T(128)}, f32[2,64,256]{2,1,0:T(8,128)S(1)}, f32[2,256]{1,0:T(2,128)S(1)}, f32[2,256,64]{1,2,0:T(8,128)S(1)}, f32[2,64]{1,0:T(2,128)S(1)}, /...) while((s32[]{:T(128)}, f32[2,64,256]{2,1,0:T(8,128)S(1)}, ...), condition=%wide.region_11.12_spmd, body=%wide.region_6.11_spmd.sunk | while | flops 127755136 | bytes 2386049 | solution.py:97
  121.0 0.4 fusion.539
  125.3 0.4 convolution_subtract_fusion.40
  126.4 0.4 fusion.539
  130.7 0.4 convolution_subtract_fusion.40
  131.5 6.6 %all-gather.8.cloned.1.call-done = bf16[256,3072]{1,0:T(8,128)(2,1)} async-done(((bf16[64,3072]{1,0:T(8,128)(2,1)}), bf16[256,3072]{1,0:T(8,128)(2,1)}) %all-gather.8.cloned.1.call-update) | async-done | bytes 1572880 | tf_op jit(solution)/shard_map/all_gather | solution.py:188
  138.6 3.2 collective-permute-start.1
  141.8 10.8 %collective-permute-done.1 = f32[2,33088]{1,0:T(2,128)S(1)} collective-permute-done((f32[2,33088]{1,0:T(2,128)S(1)}, f32[2,33088]{1,0:T(2,128)S(1)}, u32[]{:S(2)}, u32[]{:S(2)}) %collective-permute-start.1) | collective-permute-done | bytes 264736 | tf_op jit(solution)/shard_map/state_hop/ppermute | solution.py:23
  153.0 10.8 %while.132 = (s32[]{:T(128)}, f32[2,64,256]{2,1,0:T(8,128)S(1)}, f32[2,256]{1,0:T(2,128)S(1)}, f32[2,256,64]{1,2,0:T(8,128)S(1)}, f32[2,64]{1,0:T(2,128)S(1)}, /...) while((s32[]{:T(128)}, f32[2,64,256]{2,1,0:T(8,128)S(1)}, ...), condition=%wide.region_17.18_spmd, body=%wide.region_12.17_spmd.sunk | while | flops 127755136 | bytes 2386049 | solution.py:97
  153.3 0.4 fusion.556
  156.0 0.4 fusion.556
  157.6 0.4 convolution_subtract_fusion.42
  161.4 0.4 fusion.556
  163.0 0.4 convolution_subtract_fusion.42
  164.4 2.1 collective-permute-start.2
  166.5 11.1 %collective-permute-done.2 = f32[2,33088]{1,0:T(2,128)S(1)} collective-permute-done((f32[2,33088]{1,0:T(2,128)S(1)}, f32[2,33088]{1,0:T(2,128)S(1)}, u32[]{:S(2)}, u32[]{:S(2)}) %collective-permute-start.2) | collective-permute-done | bytes 264736 | tf_op jit(solution)/shard_map/state_hop/ppermute | solution.py:23
  178.0 10.8 %while.133 = (s32[]{:T(128)}, f32[2,64,256]{2,1,0:T(8,128)S(1)}, f32[2,256]{1,0:T(2,128)S(1)}, f32[2,256,64]{1,2,0:T(8,128)S(1)}, f32[2,64]{1,0:T(2,128)S(1)}, /...) while((s32[]{:T(128)}, f32[2,64,256]{2,1,0:T(8,128)S(1)}, ...), condition=%wide.region_23.24_spmd, body=%wide.region_18.23_spmd.sunk | while | flops 127755136 | bytes 2386049 | solution.py:97
  178.2 0.4 fusion.573
  180.9 0.4 fusion.573
  182.6 0.4 convolution_subtract_fusion.44
  188.0 0.4 convolution_subtract_fusion.44
  189.3 1.9 collective-permute-start.3
  191.2 10.3 %collective-permute-done.3 = f32[2,33088]{1,0:T(2,128)S(1)} collective-permute-done((f32[2,33088]{1,0:T(2,128)S(1)}, f32[2,33088]{1,0:T(2,128)S(1)}, u32[]{:S(2)}, u32[]{:S(2)}) %collective-permute-start.3) | collective-permute-done | bytes 264736 | tf_op jit(solution)/shard_map/state_hop/ppermute | solution.py:23
  202.0 10.8 %while.134 = (s32[]{:T(128)}, f32[2,64,256]{2,1,0:T(8,128)S(1)}, f32[2,256]{1,0:T(2,128)S(1)}, f32[2,256,64]{1,2,0:T(8,128)S(1)}, f32[2,64]{1,0:T(2,128)S(1)}, /...) while((s32[]{:T(128)}, f32[2,64,256]{2,1,0:T(8,128)S(1)}, ...), condition=%wide.region_29.30_spmd, body=%wide.region_24.29_spmd.sunk | while | flops 127755136 | bytes 2386049 | solution.py:97
  202.3 0.4 fusion.590
  205.0 0.4 fusion.590
  206.6 0.4 convolution_subtract_fusion.46
  212.0 0.4 convolution_subtract_fusion.46
  213.3 1.9 collective-permute-start.4
  215.3 10.0 %collective-permute-done.4 = f32[2,33088]{1,0:T(2,128)S(1)} collective-permute-done((f32[2,33088]{1,0:T(2,128)S(1)}, f32[2,33088]{1,0:T(2,128)S(1)}, u32[]{:S(2)}, u32[]{:S(2)}) %collective-permute-start.4) | collective-permute-done | bytes 264736 | tf_op jit(solution)/shard_map/state_hop/ppermute | solution.py:23
  225.7 10.8 %while.135 = (s32[]{:T(128)}, f32[2,64,256]{2,1,0:T(8,128)S(1)}, f32[2,256]{1,0:T(2,128)S(1)}, f32[2,256,64]{1,2,0:T(8,128)S(1)}, f32[2,64]{1,0:T(2,128)S(1)}, /...) while((s32[]{:T(128)}, f32[2,64,256]{2,1,0:T(8,128)S(1)}, ...), condition=%wide.region_35.36_spmd, body=%wide.region_30.35_spmd.sunk | while | flops 127755136 | bytes 2386049 | solution.py:97
  228.6 0.4 fusion.607
  230.3 0.4 convolution_subtract_fusion.48
  235.7 0.4 convolution_subtract_fusion.48
  237.0 1.9 collective-permute-start.5
  238.9 10.0 %collective-permute-done.5 = f32[2,33088]{1,0:T(2,128)S(1)} collective-permute-done((f32[2,33088]{1,0:T(2,128)S(1)}, f32[2,33088]{1,0:T(2,128)S(1)}, u32[]{:S(2)}, u32[]{:S(2)}) %collective-permute-start.5) | collective-permute-done | bytes 264736 | tf_op jit(solution)/shard_map/state_hop/ppermute | solution.py:23
  249.3 10.8 %while.136 = (s32[]{:T(128)}, f32[2,64,256]{2,1,0:T(8,128)S(1)}, f32[2,256]{1,0:T(2,128)S(1)}, f32[2,256,64]{1,2,0:T(8,128)S(1)}, f32[2,64]{1,0:T(2,128)S(1)}, /...) while((s32[]{:T(128)}, f32[2,64,256]{2,1,0:T(8,128)S(1)}, ...), condition=%wide.region_41.42_spmd, body=%wide.region_36.41_spmd.sunk | while | flops 127755136 | bytes 2386049 | solution.py:97
  252.3 0.4 fusion.624
  253.9 0.4 convolution_subtract_fusion.50
  259.4 0.4 convolution_subtract_fusion.50
  260.7 2.1 collective-permute-start.6
  263.0 9.6 %collective-permute-done.6 = f32[2,33088]{1,0:T(2,128)S(1)} collective-permute-done((f32[2,33088]{1,0:T(2,128)S(1)}, f32[2,33088]{1,0:T(2,128)S(1)}, u32[]{:S(2)}, u32[]{:S(2)}) %collective-permute-start.6) | collective-permute-done | bytes 264736 | tf_op jit(solution)/shard_map/state_hop/ppermute | solution.py:23
  273.0 21.9 %while.137 = (s32[]{:T(128)}, f32[2,64,256]{2,1,0:T(8,128)S(1)}, f32[2,256]{1,0:T(2,128)S(1)}, f32[2,256,64]{1,2,0:T(8,128)S(1)}, f32[2,64]{1,0:T(2,128)S(1)}, /...) while((s32[]{:T(128)}, f32[2,64,256]{2,1,0:T(8,128)S(1)}, ...), condition=%wide.region_49.50_spmd, body=%wide.region_42.49_spmd.sunk | while | flops 273236992 | bytes 4953757 | solution.py:97
  277.7 0.4 convolution_subtract_fusion.52
  283.2 0.4 convolution_subtract_fusion.52
  288.7 0.4 convolution_subtract_fusion.52
  294.1 0.4 convolution_subtract_fusion.52
  295.1 6.5 %all_to_all.5 = bf16[4,2,4096]{2,1,0:T(2,128)(2,1)S(1)} all-to-all(bf16[4,2,4096]{2,1,0:T(2,128)(2,1)S(1)} %reshape.536), channel_id=1, replica_groups=mesh['seq'=8,'xlo'=2,'z'=8,'core'=2] {'xlo','core'}, dimensions={0} | all-to-all | bytes 131072 | tf_op jit(solution)/shard_map/output_mix/all_to_all | solution.py:234
  301.8 0.4 fusion.195
  302.3 1.2 convert_element_type.32.part_ref
  303.5 24.1 %output_mix.1 = bf16[8,48,1024]{2,1,0:T(8,128)(2,1)} custom-call(bf16[8,48,1024]{2,1,0:T(8,128)(2,1)} %convert_element_type.32.part_ref), custom_call_target="tpu_custom_call" | custom-call | bytes 1572864 | tf_op jit(solution)/shard_map/output_mix/pallas_call | solution.py:146
  327.6 1.3 reduce_sum.318
  328.9 0.7 convert_element_type.33
  (664 shorter events, 90.6 us)
Async XLA Ops:
  6.5 84.1 %copy-start.7 = (bf16[192,3072]{1,0:T(8,128)(2,1)S(1)}, bf16[192,3072]{1,0:T(8,128)(2,1)}, u32[]{:S(2)}) copy-start(bf16[192,3072]{1,0:T(8,128)(2,1)} %param.28) | copy-start | bytes 3538948
  6.5 84.1 %copy-start.8 = (bf16[1,3072]{1,0:T(2,128)(2,1)S(1)}, bf16[1,3072]{1,0:T(2,128)(2,1)}, u32[]{:S(2)}) copy-start(bf16[1,3072]{1,0:T(2,128)(2,1)} %param.29) | copy-start | bytes 18436
  6.5 63.5 %all-gather.4.cloned.1.call-start = ((), (), s32[]{:S(2)}) async-start(), calls=%async_computation.1 | async-start | bytes 2359296 | tf_op jit(solution)/shard_map/all_gather | solution.py:185
  38.7 51.9 %all-gather.6.cloned.1.call-start = ((), (), s32[]{:S(2)}) async-start(), calls=%async_computation.2 | async-start | bytes 4718592 | tf_op jit(solution)/shard_map/all_gather | solution.py:186
  70.1 68.0 %all-gather.8.cloned.1.call-start = ((), (), s32[]{:S(2)}) async-start(), calls=%async_computation.3 | async-start | bytes 1966080 | tf_op jit(solution)/shard_map/all_gather | solution.py:188
  93.7 1.0 copy-start
  93.7 1.1 copy-start.4
  93.7 1.1 copy-start.5
  93.8 1.1 copy-start.3
  93.8 1.1 copy-start.1
  93.8 1.1 copy-start.2
  106.2 14.1 %collective-permute-start = (f32[2,33088]{1,0:T(2,128)S(1)}, f32[2,33088]{1,0:T(2,128)S(1)}, u32[]{:S(2)}, u32[]{:S(2)}) collective-permute-start(f32[2,33088]{1,0:T(2,128)S(1)} %pad_maximum_fusion), channel_id=1, source_target_pairs={{0,32},{32,64},{64,96},{96,128},{128,160},{160,192},{192,224},{1,3... | collective-permute-start | bytes 794120 | tf_op jit(solution)/shard_map/state_hop/ppermute | solution.py:23
  138.6 14.0 %collective-permute-start.1 = (f32[2,33088]{1,0:T(2,128)S(1)}, f32[2,33088]{1,0:T(2,128)S(1)}, u32[]{:S(2)}, u32[]{:S(2)}) collective-permute-start(f32[2,33088]{1,0:T(2,128)S(1)} %pad_maximum_fusion.1), channel_id=1, source_target_pairs={{0,32},{32,64},{64,96},{96,128},{128,160},{160,192},{192,224},{1,3... | collective-permute-start | bytes 794120 | tf_op jit(solution)/shard_map/state_hop/ppermute | solution.py:23
  164.4 13.2 %collective-permute-start.2 = (f32[2,33088]{1,0:T(2,128)S(1)}, f32[2,33088]{1,0:T(2,128)S(1)}, u32[]{:S(2)}, u32[]{:S(2)}) collective-permute-start(f32[2,33088]{1,0:T(2,128)S(1)} %pad_maximum_fusion.2), channel_id=1, source_target_pairs={{0,32},{32,64},{64,96},{96,128},{128,160},{160,192},{192,224},{1,3... | collective-permute-start | bytes 794120 | tf_op jit(solution)/shard_map/state_hop/ppermute | solution.py:23
  189.3 12.2 %collective-permute-start.3 = (f32[2,33088]{1,0:T(2,128)S(1)}, f32[2,33088]{1,0:T(2,128)S(1)}, u32[]{:S(2)}, u32[]{:S(2)}) collective-permute-start(f32[2,33088]{1,0:T(2,128)S(1)} %pad_maximum_fusion.3), channel_id=1, source_target_pairs={{0,32},{32,64},{64,96},{96,128},{128,160},{160,192},{192,224},{1,3... | collective-permute-start | bytes 794120 | tf_op jit(solution)/shard_map/state_hop/ppermute | solution.py:23
  213.3 11.9 %collective-permute-start.4 = (f32[2,33088]{1,0:T(2,128)S(1)}, f32[2,33088]{1,0:T(2,128)S(1)}, u32[]{:S(2)}, u32[]{:S(2)}) collective-permute-start(f32[2,33088]{1,0:T(2,128)S(1)} %pad_maximum_fusion.4), channel_id=1, source_target_pairs={{0,32},{32,64},{64,96},{96,128},{128,160},{160,192},{192,224},{1,3... | collective-permute-start | bytes 794120 | tf_op jit(solution)/shard_map/state_hop/ppermute | solution.py:23
  237.0 11.9 %collective-permute-start.5 = (f32[2,33088]{1,0:T(2,128)S(1)}, f32[2,33088]{1,0:T(2,128)S(1)}, u32[]{:S(2)}, u32[]{:S(2)}) collective-permute-start(f32[2,33088]{1,0:T(2,128)S(1)} %pad_maximum_fusion.5), channel_id=1, source_target_pairs={{0,32},{32,64},{64,96},{96,128},{128,160},{160,192},{192,224},{1,3... | collective-permute-start | bytes 794120 | tf_op jit(solution)/shard_map/state_hop/ppermute | solution.py:23
  260.7 11.9 %collective-permute-start.6 = (f32[2,33088]{1,0:T(2,128)S(1)}, f32[2,33088]{1,0:T(2,128)S(1)}, u32[]{:S(2)}, u32[]{:S(2)}) collective-permute-start(f32[2,33088]{1,0:T(2,128)S(1)} %pad_maximum_fusion.6), channel_id=1, source_target_pairs={{0,32},{32,64},{64,96},{96,128},{128,160},{160,192},{192,224},{1,3... | collective-permute-start | bytes 794120 | tf_op jit(solution)/shard_map/state_hop/ppermute | solution.py:23
  273.0 28.7 %copy-start.6 = (bf16[256,3072]{1,0:T(8,128)(2,1)S(1)}, bf16[256,3072]{1,0:T(8,128)(2,1)}, u32[]{:S(2)}) copy-start(bf16[256,3072]{1,0:T(8,128)(2,1)} %all-gather.8.cloned.1.call-done) | copy-start | bytes 4718596
Sparse Core Ops, SparseCore 0:
  38.8 31.1 all-gather.3
  71.8 18.7 all-gather.5
  109.9 28.1 all-gather.7

commit v7 on v4

--- a/solution.py
+++ b/solution.py
@@ -219,7 +219,10 @@
             w_out_pair, finals = lax.optimization_barrier((w_out_pair, finals))
         if turn_idx + 1 < seq_count:
             with jax.named_scope("state_hop"):
-                received = unpack_state(passed_along(pack_state(finals), "seq", 1), finals)
+                origin = pack_state(start_states)
+                change = (pack_state(finals) - origin).astype(jnp.bfloat16)
+                moved = passed_along(change, "seq", 1).astype(jnp.float32) + origin
+                received = unpack_state(moved, finals)
             incoming = jax.tree.map(partial(jnp.where, first_device), start_states, received)
     heads_rows = results.astype(jnp.bfloat16)
     with jax.named_scope("output_mix"):

time: 322 us -> 312 us (0.969)
  waiting for transfers between devices: 148 us -> 134 us
    ppermute x7, waiting for transfers between devices: 72.5 us -> 57.7 us  [passed_along(): return lax.ppermute(array, axis, pairs)]
where the time goes in v7:
time: 312 us
  waiting for transfers between devices  134 us (43%)
  matrix products  77.1 us (25%)
  other arithmetic  25.2 us (8%)
  Pallas kernels  24 us (8%)
  starting transfers between devices  16.7 us (5%)
  between operations  14.9 us (5%)
  local copies, waits for them, and re-layouts  10.4 us (3%)
  blocking collectives  6.49 us (2%)
    dot_general x256, matrix products, matmul(): jnp.dot(left, right, precision=lax.Precision.HIGHEST, preferred_element_t...  73.3 us
    all_gather x1, waiting for transfers between devices, on_device(): gathered = lax.all_gather(tokens, row_axes, axis=1, tiled=True)  68.1 us
    ppermute x7, waiting for transfers between devices, passed_along(): return lax.ppermute(array, axis, pairs)  57.7 us
    pallas_call x1, Pallas kernels, exchange_over_z(): pl.pallas_call(partial(exchange_kernel, peer_count), out_shape=jax.ShapeD...  24 us
    ppermute x7, starting transfers between devices, passed_along(): return lax.ppermute(array, axis, pairs)  16.6 us
    all_gather x1, waiting for transfers between devices, on_device(): w_out_pair = lax.all_gather(w_out, pair_axes, axis=0, tiled=True)  7.94 us
    reduce_sum x32, other arithmetic, mini_step(): jnp.sum(grad_out, axis=-1, keepdims=True)  6.92 us
    all_to_all x1, blocking collectives, on_device(): by_head = lax.all_to_all(by_owner, pair_axes, 0, 0, tiled=True)  6.49 us
  transfers between devices with their start and end apart: 9, of which 9 were waited for; matrix products, arithmetic and copies ran while one was open for 4% of the time, Pallas kernels for 0%

profile of v7, /device:TPU:4, one launch (start us, length us, event | category | flops | bytes accessed | tf_op | source)
XLA Modules:
  0.0 311.8 jit_solution(15397213608246318698)
XLA Ops:
  6.5 0.7 all-gather.3.cloned.1.call-update
  7.9 0.9 copy.201
  9.0 0.9 copy.279
  9.9 68.1 %all-gather.3.cloned.1.call-done = bf16[2,256,3072]{2,1,0:T(8,128)(2,1)} async-done(((bf16[2,8,3072]{2,1,0:T(8,128)(2,1)}), bf16[2,256,3072]{2,1,0:T(8,128)(2,1)}) %all-gather.3.cloned.1.call-update) | async-done | bytes 3145744 | tf_op jit(solution)/shard_map/all_gather | solution.py:184
  78.0 3.4 %fusion.202 = f32[2,256,193]{1,2,0:T(8,128)S(1)} fusion(bf16[2,256,3072]{2,1,0:T(8,128)(2,1)} %all-gather.3.cloned.1.call-done, bf16[1,3072]{1,0:T(2,128)(2,1)} %param.29, bf16[192,3072]{1,0:T(8,128)(2,1)} %param.28), kind=kOutput, calls=%fused_computation.369 | convolution fusion | flops 609497088 | bytes 4726784 | tf_op jit(solution)/shard_map/vkd,cd->vkc/dot_general | solution.py:187
  82.3 10.8 %while.130 = (s32[]{:T(128)}, f32[2,64,256]{2,1,0:T(8,128)S(1)}, f32[2,256]{1,0:T(2,128)S(1)}, f32[2,256,64]{1,2,0:T(8,128)S(1)}, f32[2,64]{1,0:T(2,128)S(1)}, /...) while((s32[]{:T(128)}, f32[2,64,256]{2,1,0:T(8,128)S(1)}, ...), condition=%wide.region_5.6_spmd, body=%wide.region_0.5_spmd.sunk | while | flops 127755136 | bytes 2386049 | solution.py:97
  84.2 0.4 convolution_subtract_fusion.38
  85.3 0.4 fusion.538
  88.0 0.4 fusion.538
  89.6 0.4 convolution_subtract_fusion.38
  90.7 0.4 fusion.538
  92.3 0.4 convolution_subtract_fusion.38
  93.8 3.4 %collective-permute-start = (bf16[2,33088]{1,0:T(2,128)(2,1)S(1)}, bf16[2,33088]{1,0:T(2,128)(2,1)S(1)}, u32[]{:S(2)}, u32[]{:S(2)}) collective-permute-start(bf16[2,33088]{1,0:T(2,128)(2,1)S(1)} %fusion.205), channel_id=1, source_target_pairs={{0,32},{32,64},{64,96},{96,128},{128,160},{160,192},{192,224},{1,3... | collective-permute-start | bytes 397064 | tf_op jit(solution)/shard_map/state_hop/ppermute | solution.py:23
  97.3 7.7 %collective-permute-done = bf16[2,33088]{1,0:T(2,128)(2,1)S(1)} collective-permute-done((bf16[2,33088]{1,0:T(2,128)(2,1)S(1)}, bf16[2,33088]{1,0:T(2,128)(2,1)S(1)}, u32[]{:S(2)}, u32[]{:S(2)}) %collective-permute-start) | collective-permute-done | bytes 132384 | tf_op jit(solution)/shard_map/state_hop/ppermute | solution.py:23
  105.6 10.8 %while.131 = (s32[]{:T(128)}, f32[2,64,256]{2,1,0:T(8,128)S(1)}, f32[2,256]{1,0:T(2,128)S(1)}, f32[2,256,64]{1,2,0:T(8,128)S(1)}, f32[2,64]{1,0:T(2,128)S(1)}, /...) while((s32[]{:T(128)}, f32[2,64,256]{2,1,0:T(8,128)S(1)}, ...), condition=%wide.region_11.12_spmd, body=%wide.region_6.11_spmd.sunk | while | flops 127755136 | bytes 2386049 | solution.py:97
  107.5 0.4 convolution_subtract_fusion.40
  108.6 0.4 fusion.555
  112.9 0.4 convolution_subtract_fusion.40
  116.4 7.9 %all-gather.5.cloned.1.call-done = bf16[256,3072]{1,0:T(8,128)(2,1)} async-done(((bf16[64,3072]{1,0:T(8,128)(2,1)}), bf16[256,3072]{1,0:T(8,128)(2,1)}) %all-gather.5.cloned.1.call-update) | async-done | bytes 1572880 | tf_op jit(solution)/shard_map/all_gather | solution.py:186
  125.0 3.2 %collective-permute-start.1 = (bf16[2,33088]{1,0:T(2,128)(2,1)S(1)}, bf16[2,33088]{1,0:T(2,128)(2,1)S(1)}, u32[]{:S(2)}, u32[]{:S(2)}) collective-permute-start(bf16[2,33088]{1,0:T(2,128)(2,1)S(1)} %fusion.206), channel_id=1, source_target_pairs={{0,32},{32,64},{64,96},{96,128},{128,160},{160,192},{192,224},{1,3... | collective-permute-start | bytes 397064 | tf_op jit(solution)/shard_map/state_hop/ppermute | solution.py:23
  128.2 8.0 %collective-permute-done.1 = bf16[2,33088]{1,0:T(2,128)(2,1)S(1)} collective-permute-done((bf16[2,33088]{1,0:T(2,128)(2,1)S(1)}, bf16[2,33088]{1,0:T(2,128)(2,1)S(1)}, u32[]{:S(2)}, u32[]{:S(2)}) %collective-permute-start.1) | collective-permute-done | bytes 132384 | tf_op jit(solution)/shard_map/state_hop/ppermute | solution.py:23
  136.8 10.8 %while.132 = (s32[]{:T(128)}, f32[2,64,256]{2,1,0:T(8,128)S(1)}, f32[2,256]{1,0:T(2,128)S(1)}, f32[2,256,64]{1,2,0:T(8,128)S(1)}, f32[2,64]{1,0:T(2,128)S(1)}, /...) while((s32[]{:T(128)}, f32[2,64,256]{2,1,0:T(8,128)S(1)}, ...), condition=%wide.region_17.18_spmd, body=%wide.region_12.17_spmd.sunk | while | flops 127755136 | bytes 2386049 | solution.py:97
  137.1 0.4 fusion.572
  141.4 0.4 convolution_subtract_fusion.42
  146.9 0.4 convolution_subtract_fusion.42
  148.3 2.1 collective-permute-start.2
  150.4 8.4 %collective-permute-done.2 = bf16[2,33088]{1,0:T(2,128)(2,1)S(1)} collective-permute-done((bf16[2,33088]{1,0:T(2,128)(2,1)S(1)}, bf16[2,33088]{1,0:T(2,128)(2,1)S(1)}, u32[]{:S(2)}, u32[]{:S(2)}) %collective-permute-start.2) | collective-permute-done | bytes 132384 | tf_op jit(solution)/shard_map/state_hop/ppermute | solution.py:23
  159.4 10.8 %while.133 = (s32[]{:T(128)}, f32[2,64,256]{2,1,0:T(8,128)S(1)}, f32[2,256]{1,0:T(2,128)S(1)}, f32[2,256,64]{1,2,0:T(8,128)S(1)}, f32[2,64]{1,0:T(2,128)S(1)}, /...) while((s32[]{:T(128)}, f32[2,64,256]{2,1,0:T(8,128)S(1)}, ...), condition=%wide.region_23.24_spmd, body=%wide.region_18.23_spmd.sunk | while | flops 127755136 | bytes 2386049 | solution.py:97
  164.0 0.4 convolution_subtract_fusion.44
  169.4 0.4 convolution_subtract_fusion.44
  170.9 1.9 collective-permute-start.3
  172.8 8.6 %collective-permute-done.3 = bf16[2,33088]{1,0:T(2,128)(2,1)S(1)} collective-permute-done((bf16[2,33088]{1,0:T(2,128)(2,1)S(1)}, bf16[2,33088]{1,0:T(2,128)(2,1)S(1)}, u32[]{:S(2)}, u32[]{:S(2)}) %collective-permute-start.3) | collective-permute-done | bytes 132384 | tf_op jit(solution)/shard_map/state_hop/ppermute | solution.py:23
  182.0 10.8 %while.134 = (s32[]{:T(128)}, f32[2,64,256]{2,1,0:T(8,128)S(1)}, f32[2,256]{1,0:T(2,128)S(1)}, f32[2,256,64]{1,2,0:T(8,128)S(1)}, f32[2,64]{1,0:T(2,128)S(1)}, /...) while((s32[]{:T(128)}, f32[2,64,256]{2,1,0:T(8,128)S(1)}, ...), condition=%wide.region_29.30_spmd, body=%wide.region_24.29_spmd.sunk | while | flops 127755136 | bytes 2386049 | solution.py:97
  186.6 0.4 convolution_subtract_fusion.46
  192.0 0.4 convolution_subtract_fusion.46
  193.4 1.9 collective-permute-start.4
  195.4 8.6 %collective-permute-done.4 = bf16[2,33088]{1,0:T(2,128)(2,1)S(1)} collective-permute-done((bf16[2,33088]{1,0:T(2,128)(2,1)S(1)}, bf16[2,33088]{1,0:T(2,128)(2,1)S(1)}, u32[]{:S(2)}, u32[]{:S(2)}) %collective-permute-start.4) | collective-permute-done | bytes 132384 | tf_op jit(solution)/shard_map/state_hop/ppermute | solution.py:23
  204.5 10.8 %while.135 = (s32[]{:T(128)}, f32[2,64,256]{2,1,0:T(8,128)S(1)}, f32[2,256]{1,0:T(2,128)S(1)}, f32[2,256,64]{1,2,0:T(8,128)S(1)}, f32[2,64]{1,0:T(2,128)S(1)}, /...) while((s32[]{:T(128)}, f32[2,64,256]{2,1,0:T(8,128)S(1)}, ...), condition=%wide.region_35.36_spmd, body=%wide.region_30.35_spmd.sunk | while | flops 127755136 | bytes 2386049 | solution.py:97
  207.5 0.4 fusion.623
  209.1 0.4 convolution_subtract_fusion.48
  214.6 0.4 convolution_subtract_fusion.48
  216.0 1.9 collective-permute-start.5
  217.9 8.6 %collective-permute-done.5 = bf16[2,33088]{1,0:T(2,128)(2,1)S(1)} collective-permute-done((bf16[2,33088]{1,0:T(2,128)(2,1)S(1)}, bf16[2,33088]{1,0:T(2,128)(2,1)S(1)}, u32[]{:S(2)}, u32[]{:S(2)}) %collective-permute-start.5) | collective-permute-done | bytes 132384 | tf_op jit(solution)/shard_map/state_hop/ppermute | solution.py:23
  227.1 10.8 %while.136 = (s32[]{:T(128)}, f32[2,64,256]{2,1,0:T(8,128)S(1)}, f32[2,256]{1,0:T(2,128)S(1)}, f32[2,256,64]{1,2,0:T(8,128)S(1)}, f32[2,64]{1,0:T(2,128)S(1)}, /...) while((s32[]{:T(128)}, f32[2,64,256]{2,1,0:T(8,128)S(1)}, ...), condition=%wide.region_41.42_spmd, body=%wide.region_36.41_spmd.sunk | while | flops 127755136 | bytes 2386049 | solution.py:97
  230.1 0.4 fusion.640
  231.7 0.4 convolution_subtract_fusion.50
  237.1 0.4 convolution_subtract_fusion.50
  238.6 2.1 collective-permute-start.6
  241.0 8.0 %collective-permute-done.6 = bf16[2,33088]{1,0:T(2,128)(2,1)S(1)} collective-permute-done((bf16[2,33088]{1,0:T(2,128)(2,1)S(1)}, bf16[2,33088]{1,0:T(2,128)(2,1)S(1)}, u32[]{:S(2)}, u32[]{:S(2)}) %collective-permute-start.6) | collective-permute-done | bytes 132384 | tf_op jit(solution)/shard_map/state_hop/ppermute | solution.py:23
  249.7 20.8 %while.137 = (s32[]{:T(128)}, f32[2,64,256]{2,1,0:T(8,128)S(1)}, f32[2,256]{1,0:T(2,128)S(1)}, f32[2,256,64]{1,2,0:T(8,128)S(1)}, f32[2,64]{1,0:T(2,128)S(1)}, /...) while((s32[]{:T(128)}, f32[2,64,256]{2,1,0:T(8,128)S(1)}, ...), condition=%wide.region_49.50_spmd, body=%wide.region_42.49_spmd.sunk | while | flops 273236992 | bytes 4856473 | solution.py:97
  250.0 0.4 fusion.671
  254.1 0.4 convolution_subtract_fusion.52
  255.2 0.4 fusion.671
  259.3 0.4 convolution_subtract_fusion.52
  260.4 0.4 fusion.671
  264.5 0.4 convolution_subtract_fusion.52
  265.6 0.4 fusion.671
  269.7 0.4 convolution_subtract_fusion.52
  270.7 6.5 %all_to_all.5 = bf16[4,2,4096]{2,1,0:T(2,128)(2,1)S(1)} all-to-all(bf16[4,2,4096]{2,1,0:T(2,128)(2,1)S(1)} %reshape.549), channel_id=1, replica_groups=mesh['seq'=8,'xlo'=2,'z'=8,'core'=2] {'xlo','core'}, dimensions={0} | all-to-all | bytes 131072 | tf_op jit(solution)/shard_map/output_mix/all_to_all | solution.py:233
  277.3 0.4 fusion.201
  277.8 1.2 convert_element_type.88.part_ref
  279.1 24.0 %output_mix.1 = bf16[8,48,1024]{2,1,0:T(8,128)(2,1)} custom-call(bf16[8,48,1024]{2,1,0:T(8,128)(2,1)} %convert_element_type.88.part_ref), custom_call_target="tpu_custom_call" | custom-call | bytes 1572864 | tf_op jit(solution)/shard_map/output_mix/pallas_call | solution.py:146
  303.0 1.3 reduce_sum.318
  304.3 0.7 convert_element_type.89
  (661 shorter events, 91.9 us)
Async XLA Ops:
  6.5 71.4 %all-gather.3.cloned.1.call-start = ((), (), s32[]{:S(2)}) async-start(), calls=%async_computation.1 | async-start | bytes 3244032 | tf_op jit(solution)/shard_map/all_gather | solution.py:184
  7.3 117.1 %all-gather.5.cloned.1.call-start = ((), (), s32[]{:S(2)}) async-start(), calls=%async_computation.2 | async-start | bytes 1966080 | tf_op jit(solution)/shard_map/all_gather | solution.py:186
  81.4 0.9 copy-start.4
  81.4 0.9 copy-start.5
  81.4 0.9 copy-start
  81.4 0.9 copy-start.3
  81.4 0.9 copy-start.1
  81.4 0.9 copy-start.2
  93.8 11.2 %collective-permute-start = (bf16[2,33088]{1,0:T(2,128)(2,1)S(1)}, bf16[2,33088]{1,0:T(2,128)(2,1)S(1)}, u32[]{:S(2)}, u32[]{:S(2)}) collective-permute-start(bf16[2,33088]{1,0:T(2,128)(2,1)S(1)} %fusion.205), channel_id=1, source_target_pairs={{0,32},{32,64},{64,96},{96,128},{128,160},{160,192},{192,224},{1,3... | collective-permute-start | bytes 397064 | tf_op jit(solution)/shard_map/state_hop/ppermute | solution.py:23
  125.0 11.2 %collective-permute-start.1 = (bf16[2,33088]{1,0:T(2,128)(2,1)S(1)}, bf16[2,33088]{1,0:T(2,128)(2,1)S(1)}, u32[]{:S(2)}, u32[]{:S(2)}) collective-permute-start(bf16[2,33088]{1,0:T(2,128)(2,1)S(1)} %fusion.206), channel_id=1, source_target_pairs={{0,32},{32,64},{64,96},{96,128},{128,160},{160,192},{192,224},{1,3... | collective-permute-start | bytes 397064 | tf_op jit(solution)/shard_map/state_hop/ppermute | solution.py:23
  148.3 10.5 %collective-permute-start.2 = (bf16[2,33088]{1,0:T(2,128)(2,1)S(1)}, bf16[2,33088]{1,0:T(2,128)(2,1)S(1)}, u32[]{:S(2)}, u32[]{:S(2)}) collective-permute-start(bf16[2,33088]{1,0:T(2,128)(2,1)S(1)} %fusion.207), channel_id=1, source_target_pairs={{0,32},{32,64},{64,96},{96,128},{128,160},{160,192},{192,224},{1,3... | collective-permute-start | bytes 397064 | tf_op jit(solution)/shard_map/state_hop/ppermute | solution.py:23
  170.9 10.5 %collective-permute-start.3 = (bf16[2,33088]{1,0:T(2,128)(2,1)S(1)}, bf16[2,33088]{1,0:T(2,128)(2,1)S(1)}, u32[]{:S(2)}, u32[]{:S(2)}) collective-permute-start(bf16[2,33088]{1,0:T(2,128)(2,1)S(1)} %fusion.208), channel_id=1, source_target_pairs={{0,32},{32,64},{64,96},{96,128},{128,160},{160,192},{192,224},{1,3... | collective-permute-start | bytes 397064 | tf_op jit(solution)/shard_map/state_hop/ppermute | solution.py:23
  193.4 10.5 %collective-permute-start.4 = (bf16[2,33088]{1,0:T(2,128)(2,1)S(1)}, bf16[2,33088]{1,0:T(2,128)(2,1)S(1)}, u32[]{:S(2)}, u32[]{:S(2)}) collective-permute-start(bf16[2,33088]{1,0:T(2,128)(2,1)S(1)} %fusion.209), channel_id=1, source_target_pairs={{0,32},{32,64},{64,96},{96,128},{128,160},{160,192},{192,224},{1,3... | collective-permute-start | bytes 397064 | tf_op jit(solution)/shard_map/state_hop/ppermute | solution.py:23
  216.0 10.5 %collective-permute-start.5 = (bf16[2,33088]{1,0:T(2,128)(2,1)S(1)}, bf16[2,33088]{1,0:T(2,128)(2,1)S(1)}, u32[]{:S(2)}, u32[]{:S(2)}) collective-permute-start(bf16[2,33088]{1,0:T(2,128)(2,1)S(1)} %fusion.210), channel_id=1, source_target_pairs={{0,32},{32,64},{64,96},{96,128},{128,160},{160,192},{192,224},{1,3... | collective-permute-start | bytes 397064 | tf_op jit(solution)/shard_map/state_hop/ppermute | solution.py:23
  238.6 10.5 %collective-permute-start.6 = (bf16[2,33088]{1,0:T(2,128)(2,1)S(1)}, bf16[2,33088]{1,0:T(2,128)(2,1)S(1)}, u32[]{:S(2)}, u32[]{:S(2)}) collective-permute-start(bf16[2,33088]{1,0:T(2,128)(2,1)S(1)} %fusion.211), channel_id=1, source_target_pairs={{0,32},{32,64},{64,96},{96,128},{128,160},{160,192},{192,224},{1,3... | collective-permute-start | bytes 397064 | tf_op jit(solution)/shard_map/state_hop/ppermute | solution.py:23
  249.7 27.6 %copy-start.6 = (bf16[256,3072]{1,0:T(8,128)(2,1)S(1)}, bf16[256,3072]{1,0:T(8,128)(2,1)}, u32[]{:S(2)}) copy-start(bf16[256,3072]{1,0:T(8,128)(2,1)} %all-gather.5.cloned.1.call-done) | copy-start | bytes 4718596
Sparse Core Ops, SparseCore 0:
  9.2 68.7 all-gather.2
  97.5 26.8 all-gather.4

commit v8 on v7

--- a/solution.py
+++ b/solution.py
@@ -98,6 +98,39 @@
     return (inner_state, results.reshape(queries.shape[0], -1))
 
 
+def hop_kernel(src_ref, dst_ref, send_sem, recv_sem):
+    place = lax.axis_index("seq")
+    count = lax.axis_size("seq")
+    right = lax.rem(place + 1, count)
+    left = lax.rem(place + count - 1, count)
+    barrier = pltpu.get_barrier_semaphore()
+    pl.semaphore_signal(barrier, inc=1, device_id={"seq": left}, device_id_type=MESH_ID)
+    pl.semaphore_wait(barrier, 1)
+    copy = pltpu.make_async_remote_copy(
+        src_ref=src_ref,
+        dst_ref=dst_ref,
+        send_sem=send_sem,
+        recv_sem=recv_sem,
+        device_id={"seq": right},
+        device_id_type=MESH_ID,
+    )
+    copy.start()
+    copy.wait()
+
+
+def hop_to_next(change):
+    moved = change.size * change.dtype.itemsize
+    return pl.pallas_call(
+        hop_kernel,
+        out_shape=jax.ShapeDtypeStruct(change.shape, change.dtype),
+        in_specs=[pl.BlockSpec(memory_space=pl.ANY)],
+        out_specs=pl.BlockSpec(memory_space=pl.ANY),
+        scratch_shapes=[pltpu.SemaphoreType.DMA(()), pltpu.SemaphoreType.DMA(())],
+        compiler_params=pltpu.CompilerParams(collective_id=1, has_side_effects=True),
+        cost_estimate=pl.CostEstimate(flops=0, bytes_accessed=2 * moved, transcendentals=0),
+    )(change)
+
+
 def pack_state(state):
     videos = state[0].shape[0]
     return jnp.concatenate([part.reshape(videos, -1) for part in state], axis=1)
@@ -221,7 +254,7 @@
             with jax.named_scope("state_hop"):
                 origin = pack_state(start_states)
                 change = (pack_state(finals) - origin).astype(jnp.bfloat16)
-                moved = passed_along(change, "seq", 1).astype(jnp.float32) + origin
+                moved = hop_to_next(change).astype(jnp.float32) + origin
                 received = unpack_state(moved, finals)
             incoming = jax.tree.map(partial(jnp.where, first_device), start_states, received)
     heads_rows = results.astype(jnp.bfloat16)

time: 312 us -> 320 us (1.026)
  Pallas kernels: 24 us -> 87.9 us
  waiting for transfers between devices: 134 us -> 81.4 us
  starting transfers between devices: 16.7 us -> 0.04 us
  other arithmetic: 25.2 us -> 36 us
    pallas_call x0 -> x7, Pallas kernels: none -> 63.9 us  [hop_to_next(): pl.pallas_call(hop_kernel, out_shape=jax.ShapeDtypeStruct(change.shape, c...]
    ppermute x7 -> x0, waiting for transfers between devices: 57.7 us -> none  [passed_along(): return lax.ppermute(array, axis, pairs)]
    ppermute x7 -> x0, starting transfers between devices: 16.6 us -> none  [passed_along(): return lax.ppermute(array, axis, pairs)]
    add x7, other arithmetic: 1.31 us -> 7.66 us  [on_device(): moved = hop_to_next(change).astype(jnp.float32) + origin]
    all_gather x1, waiting for transfers between devices: 7.94 us -> 13.5 us  [on_device(): w_out_pair = lax.all_gather(w_out, pair_axes, axis=0, tiled=True)]
    convert_element_type x7, other arithmetic: 1.68 us -> 6.21 us  [on_device(): change = (pack_state(finals) - origin).astype(jnp.bfloat16)]
  transfers between devices with their start and end apart: 9 -> 2, of which waited for: 9 -> 2; matrix products, arithmetic and copies ran while one was open for 4% -> 4% of each run, Pallas kernels for 0% -> 0%
where the time goes in v8:
time: 320 us; the launch traced here: 319 us
  Pallas kernels  87.9 us (27%)
  waiting for transfers between devices  81.4 us (25%)
  matrix products  78.4 us (25%)
  other arithmetic  36 us (11%)
  between operations  14.9 us (5%)
  local copies, waits for them, and re-layouts  11.3 us (4%)
  blocking collectives  6.49 us (2%)
    dot_general x256, matrix products, matmul(): jnp.dot(left, right, precision=lax.Precision.HIGHEST, preferred_element_t...  73.2 us
    all_gather x1, waiting for transfers between devices, on_device(): gathered = lax.all_gather(tokens, row_axes, axis=1, tiled=True)  67.1 us
    pallas_call x7, Pallas kernels, hop_to_next(): pl.pallas_call(hop_kernel, out_shape=jax.ShapeDtypeStruct(change.shape, c...  63.9 us
    pallas_call x1, Pallas kernels, exchange_over_z(): pl.pallas_call(partial(exchange_kernel, peer_count), out_shape=jax.ShapeD...  23.9 us
    all_gather x1, waiting for transfers between devices, on_device(): w_out_pair = lax.all_gather(w_out, pair_axes, axis=0, tiled=True)  13.5 us
    add x7, other arithmetic, on_device(): moved = hop_to_next(change).astype(jnp.float32) + origin  7.66 us
    reduce_sum x32, other arithmetic, mini_step(): jnp.sum(grad_out, axis=-1, keepdims=True)  6.92 us
    all_to_all x1, blocking collectives, on_device(): by_head = lax.all_to_all(by_owner, pair_axes, 0, 0, tiled=True)  6.49 us
  transfers between devices with their start and end apart: 2, of which 2 were waited for; matrix products, arithmetic and copies ran while one was open for 4% of the time, Pallas kernels for 0%

profile of v8, /device:TPU:4, one launch (start us, length us, event | category | flops | bytes accessed | tf_op | source)
XLA Modules:
  0.0 319.2 jit_solution(5406531200753179137)
XLA Ops:
  6.5 0.7 all-gather.3.cloned.1.call-update
  8.0 0.9 copy.201
  9.0 0.9 copy.279
  9.9 0.9 copy.195
  10.9 67.1 %all-gather.3.cloned.1.call-done = bf16[2,256,3072]{2,1,0:T(8,128)(2,1)} async-done(((bf16[2,8,3072]{2,1,0:T(8,128)(2,1)}), bf16[2,256,3072]{2,1,0:T(8,128)(2,1)}) %all-gather.3.cloned.1.call-update) | async-done | bytes 3145744 | tf_op jit(solution)/shard_map/all_gather | solution.py:217
  78.0 3.4 %fusion.202 = f32[2,256,193]{1,2,0:T(8,128)S(1)} fusion(bf16[2,256,3072]{2,1,0:T(8,128)(2,1)} %all-gather.3.cloned.1.call-done, bf16[1,3072]{1,0:T(2,128)(2,1)} %param.29, bf16[192,3072]{1,0:T(8,128)(2,1)} %param.28), kind=kOutput, calls=%fused_computation.369 | convolution fusion | flops 609497088 | bytes 4726784 | tf_op jit(solution)/shard_map/vkd,cd->vkc/dot_general | solution.py:220
  82.3 10.8 %while.130 = (s32[]{:T(128)}, f32[2,64,256]{2,1,0:T(8,128)S(1)}, f32[2,256]{1,0:T(2,128)S(1)}, f32[2,256,64]{1,2,0:T(8,128)S(1)}, f32[2,64]{1,0:T(2,128)S(1)}, /...) while((s32[]{:T(128)}, f32[2,64,256]{2,1,0:T(8,128)S(1)}, ...), condition=%wide.region_5.6_spmd, body=%wide.region_0.5_spmd.sunk | while | flops 127755136 | bytes 2386049 | solution.py:97
  86.9 0.4 convolution_subtract_fusion.38
  89.6 0.4 convolution_subtract_fusion.38
  92.3 0.4 convolution_subtract_fusion.38
  93.6 0.9 fusion.205.src_ref
  94.5 9.6 %state_hop.7 = bf16[2,33088]{1,0:T(2,128)(2,1)} custom-call(bf16[2,33088]{1,0:T(2,128)(2,1)} %fusion.205.src_ref), custom_call_target="tpu_custom_call" | custom-call | bytes 264704 | tf_op jit(solution)/shard_map/state_hop/pallas_call | solution.py:123
  104.1 1.1 convert_add_fusion.6
  105.6 10.8 %while.131 = (s32[]{:T(128)}, f32[2,64,256]{2,1,0:T(8,128)S(1)}, f32[2,256]{1,0:T(2,128)S(1)}, f32[2,256,64]{1,2,0:T(8,128)S(1)}, f32[2,64]{1,0:T(2,128)S(1)}, /...) while((s32[]{:T(128)}, f32[2,64,256]{2,1,0:T(8,128)S(1)}, ...), condition=%wide.region_11.12_spmd, body=%wide.region_6.11_spmd.sunk | while | flops 127755136 | bytes 2386049 | solution.py:97
  107.5 0.4 convolution_subtract_fusion.40
  110.2 0.4 convolution_subtract_fusion.40
  112.9 0.4 convolution_subtract_fusion.40
  115.6 0.4 convolution_subtract_fusion.40
  116.7 13.5 %all-gather.5.cloned.1.call-done = bf16[256,3072]{1,0:T(8,128)(2,1)} async-done(((bf16[64,3072]{1,0:T(8,128)(2,1)}), bf16[256,3072]{1,0:T(8,128)(2,1)}) %all-gather.5.cloned.1.call-update) | async-done | bytes 1572880 | tf_op jit(solution)/shard_map/all_gather | solution.py:219
  130.6 0.9 fusion.206.src_ref
  131.5 9.7 %state_hop.8 = bf16[2,33088]{1,0:T(2,128)(2,1)} custom-call(bf16[2,33088]{1,0:T(2,128)(2,1)} %fusion.206.src_ref), custom_call_target="tpu_custom_call" | custom-call | bytes 264704 | tf_op jit(solution)/shard_map/state_hop/pallas_call | solution.py:123
  141.2 1.1 convert_add_fusion.5
  142.8 10.8 %while.132 = (s32[]{:T(128)}, f32[2,64,256]{2,1,0:T(8,128)S(1)}, f32[2,256]{1,0:T(2,128)S(1)}, f32[2,256,64]{1,2,0:T(8,128)S(1)}, f32[2,64]{1,0:T(2,128)S(1)}, /...) while((s32[]{:T(128)}, f32[2,64,256]{2,1,0:T(8,128)S(1)}, ...), condition=%wide.region_17.18_spmd, body=%wide.region_12.17_spmd.sunk | while | flops 127755136 | bytes 2386049 | solution.py:97
  150.1 0.4 convolution_subtract_fusion.42
  152.8 0.4 convolution_subtract_fusion.42
  154.0 0.9 fusion.207.src_ref
  154.9 8.9 %state_hop.9 = bf16[2,33088]{1,0:T(2,128)(2,1)} custom-call(bf16[2,33088]{1,0:T(2,128)(2,1)} %fusion.207.src_ref), custom_call_target="tpu_custom_call" | custom-call | bytes 264704 | tf_op jit(solution)/shard_map/state_hop/pallas_call | solution.py:123
  163.8 1.1 convert_add_fusion.4
  165.3 10.8 %while.133 = (s32[]{:T(128)}, f32[2,64,256]{2,1,0:T(8,128)S(1)}, f32[2,256]{1,0:T(2,128)S(1)}, f32[2,256,64]{1,2,0:T(8,128)S(1)}, f32[2,64]{1,0:T(2,128)S(1)}, /...) while((s32[]{:T(128)}, f32[2,64,256]{2,1,0:T(8,128)S(1)}, ...), condition=%wide.region_23.24_spmd, body=%wide.region_18.23_spmd.sunk | while | flops 127755136 | bytes 2386049 | solution.py:97
  172.6 0.4 convolution_subtract_fusion.44
  175.3 0.4 convolution_subtract_fusion.44
  176.5 0.9 fusion.208.src_ref
  177.4 8.9 %state_hop.10 = bf16[2,33088]{1,0:T(2,128)(2,1)} custom-call(bf16[2,33088]{1,0:T(2,128)(2,1)} %fusion.208.src_ref), custom_call_target="tpu_custom_call" | custom-call | bytes 264704 | tf_op jit(solution)/shard_map/state_hop/pallas_call | solution.py:123
  186.3 1.1 convert_add_fusion.3
  187.9 11.0 %while.134 = (s32[]{:T(128)}, f32[2,64,256]{2,1,0:T(8,128)S(1)}, f32[2,256]{1,0:T(2,128)S(1)}, f32[2,256,64]{1,2,0:T(8,128)S(1)}, f32[2,64]{1,0:T(2,128)S(1)}, /...) while((s32[]{:T(128)}, f32[2,64,256]{2,1,0:T(8,128)S(1)}, ...), condition=%wide.region_29.30_spmd, body=%wide.region_24.29_spmd.sunk | while | flops 127755136 | bytes 2386049 | solution.py:97
  190.0 0.4 convolution_subtract_fusion.46
  192.7 0.4 convolution_subtract_fusion.46
  195.4 0.4 convolution_subtract_fusion.46
  198.1 0.4 convolution_subtract_fusion.46
  199.3 0.9 fusion.209.src_ref
  200.2 8.9 %state_hop.11 = bf16[2,33088]{1,0:T(2,128)(2,1)} custom-call(bf16[2,33088]{1,0:T(2,128)(2,1)} %fusion.209.src_ref), custom_call_target="tpu_custom_call" | custom-call | bytes 264704 | tf_op jit(solution)/shard_map/state_hop/pallas_call | solution.py:123
  209.1 1.1 convert_add_fusion.2
  210.6 10.8 %while.135 = (s32[]{:T(128)}, f32[2,64,256]{2,1,0:T(8,128)S(1)}, f32[2,256]{1,0:T(2,128)S(1)}, f32[2,256,64]{1,2,0:T(8,128)S(1)}, f32[2,64]{1,0:T(2,128)S(1)}, /...) while((s32[]{:T(128)}, f32[2,64,256]{2,1,0:T(8,128)S(1)}, ...), condition=%wide.region_35.36_spmd, body=%wide.region_30.35_spmd.sunk | while | flops 127755136 | bytes 2386049 | solution.py:97
  217.9 0.4 convolution_subtract_fusion.48
  220.6 0.4 convolution_subtract_fusion.48
  221.8 0.9 fusion.210.src_ref
  222.7 8.9 %state_hop.12 = bf16[2,33088]{1,0:T(2,128)(2,1)} custom-call(bf16[2,33088]{1,0:T(2,128)(2,1)} %fusion.210.src_ref), custom_call_target="tpu_custom_call" | custom-call | bytes 264704 | tf_op jit(solution)/shard_map/state_hop/pallas_call | solution.py:123
  231.6 1.1 convert_add_fusion.1
  233.2 10.8 %while.136 = (s32[]{:T(128)}, f32[2,64,256]{2,1,0:T(8,128)S(1)}, f32[2,256]{1,0:T(2,128)S(1)}, f32[2,256,64]{1,2,0:T(8,128)S(1)}, f32[2,64]{1,0:T(2,128)S(1)}, /...) while((s32[]{:T(128)}, f32[2,64,256]{2,1,0:T(8,128)S(1)}, ...), condition=%wide.region_41.42_spmd, body=%wide.region_36.41_spmd.sunk | while | flops 127755136 | bytes 2386049 | solution.py:97
  240.5 0.4 convolution_subtract_fusion.50
  243.2 0.4 convolution_subtract_fusion.50
  244.4 0.9 fusion.211.src_ref
  245.3 8.9 %state_hop.13 = bf16[2,33088]{1,0:T(2,128)(2,1)} custom-call(bf16[2,33088]{1,0:T(2,128)(2,1)} %fusion.211.src_ref), custom_call_target="tpu_custom_call" | custom-call | bytes 264704 | tf_op jit(solution)/shard_map/state_hop/pallas_call | solution.py:123
  254.2 1.1 convert_add_fusion
  255.7 20.8 %while.137 = (s32[]{:T(128)}, f32[2,64,256]{2,1,0:T(8,128)S(1)}, f32[2,256]{1,0:T(2,128)S(1)}, f32[2,256,64]{1,2,0:T(8,128)S(1)}, f32[2,64]{1,0:T(2,128)S(1)}, /...) while((s32[]{:T(128)}, f32[2,64,256]{2,1,0:T(8,128)S(1)}, ...), condition=%wide.region_49.50_spmd, body=%wide.region_42.49_spmd.sunk | while | flops 273236992 | bytes 4856473 | solution.py:97
  260.1 0.4 convolution_subtract_fusion.52
  265.3 0.4 convolution_subtract_fusion.52
  275.7 0.4 convolution_subtract_fusion.52
  276.7 6.5 %all_to_all.5 = bf16[4,2,4096]{2,1,0:T(2,128)(2,1)S(1)} all-to-all(bf16[4,2,4096]{2,1,0:T(2,128)(2,1)S(1)} %reshape.549), channel_id=1, replica_groups=mesh['seq'=8,'xlo'=2,'z'=8,'core'=2] {'xlo','core'}, dimensions={0} | all-to-all | bytes 131072 | tf_op jit(solution)/shard_map/output_mix/all_to_all | solution.py:266
  283.3 1.8 fusion.201
  285.2 1.2 convert_element_type.88.part_ref
  286.5 23.9 %output_mix.1 = bf16[8,48,1024]{2,1,0:T(8,128)(2,1)} custom-call(bf16[8,48,1024]{2,1,0:T(8,128)(2,1)} %convert_element_type.88.part_ref), custom_call_target="tpu_custom_call" | custom-call | bytes 1572864 | tf_op jit(solution)/shard_map/output_mix/pallas_call | solution.py:179
  310.4 1.3 reduce_sum.318
  311.7 0.7 convert_element_type.89
  (652 shorter events, 92.0 us)
Async XLA Ops:
  6.5 71.4 %all-gather.3.cloned.1.call-start = ((), (), s32[]{:S(2)}) async-start(), calls=%async_computation.1 | async-start | bytes 3244032 | tf_op jit(solution)/shard_map/all_gather | solution.py:217
  7.3 123.0 %all-gather.5.cloned.1.call-start = ((), (), s32[]{:S(2)}) async-start(), calls=%async_computation.2 | async-start | bytes 1966080 | tf_op jit(solution)/shard_map/all_gather | solution.py:219
  81.4 0.9 copy-start.4
  81.4 0.9 copy-start.5
  81.4 0.9 copy-start
  81.4 0.9 copy-start.3
  81.4 0.9 copy-start.1
  81.4 0.9 copy-start.2
Sparse Core Ops, SparseCore 0:
  9.2 68.7 all-gather.2
  105.7 24.4 all-gather.4

commit v9 on v7

--- a/solution.py
+++ b/solution.py
@@ -215,8 +215,6 @@
     incoming = start_states
     for turn_idx in range(seq_count):
         finals, results = jax.vmap(segment)(incoming, queries, key_rows, value_rows, lr_rows)
-        if turn_idx == 1:
-            w_out_pair, finals = lax.optimization_barrier((w_out_pair, finals))
         if turn_idx + 1 < seq_count:
             with jax.named_scope("state_hop"):
                 origin = pack_state(start_states)

time: 312 us -> 304 us (0.974)
  waiting for transfers between devices: 134 us -> 127 us
    all_gather x1, waiting for transfers between devices: 7.94 us -> 0.02 us  [on_device(): w_out_pair = lax.all_gather(w_out, pair_axes, axis=0, tiled=True)]
  transfers between devices with their start and end apart: 9 -> 9, of which waited for: 9 -> 8; matrix products, arithmetic and copies ran while one was open for 4% -> 8% of each run, Pallas kernels for 0% -> 0%
where the time goes in v9:
time: 304 us; the launch traced here: 303 us
  waiting for transfers between devices  127 us (42%)
  matrix products  78.5 us (26%)
  other arithmetic  25.2 us (8%)
  Pallas kernels  22.6 us (7%)
  starting transfers between devices  15.4 us (5%)
  between operations  14.9 us (5%)
  local copies, waits for them, and re-layouts  10.5 us (3%)
  blocking collectives  6.49 us (2%)
    dot_general x256, matrix products, matmul(): jnp.dot(left, right, precision=lax.Precision.HIGHEST, preferred_element_t...  73.3 us
    all_gather x1, waiting for transfers between devices, on_device(): gathered = lax.all_gather(tokens, row_axes, axis=1, tiled=True)  68.1 us
    ppermute x7, waiting for transfers between devices, passed_along(): return lax.ppermute(array, axis, pairs)  58.3 us
    pallas_call x1, Pallas kernels, exchange_over_z(): pl.pallas_call(partial(exchange_kernel, peer_count), out_shape=jax.ShapeD...  22.6 us
    ppermute x7, starting transfers between devices, passed_along(): return lax.ppermute(array, axis, pairs)  15.3 us
    reduce_sum x32, other arithmetic, mini_step(): jnp.sum(grad_out, axis=-1, keepdims=True)  6.92 us
    all_to_all x1, blocking collectives, on_device(): by_head = lax.all_to_all(by_owner, pair_axes, 0, 0, tiled=True)  6.49 us
  transfers between devices with their start and end apart: 9, of which 8 were waited for; matrix products, arithmetic and copies ran while one was open for 8% of the time, Pallas kernels for 0%

profile of v9, /device:TPU:4, one launch (start us, length us, event | category | flops | bytes accessed | tf_op | source)
XLA Modules:
  0.0 303.2 jit_solution(11178596231710705579)
XLA Ops:
  6.5 0.7 all-gather.3.cloned.1.call-update
  7.9 0.9 copy.201
  9.0 0.9 copy.279
  9.9 68.1 %all-gather.3.cloned.1.call-done = bf16[2,256,3072]{2,1,0:T(8,128)(2,1)} async-done(((bf16[2,8,3072]{2,1,0:T(8,128)(2,1)}), bf16[2,256,3072]{2,1,0:T(8,128)(2,1)}) %all-gather.3.cloned.1.call-update) | async-done | bytes 3145744 | tf_op jit(solution)/shard_map/all_gather | solution.py:184
  78.0 3.4 %fusion.202 = f32[2,256,193]{1,2,0:T(8,128)S(1)} fusion(bf16[2,256,3072]{2,1,0:T(8,128)(2,1)} %all-gather.3.cloned.1.call-done, bf16[1,3072]{1,0:T(2,128)(2,1)} %param.29, bf16[192,3072]{1,0:T(8,128)(2,1)} %param.28), kind=kOutput, calls=%fused_computation.369 | convolution fusion | flops 609497088 | bytes 4726784 | tf_op jit(solution)/shard_map/vkd,cd->vkc/dot_general | solution.py:187
  82.3 10.8 %while.130 = (s32[]{:T(128)}, f32[2,64,256]{2,1,0:T(8,128)S(1)}, f32[2,256]{1,0:T(2,128)S(1)}, f32[2,256,64]{1,2,0:T(8,128)S(1)}, f32[2,64]{1,0:T(2,128)S(1)}, /...) while((s32[]{:T(128)}, f32[2,64,256]{2,1,0:T(8,128)S(1)}, ...), condition=%wide.region_5.6_spmd, body=%wide.region_0.5_spmd.sunk | while | flops 127755136 | bytes 2386049 | solution.py:97
  84.2 0.4 convolution_subtract_fusion.38
  87.0 0.4 convolution_subtract_fusion.38
  89.7 0.4 convolution_subtract_fusion.38
  92.4 0.4 convolution_subtract_fusion.38
  93.8 3.4 %collective-permute-start = (bf16[2,33088]{1,0:T(2,128)(2,1)S(1)}, bf16[2,33088]{1,0:T(2,128)(2,1)S(1)}, u32[]{:S(2)}, u32[]{:S(2)}) collective-permute-start(bf16[2,33088]{1,0:T(2,128)(2,1)S(1)} %fusion.205), channel_id=1, source_target_pairs={{0,32},{32,64},{64,96},{96,128},{128,160},{160,192},{192,224},{1,3... | collective-permute-start | bytes 397064 | tf_op jit(solution)/shard_map/state_hop/ppermute | solution.py:23
  97.3 7.6 %collective-permute-done = bf16[2,33088]{1,0:T(2,128)(2,1)S(1)} collective-permute-done((bf16[2,33088]{1,0:T(2,128)(2,1)S(1)}, bf16[2,33088]{1,0:T(2,128)(2,1)S(1)}, u32[]{:S(2)}, u32[]{:S(2)}) %collective-permute-start) | collective-permute-done | bytes 132384 | tf_op jit(solution)/shard_map/state_hop/ppermute | solution.py:23
  105.6 10.8 %while.131 = (s32[]{:T(128)}, f32[2,64,256]{2,1,0:T(8,128)S(1)}, f32[2,256]{1,0:T(2,128)S(1)}, f32[2,256,64]{1,2,0:T(8,128)S(1)}, f32[2,64]{1,0:T(2,128)S(1)}, /...) while((s32[]{:T(128)}, f32[2,64,256]{2,1,0:T(8,128)S(1)}, ...), condition=%wide.region_11.12_spmd, body=%wide.region_6.11_spmd.sunk | while | flops 127755136 | bytes 2386049 | solution.py:97
  105.9 0.4 fusion.555
  108.6 0.4 fusion.555
  111.3 0.4 fusion.555
  114.0 0.4 fusion.555
  115.6 0.4 convolution_subtract_fusion.40
  117.0 1.9 collective-permute-start.1
  119.0 8.6 %collective-permute-done.1 = bf16[2,33088]{1,0:T(2,128)(2,1)S(1)} collective-permute-done((bf16[2,33088]{1,0:T(2,128)(2,1)S(1)}, bf16[2,33088]{1,0:T(2,128)(2,1)S(1)}, u32[]{:S(2)}, u32[]{:S(2)}) %collective-permute-start.1) | collective-permute-done | bytes 132384 | tf_op jit(solution)/shard_map/state_hop/ppermute | solution.py:23
  128.2 10.8 %while.132 = (s32[]{:T(128)}, f32[2,64,256]{2,1,0:T(8,128)S(1)}, f32[2,256]{1,0:T(2,128)S(1)}, f32[2,256,64]{1,2,0:T(8,128)S(1)}, f32[2,64]{1,0:T(2,128)S(1)}, /...) while((s32[]{:T(128)}, f32[2,64,256]{2,1,0:T(8,128)S(1)}, ...), condition=%wide.region_17.18_spmd, body=%wide.region_12.17_spmd.sunk | while | flops 127755136 | bytes 2386049 | solution.py:97
  131.1 0.4 fusion.572
  133.8 0.4 fusion.572
  135.5 0.4 convolution_subtract_fusion.42
  136.5 0.4 fusion.572
  138.2 0.4 convolution_subtract_fusion.42
  139.6 2.1 collective-permute-start.2
  141.7 8.4 %collective-permute-done.2 = bf16[2,33088]{1,0:T(2,128)(2,1)S(1)} collective-permute-done((bf16[2,33088]{1,0:T(2,128)(2,1)S(1)}, bf16[2,33088]{1,0:T(2,128)(2,1)S(1)}, u32[]{:S(2)}, u32[]{:S(2)}) %collective-permute-start.2) | collective-permute-done | bytes 132384 | tf_op jit(solution)/shard_map/state_hop/ppermute | solution.py:23
  150.7 10.8 %while.133 = (s32[]{:T(128)}, f32[2,64,256]{2,1,0:T(8,128)S(1)}, f32[2,256]{1,0:T(2,128)S(1)}, f32[2,256,64]{1,2,0:T(8,128)S(1)}, f32[2,64]{1,0:T(2,128)S(1)}, /...) while((s32[]{:T(128)}, f32[2,64,256]{2,1,0:T(8,128)S(1)}, ...), condition=%wide.region_23.24_spmd, body=%wide.region_18.23_spmd.sunk | while | flops 127755136 | bytes 2386049 | solution.py:97
  153.7 0.4 fusion.589
  158.0 0.4 convolution_subtract_fusion.44
  160.7 0.4 convolution_subtract_fusion.44
  162.2 1.9 collective-permute-start.3
  164.1 8.6 %collective-permute-done.3 = bf16[2,33088]{1,0:T(2,128)(2,1)S(1)} collective-permute-done((bf16[2,33088]{1,0:T(2,128)(2,1)S(1)}, bf16[2,33088]{1,0:T(2,128)(2,1)S(1)}, u32[]{:S(2)}, u32[]{:S(2)}) %collective-permute-start.3) | collective-permute-done | bytes 132384 | tf_op jit(solution)/shard_map/state_hop/ppermute | solution.py:23
  173.3 10.8 %while.134 = (s32[]{:T(128)}, f32[2,64,256]{2,1,0:T(8,128)S(1)}, f32[2,256]{1,0:T(2,128)S(1)}, f32[2,256,64]{1,2,0:T(8,128)S(1)}, f32[2,64]{1,0:T(2,128)S(1)}, /...) while((s32[]{:T(128)}, f32[2,64,256]{2,1,0:T(8,128)S(1)}, ...), condition=%wide.region_29.30_spmd, body=%wide.region_24.29_spmd.sunk | while | flops 127755136 | bytes 2386049 | solution.py:97
  176.3 0.4 fusion.606
  180.6 0.4 convolution_subtract_fusion.46
  183.3 0.4 convolution_subtract_fusion.46
  184.8 1.9 collective-permute-start.4
  186.7 8.6 %collective-permute-done.4 = bf16[2,33088]{1,0:T(2,128)(2,1)S(1)} collective-permute-done((bf16[2,33088]{1,0:T(2,128)(2,1)S(1)}, bf16[2,33088]{1,0:T(2,128)(2,1)S(1)}, u32[]{:S(2)}, u32[]{:S(2)}) %collective-permute-start.4) | collective-permute-done | bytes 132384 | tf_op jit(solution)/shard_map/state_hop/ppermute | solution.py:23
  195.9 10.8 %while.135 = (s32[]{:T(128)}, f32[2,64,256]{2,1,0:T(8,128)S(1)}, f32[2,256]{1,0:T(2,128)S(1)}, f32[2,256,64]{1,2,0:T(8,128)S(1)}, f32[2,64]{1,0:T(2,128)S(1)}, /...) while((s32[]{:T(128)}, f32[2,64,256]{2,1,0:T(8,128)S(1)}, ...), condition=%wide.region_35.36_spmd, body=%wide.region_30.35_spmd.sunk | while | flops 127755136 | bytes 2386049 | solution.py:97
  198.9 0.4 fusion.623
  203.2 0.4 convolution_subtract_fusion.48
  205.9 0.4 convolution_subtract_fusion.48
  207.4 1.9 collective-permute-start.5
  209.3 8.6 %collective-permute-done.5 = bf16[2,33088]{1,0:T(2,128)(2,1)S(1)} collective-permute-done((bf16[2,33088]{1,0:T(2,128)(2,1)S(1)}, bf16[2,33088]{1,0:T(2,128)(2,1)S(1)}, u32[]{:S(2)}, u32[]{:S(2)}) %collective-permute-start.5) | collective-permute-done | bytes 132384 | tf_op jit(solution)/shard_map/state_hop/ppermute | solution.py:23
  218.5 10.8 %while.136 = (s32[]{:T(128)}, f32[2,64,256]{2,1,0:T(8,128)S(1)}, f32[2,256]{1,0:T(2,128)S(1)}, f32[2,256,64]{1,2,0:T(8,128)S(1)}, f32[2,64]{1,0:T(2,128)S(1)}, /...) while((s32[]{:T(128)}, f32[2,64,256]{2,1,0:T(8,128)S(1)}, ...), condition=%wide.region_41.42_spmd, body=%wide.region_36.41_spmd.sunk | while | flops 127755136 | bytes 2386049 | solution.py:97
  221.4 0.4 fusion.640
  225.8 0.4 convolution_subtract_fusion.50
  228.5 0.4 convolution_subtract_fusion.50
  229.9 2.1 collective-permute-start.6
  232.4 8.0 %collective-permute-done.6 = bf16[2,33088]{1,0:T(2,128)(2,1)S(1)} collective-permute-done((bf16[2,33088]{1,0:T(2,128)(2,1)S(1)}, bf16[2,33088]{1,0:T(2,128)(2,1)S(1)}, u32[]{:S(2)}, u32[]{:S(2)}) %collective-permute-start.6) | collective-permute-done | bytes 132384 | tf_op jit(solution)/shard_map/state_hop/ppermute | solution.py:23
  241.0 20.8 %while.137 = (s32[]{:T(128)}, f32[2,64,256]{2,1,0:T(8,128)S(1)}, f32[2,256]{1,0:T(2,128)S(1)}, f32[2,256,64]{1,2,0:T(8,128)S(1)}, f32[2,64]{1,0:T(2,128)S(1)}, /...) while((s32[]{:T(128)}, f32[2,64,256]{2,1,0:T(8,128)S(1)}, ...), condition=%wide.region_49.50_spmd, body=%wide.region_42.49_spmd.sunk | while | flops 273236992 | bytes 4856473 | solution.py:97
  245.4 0.4 convolution_subtract_fusion.52
  246.5 0.4 fusion.671
  250.6 0.4 convolution_subtract_fusion.52
  255.8 0.4 convolution_subtract_fusion.52
  261.0 0.4 convolution_subtract_fusion.52
  262.0 6.5 %all_to_all.5 = bf16[4,2,4096]{2,1,0:T(2,128)(2,1)S(1)} all-to-all(bf16[4,2,4096]{2,1,0:T(2,128)(2,1)S(1)} %reshape.549), channel_id=1, replica_groups=mesh['seq'=8,'xlo'=2,'z'=8,'core'=2] {'xlo','core'}, dimensions={0} | all-to-all | bytes 131072 | tf_op jit(solution)/shard_map/output_mix/all_to_all | solution.py:231
  268.7 1.8 fusion.201
  270.6 1.2 convert_element_type.88.part_ref
  271.8 22.6 %output_mix.1 = bf16[8,48,1024]{2,1,0:T(8,128)(2,1)} custom-call(bf16[8,48,1024]{2,1,0:T(8,128)(2,1)} %convert_element_type.88.part_ref), custom_call_target="tpu_custom_call" | custom-call | bytes 1572864 | tf_op jit(solution)/shard_map/output_mix/pallas_call | solution.py:146
  294.4 1.3 reduce_sum.318
  295.7 0.7 convert_element_type.89
  (659 shorter events, 91.6 us)
Async XLA Ops:
  6.5 71.4 %all-gather.3.cloned.1.call-start = ((), (), s32[]{:S(2)}) async-start(), calls=%async_computation.1 | async-start | bytes 3244032 | tf_op jit(solution)/shard_map/all_gather | solution.py:184
  7.3 261.4 %all-gather.5.cloned.1.call-start = ((), (), s32[]{:S(2)}) async-start(), calls=%async_computation.2 | async-start | bytes 1966080 | tf_op jit(solution)/shard_map/all_gather | solution.py:186
  81.4 0.9 copy-start.4
  81.4 0.9 copy-start.5
  81.4 0.9 copy-start
  81.4 0.9 copy-start.3
  81.4 0.9 copy-start.1
  81.4 0.9 copy-start.2
  93.8 11.2 %collective-permute-start = (bf16[2,33088]{1,0:T(2,128)(2,1)S(1)}, bf16[2,33088]{1,0:T(2,128)(2,1)S(1)}, u32[]{:S(2)}, u32[]{:S(2)}) collective-permute-start(bf16[2,33088]{1,0:T(2,128)(2,1)S(1)} %fusion.205), channel_id=1, source_target_pairs={{0,32},{32,64},{64,96},{96,128},{128,160},{160,192},{192,224},{1,3... | collective-permute-start | bytes 397064 | tf_op jit(solution)/shard_map/state_hop/ppermute | solution.py:23
  117.0 10.5 %collective-permute-start.1 = (bf16[2,33088]{1,0:T(2,128)(2,1)S(1)}, bf16[2,33088]{1,0:T(2,128)(2,1)S(1)}, u32[]{:S(2)}, u32[]{:S(2)}) collective-permute-start(bf16[2,33088]{1,0:T(2,128)(2,1)S(1)} %fusion.206), channel_id=1, source_target_pairs={{0,32},{32,64},{64,96},{96,128},{128,160},{160,192},{192,224},{1,3... | collective-permute-start | bytes 397064 | tf_op jit(solution)/shard_map/state_hop/ppermute | solution.py:23
  139.6 10.5 %collective-permute-start.2 = (bf16[2,33088]{1,0:T(2,128)(2,1)S(1)}, bf16[2,33088]{1,0:T(2,128)(2,1)S(1)}, u32[]{:S(2)}, u32[]{:S(2)}) collective-permute-start(bf16[2,33088]{1,0:T(2,128)(2,1)S(1)} %fusion.207), channel_id=1, source_target_pairs={{0,32},{32,64},{64,96},{96,128},{128,160},{160,192},{192,224},{1,3... | collective-permute-start | bytes 397064 | tf_op jit(solution)/shard_map/state_hop/ppermute | solution.py:23
  162.2 10.5 %collective-permute-start.3 = (bf16[2,33088]{1,0:T(2,128)(2,1)S(1)}, bf16[2,33088]{1,0:T(2,128)(2,1)S(1)}, u32[]{:S(2)}, u32[]{:S(2)}) collective-permute-start(bf16[2,33088]{1,0:T(2,128)(2,1)S(1)} %fusion.208), channel_id=1, source_target_pairs={{0,32},{32,64},{64,96},{96,128},{128,160},{160,192},{192,224},{1,3... | collective-permute-start | bytes 397064 | tf_op jit(solution)/shard_map/state_hop/ppermute | solution.py:23
  184.8 10.5 %collective-permute-start.4 = (bf16[2,33088]{1,0:T(2,128)(2,1)S(1)}, bf16[2,33088]{1,0:T(2,128)(2,1)S(1)}, u32[]{:S(2)}, u32[]{:S(2)}) collective-permute-start(bf16[2,33088]{1,0:T(2,128)(2,1)S(1)} %fusion.209), channel_id=1, source_target_pairs={{0,32},{32,64},{64,96},{96,128},{128,160},{160,192},{192,224},{1,3... | collective-permute-start | bytes 397064 | tf_op jit(solution)/shard_map/state_hop/ppermute | solution.py:23
  207.4 10.5 %collective-permute-start.5 = (bf16[2,33088]{1,0:T(2,128)(2,1)S(1)}, bf16[2,33088]{1,0:T(2,128)(2,1)S(1)}, u32[]{:S(2)}, u32[]{:S(2)}) collective-permute-start(bf16[2,33088]{1,0:T(2,128)(2,1)S(1)} %fusion.210), channel_id=1, source_target_pairs={{0,32},{32,64},{64,96},{96,128},{128,160},{160,192},{192,224},{1,3... | collective-permute-start | bytes 397064 | tf_op jit(solution)/shard_map/state_hop/ppermute | solution.py:23
  229.9 10.5 %collective-permute-start.6 = (bf16[2,33088]{1,0:T(2,128)(2,1)S(1)}, bf16[2,33088]{1,0:T(2,128)(2,1)S(1)}, u32[]{:S(2)}, u32[]{:S(2)}) collective-permute-start(bf16[2,33088]{1,0:T(2,128)(2,1)S(1)} %fusion.211), channel_id=1, source_target_pairs={{0,32},{32,64},{64,96},{96,128},{128,160},{160,192},{192,224},{1,3... | collective-permute-start | bytes 397064 | tf_op jit(solution)/shard_map/state_hop/ppermute | solution.py:23
Sparse Core Ops, SparseCore 0:
  9.2 68.7 all-gather.2
  232.5 27.2 all-gather.4
